TPU v7x, 256 devices: a whole 4x4x8 slice. The times are simulated.
256 devices in a mesh: seq: 32 (over y, x, core), section: 8 (over z).
Axes of the slice: x: 4, y: 4, z: 8, core: 2. Of those that a mesh axis runs over, the one named last changes fastest.
Arguments:
- cotangent: bfloat16 [1, 4096, 768], P(None, 'seq'), may hold values from -6 to 6
- projected: bfloat16 [8, 1, 4096, 2304], P('section', None, 'seq'), may hold values from -6 to 6
- w_in: bfloat16 [8, 768, 2304], P('section'), may hold values from -0.21875 to 0.21875
- w_out: bfloat16 [8, 768, 768], P('section'), may hold values from -0.0546875 to 0.0546875
- short_filter: float32 [8, 3, 2304], P('section'), may hold values from -3.5 to 3.5
- long_filter: float32 [8, 4096, 768], P('section', 'seq'), may hold values from -1.1 to 1.1, as said below
- filter_bias: float32 [8, 768], P('section'), may hold values from 0.3 to 0.9
Outputs:
- grads: bfloat16 [8, 1, 4096, 768], P('section', None, 'seq')
Inputs may be any that keep to these rules, and one draw needn't show every extreme that they name: `long_filter`: row t of a section's long filter is its response at lag t.
All inputs are finite; a program needn't handle non-finite values.
Results may differ from a plain program's by a relative error of at most 0.03.
Values may be sent and summed in bfloat16 or wider, within the bound.
A program may use at most 64 MiB of HBM per device.

v0:
```python
import math

import jax
import jax.numpy as jnp
from jax import lax
from jax.sharding import PartitionSpec as P

accuracy = lax.Precision.HIGH


def shifted(value, axis, by):
    count = lax.axis_size(axis)
    pairs = [(i, i + by) for i in range(count) if 0 <= i + by < count]
    return lax.ppermute(value, axis, pairs)


def phase_table(height, breadth, period):
    row_ids = lax.broadcasted_iota(jnp.int32, (height, breadth), 0)
    col_ids = lax.broadcasted_iota(jnp.int32, (height, breadth), 1)
    angle = (row_ids * col_ids % period).astype(jnp.float32) * (2.0 * math.pi / period)
    return (jnp.cos(angle), jnp.sin(angle))


def forward_spectrum(series, inner):
    length, chans = series.shape
    outer = 2 * length // inner
    blocks = series.reshape(length // inner, inner, chans)
    cos_outer, sin_outer = phase_table(outer, length // inner, outer)
    real_one = jnp.einsum("kn,nbc->cbk", cos_outer, blocks, precision=accuracy)
    imag_one = -jnp.einsum("kn,nbc->cbk", sin_outer, blocks, precision=accuracy)
    cos_twist, sin_twist = phase_table(inner, outer, 2 * length)
    real_two = real_one * cos_twist + imag_one * sin_twist
    imag_two = imag_one * cos_twist - real_one * sin_twist
    cos_inner, sin_inner = phase_table(inner, inner, inner)
    real = jnp.einsum("jb,cbk->cjk", cos_inner, real_two, precision=accuracy) + jnp.einsum(
        "jb,cbk->cjk", sin_inner, imag_two, precision=accuracy
    )
    imag = jnp.einsum("jb,cbk->cjk", cos_inner, imag_two, precision=accuracy) - jnp.einsum(
        "jb,cbk->cjk", sin_inner, real_two, precision=accuracy
    )
    return (real, imag)


def inverse_spectrum(real, imag, inner):
    chans, _, outer = real.shape
    length = outer * inner // 2
    cos_inner, sin_inner = phase_table(inner, inner, inner)
    real_one = jnp.einsum("jb,cjk->cbk", cos_inner, real, precision=accuracy) - jnp.einsum(
        "jb,cjk->cbk", sin_inner, imag, precision=accuracy
    )
    imag_one = jnp.einsum("jb,cjk->cbk", cos_inner, imag, precision=accuracy) + jnp.einsum(
        "jb,cjk->cbk", sin_inner, real, precision=accuracy
    )
    cos_twist, sin_twist = phase_table(inner, outer, 2 * length)
    real_two = real_one * cos_twist - imag_one * sin_twist
    imag_two = imag_one * cos_twist + real_one * sin_twist
    cos_outer, sin_outer = phase_table(outer, length // inner, outer)
    series = jnp.einsum("kn,cbk->nbc", cos_outer, real_two, precision=accuracy) - jnp.einsum(
        "kn,cbk->nbc", sin_outer, imag_two, precision=accuracy
    )
    return series.reshape(length, chans) / (2.0 * length)


def channel_conv(series, spectrum, bias_part, adjoint, inner):
    values = series.astype(jnp.float32)
    real, imag = forward_spectrum(values, inner)
    filter_real, filter_imag = spectrum
    if adjoint:
        prod_real = real * filter_real + imag * filter_imag
        prod_imag = imag * filter_real - real * filter_imag
    else:
        prod_real = real * filter_real - imag * filter_imag
        prod_imag = real * filter_imag + imag * filter_real
    return (inverse_spectrum(prod_real, prod_imag, inner) + bias_part * values).astype(jnp.bfloat16)


def when(active, action, *operands):

    def skipped(*inputs):
        return jax.tree.map(jnp.zeros_like, action(*inputs))

    return lax.cond(active, action, skipped, *operands)


def shards(cotangent, projected, w_in, w_out, short_filter, long_filter, filter_bias):
    seq_count = lax.axis_size("seq")
    seq_place = lax.axis_index("seq")
    section_count = lax.axis_size("section")
    section_place = lax.axis_index("section")
    micro = projected.shape[1]
    height = projected.shape[2]
    width = w_out.shape[2]
    length = height * seq_count
    inner = math.gcd(length, 32)
    chans = width // seq_count
    filter_local = lax.all_to_all(
        long_filter[0].astype(jnp.bfloat16), "seq", split_axis=1, concat_axis=0, tiled=True
    ).astype(jnp.float32)
    spectrum = forward_spectrum(filter_local, inner)
    bias_part = lax.dynamic_slice_in_dim(filter_bias[0], seq_place * chans, chans, 0)
    weight_in = w_in[0]
    weight_out = w_out[0]
    taps = short_filter[0]
    stored = projected[0]
    last_section = section_place == section_count - 1
    contract = (((1,), (1,)), ((), ()))

    def forward_part(grad_out, proj, rim):
        padded = jnp.concatenate([rim, proj], axis=0).astype(jnp.float32)
        mixed = taps[0] * padded[2:] + taps[1] * padded[1:-1] + taps[2] * padded[:-2]
        query = mixed[:, :width]
        keys = mixed[:, width : 2 * width]
        values = mixed[:, 2 * width :]
        product = (keys * values).astype(jnp.bfloat16)
        d_out = lax.dot_general(grad_out, weight_out, contract, preferred_element_type=jnp.float32)
        d_conv = (d_out * query).astype(jnp.bfloat16)
        return (product, d_conv, d_out, keys, values)

    def causal(series):
        return channel_conv(series, spectrum, bias_part, False, inner)

    def adjoint(series):
        return channel_conv(series, spectrum, bias_part, True, inner)

    def backward_part(d_out, conv, d_prod, keys, values):
        d_prod_wide = d_prod.astype(jnp.float32)
        return jnp.concatenate(
            [d_out * conv.astype(jnp.float32), d_prod_wide * values, d_prod_wide * keys], axis=1
        ).astype(jnp.bfloat16)

    def input_part(grad_out, d_mixed, rim):
        padded = jnp.concatenate([d_mixed, rim], axis=0).astype(jnp.float32)
        d_proj = (taps[0] * padded[:-2] + taps[1] * padded[1:-1] + taps[2] * padded[2:]).astype(
            jnp.bfloat16
        )
        total = grad_out.astype(jnp.float32) + lax.dot_general(
            d_proj, weight_in, contract, preferred_element_type=jnp.float32
        )
        return total.astype(jnp.bfloat16)

    def tick(step, carry):
        incoming, grads = carry
        index = step - (section_count - 1 - section_place)
        active = (index >= 0) & (index < micro)
        slot = jnp.clip(index, 0, micro - 1)
        top = lax.dynamic_index_in_dim(cotangent, slot, 0, keepdims=False)
        grad_out = jnp.where(last_section, top, incoming)
        proj = lax.dynamic_index_in_dim(stored, slot, 0, keepdims=False)
        rim = shifted(proj[height - 2 :], "seq", 1)
        product, d_conv, d_out, keys, values = when(active, forward_part, grad_out, proj, rim)
        product_local = lax.all_to_all(product, "seq", split_axis=1, concat_axis=0, tiled=True)
        conv = lax.all_to_all(
            when(active, causal, product_local), "seq", split_axis=0, concat_axis=1, tiled=True
        )
        d_conv_local = lax.all_to_all(d_conv, "seq", split_axis=1, concat_axis=0, tiled=True)
        d_prod = lax.all_to_all(
            when(active, adjoint, d_conv_local), "seq", split_axis=0, concat_axis=1, tiled=True
        )
        d_mixed = when(active, backward_part, d_out, conv, d_prod, keys, values)
        rim_below = shifted(d_mixed[:2], "seq", -1)
        d_input = when(active, input_part, grad_out, d_mixed, rim_below)
        grads = jnp.where(active, lax.dynamic_update_index_in_dim(grads, d_input, slot, 0), grads)
        incoming = shifted(d_input, "section", -1)
        return (incoming, grads)

    start = (
        jnp.zeros((height, width), jnp.bfloat16),
        jnp.zeros((micro, height, width), jnp.bfloat16),
    )
    incoming, grads = lax.fori_loop(0, micro + section_count - 1, tick, start)
    return grads[None]


def solution(mesh):
    return jax.shard_map(
        shards,
        mesh=mesh,
        in_specs=(
            P(None, "seq", None),
            P("section", None, "seq", None),
            P("section", None, None),
            P("section", None, None),
            P("section", None, None),
            P("section", "seq", None),
            P("section", None),
        ),
        out_specs=P("section", None, "seq", None),
        check_vma=False,
    )
```

profile of v0, /device:TPU:1, one launch (start us, length us, event | category | flops | bytes accessed | tf_op | source)
XLA Modules:
  0.0 906.4 jit_solution(6465563738118759012)
XLA Ops:
  0.8 4.5 collective-permute-start.2
  8.5 6.9 all-to-all-start.4
  16.1 7.5 all-to-all-done.4
  28.4 878.0 %while.18 = (s32[]{:T(128)}, bf16[128,768]{1,0:T(8,128)(2,1)S(1)}, bf16[1,128,768]{2,1,0:T(8,128)(2,1)}, s32[]{:T(128)}, pred[]{:T(512)}, /*index=5*/bf16[1,128,...) while((s32[]{:T(128)}, bf16[128,768]{1,0:T(8,128)(2,1)S(1)}, ...), condition=%wide.region_11.12_spmd.clone, body=%wide.region_0.11_spmd.clone.sunk | while | flops 2441809920 | bytes 103440336 | solution.py:170
  38.1 7.4 all-to-all-done.2
  52.2 6.0 all-to-all-done
  58.3 4.4 all-to-all-start.3
  65.0 6.1 all-to-all-done.3
  74.9 8.3 all-to-all-done.1
  90.6 6.0 collective-permute-done.1
  101.5 5.4 all-to-all-start.2
  107.7 7.4 all-to-all-done.2
  115.1 4.4 all-to-all-start
  121.8 6.0 all-to-all-done
  127.9 4.4 all-to-all-start.3
  134.6 6.1 all-to-all-done.3
  144.5 8.3 all-to-all-done.1
  160.2 6.0 collective-permute-done.1
  171.1 5.4 all-to-all-start.2
  177.3 7.4 all-to-all-done.2
  191.4 6.0 all-to-all-done
  197.5 4.4 all-to-all-start.3
  204.2 6.1 all-to-all-done.3
  214.0 8.3 all-to-all-done.1
  229.8 6.0 collective-permute-done.1
  240.7 5.4 all-to-all-start.2
  246.9 7.4 all-to-all-done.2
  261.0 6.0 all-to-all-done
  267.1 4.4 all-to-all-start.3
  273.8 6.1 all-to-all-done.3
  283.6 8.3 all-to-all-done.1
  299.4 7.2 collective-permute-done.1
  311.4 5.5 all-to-all-start.2
  317.7 7.4 all-to-all-done.2
  331.8 6.0 all-to-all-done
  337.9 4.4 all-to-all-start.3
  344.6 6.1 all-to-all-done.3
  354.4 8.3 all-to-all-done.1
  370.2 7.0 collective-permute-done.1
  382.0 5.5 all-to-all-start.2
  388.3 7.4 all-to-all-done.2
  402.4 6.0 all-to-all-done
  408.5 4.4 all-to-all-start.3
  415.2 6.1 all-to-all-done.3
  425.1 8.3 all-to-all-done.1
  440.8 7.0 collective-permute-done.1
  452.6 5.5 all-to-all-start.2
  458.9 7.4 all-to-all-done.2
  473.1 6.0 all-to-all-done
  479.1 4.4 all-to-all-start.3
  485.8 6.1 all-to-all-done.3
  495.7 8.3 all-to-all-done.1
  511.4 284.7 %collective-permute-done.1 = bf16[128,768]{1,0:T(8,128)(2,1)S(1)} collective-permute-done((bf16[128,768]{1,0:T(8,128)(2,1)}, bf16[128,768]{1,0:T(8,128)(2,1)S(1)}, u32[]{:S(2)}, u32[]{:S(2)}) %collective-permute-start.1) | collective-permute-done | bytes 196640 | tf_op jit(solution)/shard_map/while/body/eval_jaxpr/ppermute | solution.py:14
  797.8 7.2 conditional.15
  805.8 5.5 all-to-all-start.2
  812.1 7.4 all-to-all-done.2
  823.9 15.8 %conditional.17 = (bf16[4096,24]{0,1:T(8,128)(2,1)}) conditional(s32[]{:T(128)} %convert_element_type.385, () %tuple.132, (bf16[32,128,24]{1,2,0:T(8,128)(2,1)S(1)}, f32[24,32,256]{2,1,0:T(8,128)S(1)}, f32[24,32,256]{2,1,0:T(8,128)S(1)}, f32[24]{0:T(128)}) %tuple.150), branch_computations={%region_3.3_spmd, %region_4.4_spmd} | conditional | flops 914325504 | bytes 34078852 | solution.py:82
  841.4 7.5 all-to-all-start.3
  848.9 16.8 %conditional.16 = (bf16[4096,24]{0,1:T(8,128)(2,1)}) conditional(s32[]{:T(128)} %convert_element_type.385, () %tuple.128, (bf16[32,128,24]{1,2,0:T(8,128)(2,1)}, f32[24,32,256]{2,1,0:T(8,128)S(1)}, f32[24,32,256]{2,1,0:T(8,128)S(1)}, f32[24]{0:T(128)}) %tuple.131), branch_computations={%region_5.5_spmd, %region_6.6_spmd} | conditional | flops 914325504 | bytes 34078852 | solution.py:82
  867.3 7.4 all-to-all-start.1
  874.7 8.3 all-to-all-done.1
  883.0 4.6 conditional.18
  892.8 6.1 conditional.19
  900.4 6.0 collective-permute-done.1
  (307 shorter events, 289.6 us)
Async XLA Ops:
  0.0 15.4 %copy-start = (f32[1,768]{1,0:T(1,128)S(1)}, f32[1,768]{1,0:T(1,128)}, u32[]{:S(2)}) copy-start(f32[1,768]{1,0:T(1,128)} %param.25) | copy-start | bytes 9220
  0.8 27.6 %collective-permute-start.2 = (bf16[2,2304]{1,0:T(2,128)(2,1)S(1)}, bf16[2,2304]{1,0:T(2,128)(2,1)S(1)}, u32[]{:S(2)}, u32[]{:S(2)}) collective-permute-start(bf16[2,2304]{1,0:T(2,128)(2,1)S(1)} %slice_bitcast_fusion), channel_id=1, source_target_pairs={{0,8},{8,16},{16,24},{24,32},{32,40},{40,48},{48,56},{56,64},{64,7... | collective-permute-start | bytes 27656 | tf_op jit(solution)/shard_map/while/body/eval_jaxpr/ppermute | solution.py:14
  8.5 15.2 %all-to-all-start.4 = ((bf16[128,32,24]{0,2,1:T(8,128)(2,1)}), bf16[128,32,24]{0,2,1:T(8,128)(2,1)S(1)}, u32[]{:S(2)}, u32[]{:S(2)}) async-start(bf16[128,32,24]{0,2,1:T(8,128)(2,1)} %bitcast.39), calls=%async_computation.4 | async-start | bytes 393216 | tf_op jit(solution)/shard_map/all_to_all | solution.py:96
  33.4 12.1 %all-to-all-start.2 = ((bf16[128,32,24]{0,2,1:T(8,128)(2,1)}), bf16[128,32,24]{0,2,1:T(8,128)(2,1)S(1)}, u32[]{:S(2)}, u32[]{:S(2)}) async-start(bf16[128,32,24]{0,2,1:T(8,128)(2,1)} %bitcast.226), calls=%async_computation.2 | async-start | bytes 393216 | tf_op jit(solution)/shard_map/while/body/eval_jaxpr/all_to_all | solution.py:155
  45.5 12.8 %all-to-all-start = ((bf16[128,32,24]{0,2,1:T(8,128)(2,1)}), bf16[128,32,24]{0,2,1:T(8,128)(2,1)}, u32[]{:S(2)}, u32[]{:S(2)}) async-start(bf16[128,32,24]{0,2,1:T(8,128)(2,1)} %bitcast.223), calls=%async_computation | async-start | bytes 393216 | tf_op jit(solution)/shard_map/while/body/eval_jaxpr/all_to_all | solution.py:151
  58.3 12.8 %all-to-all-start.3 = ((bf16[32,128,24]{1,2,0:T(8,128)(2,1)}), bf16[32,128,24]{1,2,0:T(8,128)(2,1)}, u32[]{:S(2)}, u32[]{:S(2)}) async-start(bf16[32,128,24]{1,2,0:T(8,128)(2,1)} %copy_bitcast_fusion.6), calls=%async_computation.3 | async-start | bytes 393216 | tf_op jit(solution)/shard_map/while/body/eval_jaxpr/all_to_all | solution.py:156
  71.1 12.1 %all-to-all-start.1 = ((bf16[32,128,24]{1,2,0:T(8,128)(2,1)}), bf16[32,128,24]{1,2,0:T(8,128)(2,1)S(1)}, u32[]{:S(2)}, u32[]{:S(2)}) async-start(bf16[32,128,24]{1,2,0:T(8,128)(2,1)} %copy_bitcast_fusion.5), calls=%async_computation.1 | async-start | bytes 393216 | tf_op jit(solution)/shard_map/while/body/eval_jaxpr/all_to_all | solution.py:152
  83.5 5.0 collective-permute-start
  88.5 2.0 copy-start.3
  89.2 7.4 collective-permute-start.1
  90.6 6.1 copy-start.4
  101.5 13.6 %all-to-all-start.2 = ((bf16[128,32,24]{0,2,1:T(8,128)(2,1)}), bf16[128,32,24]{0,2,1:T(8,128)(2,1)S(1)}, u32[]{:S(2)}, u32[]{:S(2)}) async-start(bf16[128,32,24]{0,2,1:T(8,128)(2,1)} %bitcast.226), calls=%async_computation.2 | async-start | bytes 393216 | tf_op jit(solution)/shard_map/while/body/eval_jaxpr/all_to_all | solution.py:155
  115.1 12.8 %all-to-all-start = ((bf16[128,32,24]{0,2,1:T(8,128)(2,1)}), bf16[128,32,24]{0,2,1:T(8,128)(2,1)}, u32[]{:S(2)}, u32[]{:S(2)}) async-start(bf16[128,32,24]{0,2,1:T(8,128)(2,1)} %bitcast.223), calls=%async_computation | async-start | bytes 393216 | tf_op jit(solution)/shard_map/while/body/eval_jaxpr/all_to_all | solution.py:151
  127.9 12.8 %all-to-all-start.3 = ((bf16[32,128,24]{1,2,0:T(8,128)(2,1)}), bf16[32,128,24]{1,2,0:T(8,128)(2,1)}, u32[]{:S(2)}, u32[]{:S(2)}) async-start(bf16[32,128,24]{1,2,0:T(8,128)(2,1)} %copy_bitcast_fusion.6), calls=%async_computation.3 | async-start | bytes 393216 | tf_op jit(solution)/shard_map/while/body/eval_jaxpr/all_to_all | solution.py:156
  140.6 12.1 %all-to-all-start.1 = ((bf16[32,128,24]{1,2,0:T(8,128)(2,1)}), bf16[32,128,24]{1,2,0:T(8,128)(2,1)S(1)}, u32[]{:S(2)}, u32[]{:S(2)}) async-start(bf16[32,128,24]{1,2,0:T(8,128)(2,1)} %copy_bitcast_fusion.5), calls=%async_computation.1 | async-start | bytes 393216 | tf_op jit(solution)/shard_map/while/body/eval_jaxpr/all_to_all | solution.py:152
  153.1 5.0 collective-permute-start
  158.1 2.0 copy-start.3
  158.8 7.4 collective-permute-start.1
  160.2 6.1 copy-start.4
  171.1 13.6 %all-to-all-start.2 = ((bf16[128,32,24]{0,2,1:T(8,128)(2,1)}), bf16[128,32,24]{0,2,1:T(8,128)(2,1)S(1)}, u32[]{:S(2)}, u32[]{:S(2)}) async-start(bf16[128,32,24]{0,2,1:T(8,128)(2,1)} %bitcast.226), calls=%async_computation.2 | async-start | bytes 393216 | tf_op jit(solution)/shard_map/while/body/eval_jaxpr/all_to_all | solution.py:155
  184.7 12.8 %all-to-all-start = ((bf16[128,32,24]{0,2,1:T(8,128)(2,1)}), bf16[128,32,24]{0,2,1:T(8,128)(2,1)}, u32[]{:S(2)}, u32[]{:S(2)}) async-start(bf16[128,32,24]{0,2,1:T(8,128)(2,1)} %bitcast.223), calls=%async_computation | async-start | bytes 393216 | tf_op jit(solution)/shard_map/while/body/eval_jaxpr/all_to_all | solution.py:151
  197.5 12.8 %all-to-all-start.3 = ((bf16[32,128,24]{1,2,0:T(8,128)(2,1)}), bf16[32,128,24]{1,2,0:T(8,128)(2,1)}, u32[]{:S(2)}, u32[]{:S(2)}) async-start(bf16[32,128,24]{1,2,0:T(8,128)(2,1)} %copy_bitcast_fusion.6), calls=%async_computation.3 | async-start | bytes 393216 | tf_op jit(solution)/shard_map/while/body/eval_jaxpr/all_to_all | solution.py:156
  210.2 12.1 %all-to-all-start.1 = ((bf16[32,128,24]{1,2,0:T(8,128)(2,1)}), bf16[32,128,24]{1,2,0:T(8,128)(2,1)S(1)}, u32[]{:S(2)}, u32[]{:S(2)}) async-start(bf16[32,128,24]{1,2,0:T(8,128)(2,1)} %copy_bitcast_fusion.5), calls=%async_computation.1 | async-start | bytes 393216 | tf_op jit(solution)/shard_map/while/body/eval_jaxpr/all_to_all | solution.py:152
  222.7 5.0 collective-permute-start
  227.7 2.0 copy-start.3
  228.4 7.4 collective-permute-start.1
  229.8 6.1 copy-start.4
  240.7 13.6 %all-to-all-start.2 = ((bf16[128,32,24]{0,2,1:T(8,128)(2,1)}), bf16[128,32,24]{0,2,1:T(8,128)(2,1)S(1)}, u32[]{:S(2)}, u32[]{:S(2)}) async-start(bf16[128,32,24]{0,2,1:T(8,128)(2,1)} %bitcast.226), calls=%async_computation.2 | async-start | bytes 393216 | tf_op jit(solution)/shard_map/while/body/eval_jaxpr/all_to_all | solution.py:155
  254.3 12.8 %all-to-all-start = ((bf16[128,32,24]{0,2,1:T(8,128)(2,1)}), bf16[128,32,24]{0,2,1:T(8,128)(2,1)}, u32[]{:S(2)}, u32[]{:S(2)}) async-start(bf16[128,32,24]{0,2,1:T(8,128)(2,1)} %bitcast.223), calls=%async_computation | async-start | bytes 393216 | tf_op jit(solution)/shard_map/while/body/eval_jaxpr/all_to_all | solution.py:151
  267.1 12.8 %all-to-all-start.3 = ((bf16[32,128,24]{1,2,0:T(8,128)(2,1)}), bf16[32,128,24]{1,2,0:T(8,128)(2,1)}, u32[]{:S(2)}, u32[]{:S(2)}) async-start(bf16[32,128,24]{1,2,0:T(8,128)(2,1)} %copy_bitcast_fusion.6), calls=%async_computation.3 | async-start | bytes 393216 | tf_op jit(solution)/shard_map/while/body/eval_jaxpr/all_to_all | solution.py:156
  279.8 12.1 %all-to-all-start.1 = ((bf16[32,128,24]{1,2,0:T(8,128)(2,1)}), bf16[32,128,24]{1,2,0:T(8,128)(2,1)S(1)}, u32[]{:S(2)}, u32[]{:S(2)}) async-start(bf16[32,128,24]{1,2,0:T(8,128)(2,1)} %copy_bitcast_fusion.5), calls=%async_computation.1 | async-start | bytes 393216 | tf_op jit(solution)/shard_map/while/body/eval_jaxpr/all_to_all | solution.py:152
  292.3 5.0 collective-permute-start
  297.2 2.0 copy-start.3
  298.0 8.6 collective-permute-start.1
  299.4 7.2 copy-start.4
  311.4 13.7 %all-to-all-start.2 = ((bf16[128,32,24]{0,2,1:T(8,128)(2,1)}), bf16[128,32,24]{0,2,1:T(8,128)(2,1)S(1)}, u32[]{:S(2)}, u32[]{:S(2)}) async-start(bf16[128,32,24]{0,2,1:T(8,128)(2,1)} %bitcast.226), calls=%async_computation.2 | async-start | bytes 393216 | tf_op jit(solution)/shard_map/while/body/eval_jaxpr/all_to_all | solution.py:155
  325.1 12.8 %all-to-all-start = ((bf16[128,32,24]{0,2,1:T(8,128)(2,1)}), bf16[128,32,24]{0,2,1:T(8,128)(2,1)}, u32[]{:S(2)}, u32[]{:S(2)}) async-start(bf16[128,32,24]{0,2,1:T(8,128)(2,1)} %bitcast.223), calls=%async_computation | async-start | bytes 393216 | tf_op jit(solution)/shard_map/while/body/eval_jaxpr/all_to_all | solution.py:151
  337.9 12.8 %all-to-all-start.3 = ((bf16[32,128,24]{1,2,0:T(8,128)(2,1)}), bf16[32,128,24]{1,2,0:T(8,128)(2,1)}, u32[]{:S(2)}, u32[]{:S(2)}) async-start(bf16[32,128,24]{1,2,0:T(8,128)(2,1)} %copy_bitcast_fusion.6), calls=%async_computation.3 | async-start | bytes 393216 | tf_op jit(solution)/shard_map/while/body/eval_jaxpr/all_to_all | solution.py:156
  350.6 12.1 %all-to-all-start.1 = ((bf16[32,128,24]{1,2,0:T(8,128)(2,1)}), bf16[32,128,24]{1,2,0:T(8,128)(2,1)S(1)}, u32[]{:S(2)}, u32[]{:S(2)}) async-start(bf16[32,128,24]{1,2,0:T(8,128)(2,1)} %copy_bitcast_fusion.5), calls=%async_computation.1 | async-start | bytes 393216 | tf_op jit(solution)/shard_map/while/body/eval_jaxpr/all_to_all | solution.py:152
  363.1 5.0 collective-permute-start
  368.8 8.4 collective-permute-start.1
  370.2 7.0 copy-start.4
  382.0 13.7 %all-to-all-start.2 = ((bf16[128,32,24]{0,2,1:T(8,128)(2,1)}), bf16[128,32,24]{0,2,1:T(8,128)(2,1)S(1)}, u32[]{:S(2)}, u32[]{:S(2)}) async-start(bf16[128,32,24]{0,2,1:T(8,128)(2,1)} %bitcast.226), calls=%async_computation.2 | async-start | bytes 393216 | tf_op jit(solution)/shard_map/while/body/eval_jaxpr/all_to_all | solution.py:155
  395.7 12.8 %all-to-all-start = ((bf16[128,32,24]{0,2,1:T(8,128)(2,1)}), bf16[128,32,24]{0,2,1:T(8,128)(2,1)}, u32[]{:S(2)}, u32[]{:S(2)}) async-start(bf16[128,32,24]{0,2,1:T(8,128)(2,1)} %bitcast.223), calls=%async_computation | async-start | bytes 393216 | tf_op jit(solution)/shard_map/while/body/eval_jaxpr/all_to_all | solution.py:151
  408.5 12.8 %all-to-all-start.3 = ((bf16[32,128,24]{1,2,0:T(8,128)(2,1)}), bf16[32,128,24]{1,2,0:T(8,128)(2,1)}, u32[]{:S(2)}, u32[]{:S(2)}) async-start(bf16[32,128,24]{1,2,0:T(8,128)(2,1)} %copy_bitcast_fusion.6), calls=%async_computation.3 | async-start | bytes 393216 | tf_op jit(solution)/shard_map/while/body/eval_jaxpr/all_to_all | solution.py:156
  421.3 12.1 %all-to-all-start.1 = ((bf16[32,128,24]{1,2,0:T(8,128)(2,1)}), bf16[32,128,24]{1,2,0:T(8,128)(2,1)S(1)}, u32[]{:S(2)}, u32[]{:S(2)}) async-start(bf16[32,128,24]{1,2,0:T(8,128)(2,1)} %copy_bitcast_fusion.5), calls=%async_computation.1 | async-start | bytes 393216 | tf_op jit(solution)/shard_map/while/body/eval_jaxpr/all_to_all | solution.py:152
  433.7 5.0 collective-permute-start
  439.4 8.4 collective-permute-start.1
  440.8 7.0 copy-start.4
  452.6 13.7 %all-to-all-start.2 = ((bf16[128,32,24]{0,2,1:T(8,128)(2,1)}), bf16[128,32,24]{0,2,1:T(8,128)(2,1)S(1)}, u32[]{:S(2)}, u32[]{:S(2)}) async-start(bf16[128,32,24]{0,2,1:T(8,128)(2,1)} %bitcast.226), calls=%async_computation.2 | async-start | bytes 393216 | tf_op jit(solution)/shard_map/while/body/eval_jaxpr/all_to_all | solution.py:155
  466.3 12.8 %all-to-all-start = ((bf16[128,32,24]{0,2,1:T(8,128)(2,1)}), bf16[128,32,24]{0,2,1:T(8,128)(2,1)}, u32[]{:S(2)}, u32[]{:S(2)}) async-start(bf16[128,32,24]{0,2,1:T(8,128)(2,1)} %bitcast.223), calls=%async_computation | async-start | bytes 393216 | tf_op jit(solution)/shard_map/while/body/eval_jaxpr/all_to_all | solution.py:151
  479.1 12.8 %all-to-all-start.3 = ((bf16[32,128,24]{1,2,0:T(8,128)(2,1)}), bf16[32,128,24]{1,2,0:T(8,128)(2,1)}, u32[]{:S(2)}, u32[]{:S(2)}) async-start(bf16[32,128,24]{1,2,0:T(8,128)(2,1)} %copy_bitcast_fusion.6), calls=%async_computation.3 | async-start | bytes 393216 | tf_op jit(solution)/shard_map/while/body/eval_jaxpr/all_to_all | solution.py:156
  491.9 12.1 %all-to-all-start.1 = ((bf16[32,128,24]{1,2,0:T(8,128)(2,1)}), bf16[32,128,24]{1,2,0:T(8,128)(2,1)S(1)}, u32[]{:S(2)}, u32[]{:S(2)}) async-start(bf16[32,128,24]{1,2,0:T(8,128)(2,1)} %copy_bitcast_fusion.5), calls=%async_computation.1 | async-start | bytes 393216 | tf_op jit(solution)/shard_map/while/body/eval_jaxpr/all_to_all | solution.py:152
  504.3 5.0 collective-permute-start
  510.0 286.1 %collective-permute-start.1 = (bf16[128,768]{1,0:T(8,128)(2,1)}, bf16[128,768]{1,0:T(8,128)(2,1)S(1)}, u32[]{:S(2)}, u32[]{:S(2)}) collective-permute-start(bf16[128,768]{1,0:T(8,128)(2,1)} %get-tuple-element.698), channel_id=1, source_target_pairs={{1,0},{2,1},{3,2},{4,3},{5,4},{6,5},{7,6},{9,8},{10,9},{11,10},{12... | collective-permute-start | bytes 589832 | tf_op jit(solution)/shard_map/while/body/eval_jaxpr/ppermute | solution.py:14
  511.4 284.7 %copy-start.4 = (bf16[1,128,768]{2,1,0:T(8,128)(2,1)}, bf16[1,128,768]{2,1,0:T(8,128)(2,1)S(1)}, u32[]{:S(2)}) copy-start(bf16[1,128,768]{2,1,0:T(8,128)(2,1)S(1)} %select_select_fusion.2) | copy-start | bytes 589828 | tf_op jit(solution)/shard_map/while
  805.8 13.7 %all-to-all-start.2 = ((bf16[128,32,24]{0,2,1:T(8,128)(2,1)}), bf16[128,32,24]{0,2,1:T(8,128)(2,1)S(1)}, u32[]{:S(2)}, u32[]{:S(2)}) async-start(bf16[128,32,24]{0,2,1:T(8,128)(2,1)} %bitcast.226), calls=%async_computation.2 | async-start | bytes 393216 | tf_op jit(solution)/shard_map/while/body/eval_jaxpr/all_to_all | solution.py:155
  819.5 21.9 %all-to-all-start = ((bf16[128,32,24]{0,2,1:T(8,128)(2,1)}), bf16[128,32,24]{0,2,1:T(8,128)(2,1)}, u32[]{:S(2)}, u32[]{:S(2)}) async-start(bf16[128,32,24]{0,2,1:T(8,128)(2,1)} %bitcast.223), calls=%async_computation | async-start | bytes 393216 | tf_op jit(solution)/shard_map/while/body/eval_jaxpr/all_to_all | solution.py:151
  841.4 25.9 %all-to-all-start.3 = ((bf16[32,128,24]{1,2,0:T(8,128)(2,1)}), bf16[32,128,24]{1,2,0:T(8,128)(2,1)}, u32[]{:S(2)}, u32[]{:S(2)}) async-start(bf16[32,128,24]{1,2,0:T(8,128)(2,1)} %copy_bitcast_fusion.6), calls=%async_computation.3 | async-start | bytes 393216 | tf_op jit(solution)/shard_map/while/body/eval_jaxpr/all_to_all | solution.py:156
  867.3 15.6 %all-to-all-start.1 = ((bf16[32,128,24]{1,2,0:T(8,128)(2,1)}), bf16[32,128,24]{1,2,0:T(8,128)(2,1)S(1)}, u32[]{:S(2)}, u32[]{:S(2)}) async-start(bf16[32,128,24]{1,2,0:T(8,128)(2,1)} %copy_bitcast_fusion.5), calls=%async_computation.1 | async-start | bytes 393216 | tf_op jit(solution)/shard_map/while/body/eval_jaxpr/all_to_all | solution.py:152
  887.8 5.0 collective-permute-start
  892.8 7.4 copy-start.3
  899.0 7.4 collective-permute-start.1
  900.4 6.1 copy-start.4
  (5 other events, 9.1 us)
where the time goes:
time: 911 us; the launch traced here: 906 us
  waiting for transfers between devices  571 us (63%)
  starting transfers between devices  187 us (21%)
  local copies, waits for them, and re-layouts  91.4 us (10%)
  matrix products  29.9 us (3%)
  other arithmetic  25.3 us (3%)
    ppermute x17, waiting for transfers between devices, shifted(): return lax.ppermute(value, axis, pairs)  353 us
    all_to_all x8, waiting for transfers between devices, tick(): lax.all_to_all(when(active, causal, product_local), 'seq', split_axis=0,...  66.1 us
    all_to_all x8, waiting for transfers between devices, tick(): lax.all_to_all(d_conv, 'seq', split_axis=1, concat_axis=0, tiled=True)  59.6 us
    all_to_all x8, waiting for transfers between devices, tick(): lax.all_to_all(when(active, adjoint, d_conv_local), 'seq', split_axis=0,...  42.4 us
    all_to_all x8, waiting for transfers between devices, tick(): lax.all_to_all(product, 'seq', split_axis=1, concat_axis=0, tiled=True)  42.3 us
    all_to_all x8, starting transfers between devices, tick(): lax.all_to_all(d_conv, 'seq', split_axis=1, concat_axis=0, tiled=True)  41.7 us
    all_to_all x8, starting transfers between devices, tick(): lax.all_to_all(when(active, adjoint, d_conv_local), 'seq', split_axis=0,...  38 us
    another operation x68, local copies, waits for them, and re-layouts  35.3 us
  transfers between devices with their start and end apart: 50, of which 47 were waited for; matrix products, arithmetic and copies ran while one was open for 9% of the time, Pallas kernels for 0%

commit v1 on v0

--- a/solution.py
+++ b/solution.py
@@ -1,3 +1,4 @@
+import functools
 import math
 
 import jax
@@ -101,20 +102,7 @@
     weight_in = w_in[0]
     weight_out = w_out[0]
     taps = short_filter[0]
-    stored = projected[0]
-    last_section = section_place == section_count - 1
     contract = (((1,), (1,)), ((), ()))
-
-    def forward_part(grad_out, proj, rim):
-        padded = jnp.concatenate([rim, proj], axis=0).astype(jnp.float32)
-        mixed = taps[0] * padded[2:] + taps[1] * padded[1:-1] + taps[2] * padded[:-2]
-        query = mixed[:, :width]
-        keys = mixed[:, width : 2 * width]
-        values = mixed[:, 2 * width :]
-        product = (keys * values).astype(jnp.bfloat16)
-        d_out = lax.dot_general(grad_out, weight_out, contract, preferred_element_type=jnp.float32)
-        d_conv = (d_out * query).astype(jnp.bfloat16)
-        return (product, d_conv, d_out, keys, values)
 
     def causal(series):
         return channel_conv(series, spectrum, bias_part, False, inner)
@@ -122,14 +110,32 @@
     def adjoint(series):
         return channel_conv(series, spectrum, bias_part, True, inner)
 
-    def backward_part(d_out, conv, d_prod, keys, values):
+    forward = []
+    for slot in range(micro):
+        proj = projected[0, slot]
+        rim = shifted(proj[height - 2 :], "seq", 1)
+        padded = jnp.concatenate([rim, proj], axis=0).astype(jnp.float32)
+        mixed = taps[0] * padded[2:] + taps[1] * padded[1:-1] + taps[2] * padded[:-2]
+        query = mixed[:, :width]
+        keys = mixed[:, width : 2 * width]
+        values = mixed[:, 2 * width :]
+        product = (keys * values).astype(jnp.bfloat16)
+        product_local = lax.all_to_all(product, "seq", split_axis=1, concat_axis=0, tiled=True)
+        conv = lax.all_to_all(causal(product_local), "seq", split_axis=0, concat_axis=1, tiled=True)
+        forward.append((query, keys, values, conv.astype(jnp.float32)))
+
+    def stage(grad_out, slot):
+        query, keys, values, conv_wide = forward[slot]
+        d_out = lax.dot_general(grad_out, weight_out, contract, preferred_element_type=jnp.float32)
+        d_conv = (d_out * query).astype(jnp.bfloat16)
+        d_conv_local = lax.all_to_all(d_conv, "seq", split_axis=1, concat_axis=0, tiled=True)
+        d_prod = lax.all_to_all(adjoint(d_conv_local), "seq", split_axis=0, concat_axis=1, tiled=True)
         d_prod_wide = d_prod.astype(jnp.float32)
-        return jnp.concatenate(
-            [d_out * conv.astype(jnp.float32), d_prod_wide * values, d_prod_wide * keys], axis=1
+        d_mixed = jnp.concatenate(
+            [d_out * conv_wide, d_prod_wide * values, d_prod_wide * keys], axis=1
         ).astype(jnp.bfloat16)
-
-    def input_part(grad_out, d_mixed, rim):
-        padded = jnp.concatenate([d_mixed, rim], axis=0).astype(jnp.float32)
+        rim_below = shifted(d_mixed[:2], "seq", -1)
+        padded = jnp.concatenate([d_mixed, rim_below], axis=0).astype(jnp.float32)
         d_proj = (taps[0] * padded[:-2] + taps[1] * padded[1:-1] + taps[2] * padded[2:]).astype(
             jnp.bfloat16
         )
@@ -143,28 +149,18 @@
         index = step - (section_count - 1 - section_place)
         active = (index >= 0) & (index < micro)
         slot = jnp.clip(index, 0, micro - 1)
-        top = lax.dynamic_index_in_dim(cotangent, slot, 0, keepdims=False)
-        grad_out = jnp.where(last_section, top, incoming)
-        proj = lax.dynamic_index_in_dim(stored, slot, 0, keepdims=False)
-        rim = shifted(proj[height - 2 :], "seq", 1)
-        product, d_conv, d_out, keys, values = when(active, forward_part, grad_out, proj, rim)
-        product_local = lax.all_to_all(product, "seq", split_axis=1, concat_axis=0, tiled=True)
-        conv = lax.all_to_all(
-            when(active, causal, product_local), "seq", split_axis=0, concat_axis=1, tiled=True
-        )
-        d_conv_local = lax.all_to_all(d_conv, "seq", split_axis=1, concat_axis=0, tiled=True)
-        d_prod = lax.all_to_all(
-            when(active, adjoint, d_conv_local), "seq", split_axis=0, concat_axis=1, tiled=True
-        )
-        d_mixed = when(active, backward_part, d_out, conv, d_prod, keys, values)
-        rim_below = shifted(d_mixed[:2], "seq", -1)
-        d_input = when(active, input_part, grad_out, d_mixed, rim_below)
+        if micro == 1:
+            d_input = stage(incoming, 0)
+        else:
+            d_input = lax.switch(slot, [functools.partial(stage, slot=m) for m in range(micro)], incoming)
         grads = jnp.where(active, lax.dynamic_update_index_in_dim(grads, d_input, slot, 0), grads)
-        incoming = shifted(d_input, "section", -1)
+        later = jnp.clip(index + 1, 0, micro - 1)
+        top = lax.dynamic_index_in_dim(cotangent, later, 0, keepdims=False)
+        incoming = jnp.where(section_place == section_count - 1, top, shifted(d_input, "section", -1))
         return (incoming, grads)
 
     start = (
-        jnp.zeros((height, width), jnp.bfloat16),
+        cotangent[0],
         jnp.zeros((micro, height, width), jnp.bfloat16),
     )
     incoming, grads = lax.fori_loop(0, micro + section_count - 1, tick, start)

time: 911 us -> 540 us (0.59)
  waiting for transfers between devices: 571 us -> 159 us
  matrix products: 29.9 us -> 133 us
  starting transfers between devices: 187 us -> 89.4 us
  blocking collectives: 0 us -> 95 us
  local copies, waits for them, and re-layouts: 91.4 us -> 42.8 us
  other arithmetic: 25.3 us -> 10.4 us
    ppermute x17, waiting for transfers between devices: 353 us -> 74.7 us  [shifted(): return lax.ppermute(value, axis, pairs)]
    all_to_all x32 -> x10, waiting for transfers between devices: 210 us -> 77.1 us  [the longest x8 64.9 us: stage(): lax.all_to_all(d_conv, 'seq', split_axis=1, concat_axis=0, tiled=True)]
    all_to_all x32 -> x10, starting transfers between devices: 149 us -> 50.1 us  [the longest x8 41.7 us: stage(): lax.all_to_all(d_conv, 'seq', split_axis=1, concat_axis=0, tiled=True)]
    all_to_all x0 -> x8, blocking collectives: none -> 95 us  [stage(): lax.all_to_all(adjoint(d_conv_local), 'seq', split_axis=0, concat_axis=1,...]
    dot_general x2 -> x16, matrix products: 6.59 us -> 45.1 us  [the longest x8 26.7 us: stage(): lax.dot_general(d_proj, weight_in, contract, preferred_element_type=jnp.f...]
    another operation x68 -> x0, local copies, waits for them, and re-layouts: 35.3 us -> none
    all_to_all x16 -> x9, local copies, waits for them, and re-layouts: 26.4 us -> 0.25 us  [the longest x8 0.22 us: stage(): lax.all_to_all(d_conv, 'seq', split_axis=1, concat_axis=0, tiled=True)]
    cond x21 -> x0, local copies, waits for them, and re-layouts: 14.1 us -> none  [the longest x16 13.2 us: when(): return lax.cond(active, action, skipped, *operands)]
  transfers between devices with their start and end apart: 50 -> 28, of which waited for: 47 -> 27; matrix products, arithmetic and copies ran while one was open for 9% -> 2% of each run, Pallas kernels for 0% -> 0%
where the time goes in v1:
time: 540 us; the launch traced here: 534 us
  waiting for transfers between devices  159 us (29%)
  matrix products  133 us (25%)
  blocking collectives  95 us (18%)
  starting transfers between devices  89.4 us (17%)
  local copies, waits for them, and re-layouts  42.8 us (8%)
  other arithmetic  10.4 us (2%)
    all_to_all x8, blocking collectives, stage(): lax.all_to_all(adjoint(d_conv_local), 'seq', split_axis=0, concat_axis=1,...  95 us
    ppermute x17, waiting for transfers between devices, shifted(): return lax.ppermute(value, axis, pairs)  74.7 us
    all_to_all x8, waiting for transfers between devices, stage(): lax.all_to_all(d_conv, 'seq', split_axis=1, concat_axis=0, tiled=True)  64.9 us
    all_to_all x8, starting transfers between devices, stage(): lax.all_to_all(d_conv, 'seq', split_axis=1, concat_axis=0, tiled=True)  41.7 us
    ppermute x17, starting transfers between devices, shifted(): return lax.ppermute(value, axis, pairs)  32.4 us
    dot_general x8, matrix products, stage(): lax.dot_general(d_proj, weight_in, contract, preferred_element_type=jnp.f...  26.7 us
    dot_general x8, matrix products, stage(): lax.dot_general(grad_out, weight_out, contract, preferred_element_type=jn...  18.4 us
    div x18, local copies, waits for them, and re-layouts, inverse_spectrum(): return series.reshape(length, chans) / (2.0 * length)  11.3 us
  transfers between devices with their start and end apart: 28, of which 27 were waited for; matrix products, arithmetic and copies ran while one was open for 2% of the time, Pallas kernels for 0%

profile of v1, /device:TPU:1, one launch (start us, length us, event | category | flops | bytes accessed | tf_op | source)
XLA Modules:
  0.0 533.8 jit_solution(445405761807380657)
XLA Ops:
  0.8 4.5 collective-permute-start.2
  11.3 6.9 %all-to-all-start.3 = ((bf16[128,32,24]{0,2,1:T(8,128)(2,1)}), bf16[128,32,24]{0,2,1:T(8,128)(2,1)S(1)}, u32[]{:S(2)}, u32[]{:S(2)}) async-start(bf16[128,32,24]{0,2,1:T(8,128)(2,1)} %bitcast.13), calls=%async_computation.3 | async-start | bytes 393216 | tf_op jit(solution)/shard_map/all_to_all | solution.py:97
  19.4 7.1 %all-to-all-done.3 = bf16[128,32,24]{0,2,1:T(8,128)(2,1)S(1)} async-done(((bf16[128,32,24]{0,2,1:T(8,128)(2,1)}), bf16[128,32,24]{0,2,1:T(8,128)(2,1)S(1)}, u32[]{:S(2)}, u32[]{:S(2)}) %all-to-all-start.3) | async-done | bytes 196640 | tf_op jit(solution)/shard_map/all_to_all | solution.py:97
  31.6 3.8 all-to-all-start.2
  37.2 6.5 %all-to-all-done.2 = bf16[128,32,24]{0,2,1:T(8,128)(2,1)S(1)} async-done(((bf16[128,32,24]{0,2,1:T(8,128)(2,1)}), bf16[128,32,24]{0,2,1:T(8,128)(2,1)S(1)}, u32[]{:S(2)}, u32[]{:S(2)}) %all-to-all-start.2) | async-done | bytes 196640 | tf_op jit(solution)/shard_map/all_to_all | solution.py:123
  55.7 2.6 copy.108
  61.1 4.5 all-to-all-start.4
  68.4 5.7 %all-to-all-done.4 = bf16[32,128,24]{1,2,0:T(8,128)(2,1)} async-done(((bf16[32,128,24]{1,2,0:T(8,128)(2,1)}), bf16[32,128,24]{1,2,0:T(8,128)(2,1)}, u32[]{:S(2)}, u32[]{:S(2)}) %all-to-all-start.4) | async-done | bytes 196640 | tf_op jit(solution)/shard_map/all_to_all | solution.py:124
  75.2 458.5 %while.19 = (s32[]{:T(128)}, bf16[128,768]{1,0:T(8,128)(2,1)S(1)}, bf16[1,128,768]{2,1,0:T(8,128)(2,1)}, pred[]{:T(512)}, bf16[1,128,768]{2,1,0:T(8,128)(2,1)S(1...) while((s32[]{:T(128)}, bf16[128,768]{1,0:T(8,128)(2,1)S(1)}, ...), condition=%wide.region_1.2_spmd.clone, body=%wide.region_0.1_spmd.clone.sunk | while | flops 1522793472 | bytes 68959000 | solution.py:166
  75.4 2.3 multiply_convert_fusion.7
  78.6 3.8 all-to-all-start
  82.5 8.1 %all-to-all-done = bf16[128,32,24]{0,2,1:T(8,128)(2,1)S(1)} async-done(((bf16[128,32,24]{0,2,1:T(8,128)(2,1)}), bf16[128,32,24]{0,2,1:T(8,128)(2,1)S(1)}, u32[]{:S(2)}, u32[]{:S(2)}) %all-to-all-start) | async-done | bytes 196640 | tf_op jit(solution)/shard_map/while/body/eval_jaxpr/all_to_all | solution.py:131
  101.9 11.9 %all_to_all.115 = bf16[32,128,24]{1,2,0:T(8,128)(2,1)S(1)} all-to-all(bf16[32,128,24]{1,2,0:T(8,128)(2,1)S(1)} %fusion.390), channel_id=1, replica_groups=mesh['seq'=32,'section'=8] {'seq'}, dimensions={0} | all-to-all | bytes 393216 | tf_op jit(solution)/shard_map/while/body/eval_jaxpr/all_to_all | solution.py:132
  116.4 2.8 collective-permute-done
  119.4 3.3 bitcast_select_fusion.4
  124.7 5.9 %collective-permute-done.1 = bf16[128,768]{1,0:T(8,128)(2,1)S(1)} collective-permute-done((bf16[128,768]{1,0:T(8,128)(2,1)S(1)}, bf16[128,768]{1,0:T(8,128)(2,1)S(1)}, u32[]{:S(2)}, u32[]{:S(2)}) %collective-permute-start.1) | collective-permute-done | bytes 196640 | tf_op jit(solution)/shard_map/while/body/eval_jaxpr/ppermute | solution.py:15
  130.7 2.3 multiply_convert_fusion.7
  133.8 5.3 %all-to-all-start = ((bf16[128,32,24]{0,2,1:T(8,128)(2,1)}), bf16[128,32,24]{0,2,1:T(8,128)(2,1)S(1)}, u32[]{:S(2)}, u32[]{:S(2)}) async-start(bf16[128,32,24]{0,2,1:T(8,128)(2,1)} %bitcast.242), calls=%async_computation | async-start | bytes 393216 | tf_op jit(solution)/shard_map/while/body/eval_jaxpr/all_to_all | solution.py:131
  139.3 8.1 %all-to-all-done = bf16[128,32,24]{0,2,1:T(8,128)(2,1)S(1)} async-done(((bf16[128,32,24]{0,2,1:T(8,128)(2,1)}), bf16[128,32,24]{0,2,1:T(8,128)(2,1)S(1)}, u32[]{:S(2)}, u32[]{:S(2)}) %all-to-all-start) | async-done | bytes 196640 | tf_op jit(solution)/shard_map/while/body/eval_jaxpr/all_to_all | solution.py:131
  158.7 11.9 %all_to_all.115 = bf16[32,128,24]{1,2,0:T(8,128)(2,1)S(1)} all-to-all(bf16[32,128,24]{1,2,0:T(8,128)(2,1)S(1)} %fusion.390), channel_id=1, replica_groups=mesh['seq'=32,'section'=8] {'seq'}, dimensions={0} | all-to-all | bytes 393216 | tf_op jit(solution)/shard_map/while/body/eval_jaxpr/all_to_all | solution.py:132
  173.2 2.8 collective-permute-done
  176.2 3.3 bitcast_select_fusion.4
  181.5 5.9 %collective-permute-done.1 = bf16[128,768]{1,0:T(8,128)(2,1)S(1)} collective-permute-done((bf16[128,768]{1,0:T(8,128)(2,1)S(1)}, bf16[128,768]{1,0:T(8,128)(2,1)S(1)}, u32[]{:S(2)}, u32[]{:S(2)}) %collective-permute-start.1) | collective-permute-done | bytes 196640 | tf_op jit(solution)/shard_map/while/body/eval_jaxpr/ppermute | solution.py:15
  190.6 5.4 %all-to-all-start = ((bf16[128,32,24]{0,2,1:T(8,128)(2,1)}), bf16[128,32,24]{0,2,1:T(8,128)(2,1)S(1)}, u32[]{:S(2)}, u32[]{:S(2)}) async-start(bf16[128,32,24]{0,2,1:T(8,128)(2,1)} %bitcast.242), calls=%async_computation | async-start | bytes 393216 | tf_op jit(solution)/shard_map/while/body/eval_jaxpr/all_to_all | solution.py:131
  196.2 8.1 %all-to-all-done = bf16[128,32,24]{0,2,1:T(8,128)(2,1)S(1)} async-done(((bf16[128,32,24]{0,2,1:T(8,128)(2,1)}), bf16[128,32,24]{0,2,1:T(8,128)(2,1)S(1)}, u32[]{:S(2)}, u32[]{:S(2)}) %all-to-all-start) | async-done | bytes 196640 | tf_op jit(solution)/shard_map/while/body/eval_jaxpr/all_to_all | solution.py:131
  215.5 11.9 %all_to_all.115 = bf16[32,128,24]{1,2,0:T(8,128)(2,1)S(1)} all-to-all(bf16[32,128,24]{1,2,0:T(8,128)(2,1)S(1)} %fusion.390), channel_id=1, replica_groups=mesh['seq'=32,'section'=8] {'seq'}, dimensions={0} | all-to-all | bytes 393216 | tf_op jit(solution)/shard_map/while/body/eval_jaxpr/all_to_all | solution.py:132
  230.1 2.8 collective-permute-done
  233.0 3.3 bitcast_select_fusion.4
  238.3 5.9 %collective-permute-done.1 = bf16[128,768]{1,0:T(8,128)(2,1)S(1)} collective-permute-done((bf16[128,768]{1,0:T(8,128)(2,1)S(1)}, bf16[128,768]{1,0:T(8,128)(2,1)S(1)}, u32[]{:S(2)}, u32[]{:S(2)}) %collective-permute-start.1) | collective-permute-done | bytes 196640 | tf_op jit(solution)/shard_map/while/body/eval_jaxpr/ppermute | solution.py:15
  244.3 2.3 multiply_convert_fusion.7
  247.5 5.4 %all-to-all-start = ((bf16[128,32,24]{0,2,1:T(8,128)(2,1)}), bf16[128,32,24]{0,2,1:T(8,128)(2,1)S(1)}, u32[]{:S(2)}, u32[]{:S(2)}) async-start(bf16[128,32,24]{0,2,1:T(8,128)(2,1)} %bitcast.242), calls=%async_computation | async-start | bytes 393216 | tf_op jit(solution)/shard_map/while/body/eval_jaxpr/all_to_all | solution.py:131
  253.0 8.1 %all-to-all-done = bf16[128,32,24]{0,2,1:T(8,128)(2,1)S(1)} async-done(((bf16[128,32,24]{0,2,1:T(8,128)(2,1)}), bf16[128,32,24]{0,2,1:T(8,128)(2,1)S(1)}, u32[]{:S(2)}, u32[]{:S(2)}) %all-to-all-start) | async-done | bytes 196640 | tf_op jit(solution)/shard_map/while/body/eval_jaxpr/all_to_all | solution.py:131
  272.4 11.9 %all_to_all.115 = bf16[32,128,24]{1,2,0:T(8,128)(2,1)S(1)} all-to-all(bf16[32,128,24]{1,2,0:T(8,128)(2,1)S(1)} %fusion.390), channel_id=1, replica_groups=mesh['seq'=32,'section'=8] {'seq'}, dimensions={0} | all-to-all | bytes 393216 | tf_op jit(solution)/shard_map/while/body/eval_jaxpr/all_to_all | solution.py:132
  286.9 2.8 collective-permute-done
  289.8 3.3 bitcast_select_fusion.4
  295.1 7.1 %collective-permute-done.1 = bf16[128,768]{1,0:T(8,128)(2,1)S(1)} collective-permute-done((bf16[128,768]{1,0:T(8,128)(2,1)S(1)}, bf16[128,768]{1,0:T(8,128)(2,1)S(1)}, u32[]{:S(2)}, u32[]{:S(2)}) %collective-permute-start.1) | collective-permute-done | bytes 196640 | tf_op jit(solution)/shard_map/while/body/eval_jaxpr/ppermute | solution.py:15
  302.3 2.3 multiply_convert_fusion.7
  305.4 5.5 %all-to-all-start = ((bf16[128,32,24]{0,2,1:T(8,128)(2,1)}), bf16[128,32,24]{0,2,1:T(8,128)(2,1)S(1)}, u32[]{:S(2)}, u32[]{:S(2)}) async-start(bf16[128,32,24]{0,2,1:T(8,128)(2,1)} %bitcast.242), calls=%async_computation | async-start | bytes 393216 | tf_op jit(solution)/shard_map/while/body/eval_jaxpr/all_to_all | solution.py:131
  311.0 8.1 %all-to-all-done = bf16[128,32,24]{0,2,1:T(8,128)(2,1)S(1)} async-done(((bf16[128,32,24]{0,2,1:T(8,128)(2,1)}), bf16[128,32,24]{0,2,1:T(8,128)(2,1)S(1)}, u32[]{:S(2)}, u32[]{:S(2)}) %all-to-all-start) | async-done | bytes 196640 | tf_op jit(solution)/shard_map/while/body/eval_jaxpr/all_to_all | solution.py:131
  330.4 11.9 %all_to_all.115 = bf16[32,128,24]{1,2,0:T(8,128)(2,1)S(1)} all-to-all(bf16[32,128,24]{1,2,0:T(8,128)(2,1)S(1)} %fusion.390), channel_id=1, replica_groups=mesh['seq'=32,'section'=8] {'seq'}, dimensions={0} | all-to-all | bytes 393216 | tf_op jit(solution)/shard_map/while/body/eval_jaxpr/all_to_all | solution.py:132
  344.9 2.8 collective-permute-done
  347.8 3.3 bitcast_select_fusion.4
  353.2 6.9 %collective-permute-done.1 = bf16[128,768]{1,0:T(8,128)(2,1)S(1)} collective-permute-done((bf16[128,768]{1,0:T(8,128)(2,1)S(1)}, bf16[128,768]{1,0:T(8,128)(2,1)S(1)}, u32[]{:S(2)}, u32[]{:S(2)}) %collective-permute-start.1) | collective-permute-done | bytes 196640 | tf_op jit(solution)/shard_map/while/body/eval_jaxpr/ppermute | solution.py:15
  360.1 2.3 multiply_convert_fusion.7
  363.3 5.5 %all-to-all-start = ((bf16[128,32,24]{0,2,1:T(8,128)(2,1)}), bf16[128,32,24]{0,2,1:T(8,128)(2,1)S(1)}, u32[]{:S(2)}, u32[]{:S(2)}) async-start(bf16[128,32,24]{0,2,1:T(8,128)(2,1)} %bitcast.242), calls=%async_computation | async-start | bytes 393216 | tf_op jit(solution)/shard_map/while/body/eval_jaxpr/all_to_all | solution.py:131
  368.9 8.1 %all-to-all-done = bf16[128,32,24]{0,2,1:T(8,128)(2,1)S(1)} async-done(((bf16[128,32,24]{0,2,1:T(8,128)(2,1)}), bf16[128,32,24]{0,2,1:T(8,128)(2,1)S(1)}, u32[]{:S(2)}, u32[]{:S(2)}) %all-to-all-start) | async-done | bytes 196640 | tf_op jit(solution)/shard_map/while/body/eval_jaxpr/all_to_all | solution.py:131
  388.2 11.9 %all_to_all.115 = bf16[32,128,24]{1,2,0:T(8,128)(2,1)S(1)} all-to-all(bf16[32,128,24]{1,2,0:T(8,128)(2,1)S(1)} %fusion.390), channel_id=1, replica_groups=mesh['seq'=32,'section'=8] {'seq'}, dimensions={0} | all-to-all | bytes 393216 | tf_op jit(solution)/shard_map/while/body/eval_jaxpr/all_to_all | solution.py:132
  402.8 2.8 collective-permute-done
  405.7 3.3 bitcast_select_fusion.4
  411.0 6.9 %collective-permute-done.1 = bf16[128,768]{1,0:T(8,128)(2,1)S(1)} collective-permute-done((bf16[128,768]{1,0:T(8,128)(2,1)S(1)}, bf16[128,768]{1,0:T(8,128)(2,1)S(1)}, u32[]{:S(2)}, u32[]{:S(2)}) %collective-permute-start.1) | collective-permute-done | bytes 196640 | tf_op jit(solution)/shard_map/while/body/eval_jaxpr/ppermute | solution.py:15
  418.0 2.3 multiply_convert_fusion.7
  421.1 5.5 %all-to-all-start = ((bf16[128,32,24]{0,2,1:T(8,128)(2,1)}), bf16[128,32,24]{0,2,1:T(8,128)(2,1)S(1)}, u32[]{:S(2)}, u32[]{:S(2)}) async-start(bf16[128,32,24]{0,2,1:T(8,128)(2,1)} %bitcast.242), calls=%async_computation | async-start | bytes 393216 | tf_op jit(solution)/shard_map/while/body/eval_jaxpr/all_to_all | solution.py:131
  426.7 8.1 %all-to-all-done = bf16[128,32,24]{0,2,1:T(8,128)(2,1)S(1)} async-done(((bf16[128,32,24]{0,2,1:T(8,128)(2,1)}), bf16[128,32,24]{0,2,1:T(8,128)(2,1)S(1)}, u32[]{:S(2)}, u32[]{:S(2)}) %all-to-all-start) | async-done | bytes 196640 | tf_op jit(solution)/shard_map/while/body/eval_jaxpr/all_to_all | solution.py:131
  446.1 11.9 %all_to_all.115 = bf16[32,128,24]{1,2,0:T(8,128)(2,1)S(1)} all-to-all(bf16[32,128,24]{1,2,0:T(8,128)(2,1)S(1)} %fusion.390), channel_id=1, replica_groups=mesh['seq'=32,'section'=8] {'seq'}, dimensions={0} | all-to-all | bytes 393216 | tf_op jit(solution)/shard_map/while/body/eval_jaxpr/all_to_all | solution.py:132
  460.6 2.8 collective-permute-done
  463.6 3.3 bitcast_select_fusion.4
  468.9 6.9 %collective-permute-done.1 = bf16[128,768]{1,0:T(8,128)(2,1)S(1)} collective-permute-done((bf16[128,768]{1,0:T(8,128)(2,1)S(1)}, bf16[128,768]{1,0:T(8,128)(2,1)S(1)}, u32[]{:S(2)}, u32[]{:S(2)}) %collective-permute-start.1) | collective-permute-done | bytes 196640 | tf_op jit(solution)/shard_map/while/body/eval_jaxpr/ppermute | solution.py:15
  475.8 2.3 multiply_convert_fusion.7
  479.0 5.5 %all-to-all-start = ((bf16[128,32,24]{0,2,1:T(8,128)(2,1)}), bf16[128,32,24]{0,2,1:T(8,128)(2,1)S(1)}, u32[]{:S(2)}, u32[]{:S(2)}) async-start(bf16[128,32,24]{0,2,1:T(8,128)(2,1)} %bitcast.242), calls=%async_computation | async-start | bytes 393216 | tf_op jit(solution)/shard_map/while/body/eval_jaxpr/all_to_all | solution.py:131
  484.6 8.1 %all-to-all-done = bf16[128,32,24]{0,2,1:T(8,128)(2,1)S(1)} async-done(((bf16[128,32,24]{0,2,1:T(8,128)(2,1)}), bf16[128,32,24]{0,2,1:T(8,128)(2,1)S(1)}, u32[]{:S(2)}, u32[]{:S(2)}) %all-to-all-start) | async-done | bytes 196640 | tf_op jit(solution)/shard_map/while/body/eval_jaxpr/all_to_all | solution.py:131
  503.9 11.9 %all_to_all.115 = bf16[32,128,24]{1,2,0:T(8,128)(2,1)S(1)} all-to-all(bf16[32,128,24]{1,2,0:T(8,128)(2,1)S(1)} %fusion.390), channel_id=1, replica_groups=mesh['seq'=32,'section'=8] {'seq'}, dimensions={0} | all-to-all | bytes 393216 | tf_op jit(solution)/shard_map/while/body/eval_jaxpr/all_to_all | solution.py:132
  518.5 2.8 collective-permute-done
  521.4 3.3 bitcast_select_fusion.4
  526.7 6.9 %collective-permute-done.1 = bf16[128,768]{1,0:T(8,128)(2,1)S(1)} collective-permute-done((bf16[128,768]{1,0:T(8,128)(2,1)S(1)}, bf16[128,768]{1,0:T(8,128)(2,1)S(1)}, u32[]{:S(2)}, u32[]{:S(2)}) %collective-permute-start.1) | collective-permute-done | bytes 196640 | tf_op jit(solution)/shard_map/while/body/eval_jaxpr/ppermute | solution.py:15
  (501 shorter events, 169.0 us)
Async XLA Ops:
  0.8 7.8 %collective-permute-start.2 = (bf16[2,2304]{1,0:T(2,128)(2,1)S(1)}, bf16[2,2304]{1,0:T(2,128)(2,1)S(1)}, u32[]{:S(2)}, u32[]{:S(2)}) collective-permute-start(bf16[2,2304]{1,0:T(2,128)(2,1)S(1)} %slice_bitcast_fusion), channel_id=1, source_target_pairs={{0,8},{8,16},{16,24},{24,32},{32,40},{40,48},{48,56},{56,64},{64,7... | collective-permute-start | bytes 27656 | tf_op jit(solution)/shard_map/ppermute | solution.py:15
  11.3 15.2 %all-to-all-start.3 = ((bf16[128,32,24]{0,2,1:T(8,128)(2,1)}), bf16[128,32,24]{0,2,1:T(8,128)(2,1)S(1)}, u32[]{:S(2)}, u32[]{:S(2)}) async-start(bf16[128,32,24]{0,2,1:T(8,128)(2,1)} %bitcast.13), calls=%async_computation.3 | async-start | bytes 393216 | tf_op jit(solution)/shard_map/all_to_all | solution.py:97
  31.6 12.1 %all-to-all-start.2 = ((bf16[128,32,24]{0,2,1:T(8,128)(2,1)}), bf16[128,32,24]{0,2,1:T(8,128)(2,1)S(1)}, u32[]{:S(2)}, u32[]{:S(2)}) async-start(bf16[128,32,24]{0,2,1:T(8,128)(2,1)} %bitcast.253), calls=%async_computation.2 | async-start | bytes 393216 | tf_op jit(solution)/shard_map/all_to_all | solution.py:123
  61.1 12.9 %all-to-all-start.4 = ((bf16[32,128,24]{1,2,0:T(8,128)(2,1)}), bf16[32,128,24]{1,2,0:T(8,128)(2,1)}, u32[]{:S(2)}, u32[]{:S(2)}) async-start(bf16[32,128,24]{1,2,0:T(8,128)(2,1)} %fusion.155), calls=%async_computation.4 | async-start | bytes 393216 | tf_op jit(solution)/shard_map/all_to_all | solution.py:124
  78.6 12.1 %all-to-all-start = ((bf16[128,32,24]{0,2,1:T(8,128)(2,1)}), bf16[128,32,24]{0,2,1:T(8,128)(2,1)S(1)}, u32[]{:S(2)}, u32[]{:S(2)}) async-start(bf16[128,32,24]{0,2,1:T(8,128)(2,1)} %bitcast.242), calls=%async_computation | async-start | bytes 393216 | tf_op jit(solution)/shard_map/while/body/eval_jaxpr/all_to_all | solution.py:131
  101.6 12.4 %copy-start.6 = (f32[128,768]{1,0:T(8,128)S(1)}, f32[128,768]{1,0:T(8,128)}, u32[]{:S(2)}) copy-start(f32[128,768]{1,0:T(8,128)} %get-tuple-element.733) | copy-start | bytes 1179652 | tf_op jit(solution)/shard_map/while
  101.6 12.4 %copy-start.7 = (f32[128,768]{1,0:T(8,128)S(1)}, f32[128,768]{1,0:T(8,128)}, u32[]{:S(2)}) copy-start(f32[128,768]{1,0:T(8,128)} %get-tuple-element.734) | copy-start | bytes 1179652 | tf_op jit(solution)/shard_map/while
  114.1 5.1 collective-permute-start
  119.3 11.3 %copy-start.3 = (f32[24,32,256]{2,1,0:T(8,128)S(1)}, f32[24,32,256]{2,1,0:T(8,128)}, u32[]{:S(2)}) copy-start(f32[24,32,256]{2,1,0:T(8,128)} %copy-done.1) | copy-start | bytes 2359300 | tf_op jit(solution)/shard_map/while
  119.3 11.3 %copy-start.5 = (f32[128,768]{1,0:T(8,128)S(1)}, f32[128,768]{1,0:T(8,128)}, u32[]{:S(2)}) copy-start(f32[128,768]{1,0:T(8,128)} %copy-done.4) | copy-start | bytes 1179652 | tf_op jit(solution)/shard_map/while
  123.4 7.2 %collective-permute-start.1 = (bf16[128,768]{1,0:T(8,128)(2,1)S(1)}, bf16[128,768]{1,0:T(8,128)(2,1)S(1)}, u32[]{:S(2)}, u32[]{:S(2)}) collective-permute-start(bf16[128,768]{1,0:T(8,128)(2,1)S(1)} %get-tuple-element.683), channel_id=1, source_target_pairs={{1,0},{2,1},{3,2},{4,3},{5,4},{6,5},{7,6},{9,8},{10,9},{11,10},{12... | collective-permute-start | bytes 589832 | tf_op jit(solution)/shard_map/while/body/eval_jaxpr/ppermute | solution.py:15
  133.8 13.6 %all-to-all-start = ((bf16[128,32,24]{0,2,1:T(8,128)(2,1)}), bf16[128,32,24]{0,2,1:T(8,128)(2,1)S(1)}, u32[]{:S(2)}, u32[]{:S(2)}) async-start(bf16[128,32,24]{0,2,1:T(8,128)(2,1)} %bitcast.242), calls=%async_computation | async-start | bytes 393216 | tf_op jit(solution)/shard_map/while/body/eval_jaxpr/all_to_all | solution.py:131
  158.4 12.4 %copy-start.6 = (f32[128,768]{1,0:T(8,128)S(1)}, f32[128,768]{1,0:T(8,128)}, u32[]{:S(2)}) copy-start(f32[128,768]{1,0:T(8,128)} %get-tuple-element.733) | copy-start | bytes 1179652 | tf_op jit(solution)/shard_map/while
  158.4 12.4 %copy-start.7 = (f32[128,768]{1,0:T(8,128)S(1)}, f32[128,768]{1,0:T(8,128)}, u32[]{:S(2)}) copy-start(f32[128,768]{1,0:T(8,128)} %get-tuple-element.734) | copy-start | bytes 1179652 | tf_op jit(solution)/shard_map/while
  170.9 5.1 collective-permute-start
  176.1 11.3 %copy-start.3 = (f32[24,32,256]{2,1,0:T(8,128)S(1)}, f32[24,32,256]{2,1,0:T(8,128)}, u32[]{:S(2)}) copy-start(f32[24,32,256]{2,1,0:T(8,128)} %copy-done.1) | copy-start | bytes 2359300 | tf_op jit(solution)/shard_map/while
  176.1 11.3 %copy-start.5 = (f32[128,768]{1,0:T(8,128)S(1)}, f32[128,768]{1,0:T(8,128)}, u32[]{:S(2)}) copy-start(f32[128,768]{1,0:T(8,128)} %copy-done.4) | copy-start | bytes 1179652 | tf_op jit(solution)/shard_map/while
  180.2 7.2 %collective-permute-start.1 = (bf16[128,768]{1,0:T(8,128)(2,1)S(1)}, bf16[128,768]{1,0:T(8,128)(2,1)S(1)}, u32[]{:S(2)}, u32[]{:S(2)}) collective-permute-start(bf16[128,768]{1,0:T(8,128)(2,1)S(1)} %get-tuple-element.683), channel_id=1, source_target_pairs={{1,0},{2,1},{3,2},{4,3},{5,4},{6,5},{7,6},{9,8},{10,9},{11,10},{12... | collective-permute-start | bytes 589832 | tf_op jit(solution)/shard_map/while/body/eval_jaxpr/ppermute | solution.py:15
  190.6 13.7 %all-to-all-start = ((bf16[128,32,24]{0,2,1:T(8,128)(2,1)}), bf16[128,32,24]{0,2,1:T(8,128)(2,1)S(1)}, u32[]{:S(2)}, u32[]{:S(2)}) async-start(bf16[128,32,24]{0,2,1:T(8,128)(2,1)} %bitcast.242), calls=%async_computation | async-start | bytes 393216 | tf_op jit(solution)/shard_map/while/body/eval_jaxpr/all_to_all | solution.py:131
  215.2 12.4 %copy-start.6 = (f32[128,768]{1,0:T(8,128)S(1)}, f32[128,768]{1,0:T(8,128)}, u32[]{:S(2)}) copy-start(f32[128,768]{1,0:T(8,128)} %get-tuple-element.733) | copy-start | bytes 1179652 | tf_op jit(solution)/shard_map/while
  215.3 12.4 %copy-start.7 = (f32[128,768]{1,0:T(8,128)S(1)}, f32[128,768]{1,0:T(8,128)}, u32[]{:S(2)}) copy-start(f32[128,768]{1,0:T(8,128)} %get-tuple-element.734) | copy-start | bytes 1179652 | tf_op jit(solution)/shard_map/while
  227.7 5.1 collective-permute-start
  233.0 11.3 %copy-start.3 = (f32[24,32,256]{2,1,0:T(8,128)S(1)}, f32[24,32,256]{2,1,0:T(8,128)}, u32[]{:S(2)}) copy-start(f32[24,32,256]{2,1,0:T(8,128)} %copy-done.1) | copy-start | bytes 2359300 | tf_op jit(solution)/shard_map/while
  237.0 7.2 %collective-permute-start.1 = (bf16[128,768]{1,0:T(8,128)(2,1)S(1)}, bf16[128,768]{1,0:T(8,128)(2,1)S(1)}, u32[]{:S(2)}, u32[]{:S(2)}) collective-permute-start(bf16[128,768]{1,0:T(8,128)(2,1)S(1)} %get-tuple-element.683), channel_id=1, source_target_pairs={{1,0},{2,1},{3,2},{4,3},{5,4},{6,5},{7,6},{9,8},{10,9},{11,10},{12... | collective-permute-start | bytes 589832 | tf_op jit(solution)/shard_map/while/body/eval_jaxpr/ppermute | solution.py:15
  247.5 13.6 %all-to-all-start = ((bf16[128,32,24]{0,2,1:T(8,128)(2,1)}), bf16[128,32,24]{0,2,1:T(8,128)(2,1)S(1)}, u32[]{:S(2)}, u32[]{:S(2)}) async-start(bf16[128,32,24]{0,2,1:T(8,128)(2,1)} %bitcast.242), calls=%async_computation | async-start | bytes 393216 | tf_op jit(solution)/shard_map/while/body/eval_jaxpr/all_to_all | solution.py:131
  272.1 12.4 %copy-start.6 = (f32[128,768]{1,0:T(8,128)S(1)}, f32[128,768]{1,0:T(8,128)}, u32[]{:S(2)}) copy-start(f32[128,768]{1,0:T(8,128)} %get-tuple-element.733) | copy-start | bytes 1179652 | tf_op jit(solution)/shard_map/while
  272.1 12.4 %copy-start.7 = (f32[128,768]{1,0:T(8,128)S(1)}, f32[128,768]{1,0:T(8,128)}, u32[]{:S(2)}) copy-start(f32[128,768]{1,0:T(8,128)} %get-tuple-element.734) | copy-start | bytes 1179652 | tf_op jit(solution)/shard_map/while
  284.6 5.1 collective-permute-start
  289.8 12.4 %copy-start.11 = (bf16[1,128,768]{2,1,0:T(8,128)(2,1)S(1)}, bf16[1,128,768]{2,1,0:T(8,128)(2,1)}, u32[]{:S(2)}) copy-start(bf16[1,128,768]{2,1,0:T(8,128)(2,1)} %get-tuple-element.758) | copy-start | bytes 589828 | tf_op jit(solution)/shard_map/while
  289.8 12.4 %copy-start.3 = (f32[24,32,256]{2,1,0:T(8,128)S(1)}, f32[24,32,256]{2,1,0:T(8,128)}, u32[]{:S(2)}) copy-start(f32[24,32,256]{2,1,0:T(8,128)} %copy-done.1) | copy-start | bytes 2359300 | tf_op jit(solution)/shard_map/while
  289.8 12.4 %copy-start.5 = (f32[128,768]{1,0:T(8,128)S(1)}, f32[128,768]{1,0:T(8,128)}, u32[]{:S(2)}) copy-start(f32[128,768]{1,0:T(8,128)} %copy-done.4) | copy-start | bytes 1179652 | tf_op jit(solution)/shard_map/while
  293.8 8.3 %collective-permute-start.1 = (bf16[128,768]{1,0:T(8,128)(2,1)S(1)}, bf16[128,768]{1,0:T(8,128)(2,1)S(1)}, u32[]{:S(2)}, u32[]{:S(2)}) collective-permute-start(bf16[128,768]{1,0:T(8,128)(2,1)S(1)} %get-tuple-element.683), channel_id=1, source_target_pairs={{1,0},{2,1},{3,2},{4,3},{5,4},{6,5},{7,6},{9,8},{10,9},{11,10},{12... | collective-permute-start | bytes 589832 | tf_op jit(solution)/shard_map/while/body/eval_jaxpr/ppermute | solution.py:15
  305.4 13.7 %all-to-all-start = ((bf16[128,32,24]{0,2,1:T(8,128)(2,1)}), bf16[128,32,24]{0,2,1:T(8,128)(2,1)S(1)}, u32[]{:S(2)}, u32[]{:S(2)}) async-start(bf16[128,32,24]{0,2,1:T(8,128)(2,1)} %bitcast.242), calls=%async_computation | async-start | bytes 393216 | tf_op jit(solution)/shard_map/while/body/eval_jaxpr/all_to_all | solution.py:131
  330.1 12.4 %copy-start.6 = (f32[128,768]{1,0:T(8,128)S(1)}, f32[128,768]{1,0:T(8,128)}, u32[]{:S(2)}) copy-start(f32[128,768]{1,0:T(8,128)} %get-tuple-element.733) | copy-start | bytes 1179652 | tf_op jit(solution)/shard_map/while
  330.1 12.4 %copy-start.7 = (f32[128,768]{1,0:T(8,128)S(1)}, f32[128,768]{1,0:T(8,128)}, u32[]{:S(2)}) copy-start(f32[128,768]{1,0:T(8,128)} %get-tuple-element.734) | copy-start | bytes 1179652 | tf_op jit(solution)/shard_map/while
  342.6 5.1 collective-permute-start
  347.8 12.2 %copy-start.11 = (bf16[1,128,768]{2,1,0:T(8,128)(2,1)S(1)}, bf16[1,128,768]{2,1,0:T(8,128)(2,1)}, u32[]{:S(2)}) copy-start(bf16[1,128,768]{2,1,0:T(8,128)(2,1)} %get-tuple-element.758) | copy-start | bytes 589828 | tf_op jit(solution)/shard_map/while
  347.8 12.2 %copy-start.3 = (f32[24,32,256]{2,1,0:T(8,128)S(1)}, f32[24,32,256]{2,1,0:T(8,128)}, u32[]{:S(2)}) copy-start(f32[24,32,256]{2,1,0:T(8,128)} %copy-done.1) | copy-start | bytes 2359300 | tf_op jit(solution)/shard_map/while
  347.8 12.2 %copy-start.5 = (f32[128,768]{1,0:T(8,128)S(1)}, f32[128,768]{1,0:T(8,128)}, u32[]{:S(2)}) copy-start(f32[128,768]{1,0:T(8,128)} %copy-done.4) | copy-start | bytes 1179652 | tf_op jit(solution)/shard_map/while
  351.9 8.2 %collective-permute-start.1 = (bf16[128,768]{1,0:T(8,128)(2,1)S(1)}, bf16[128,768]{1,0:T(8,128)(2,1)S(1)}, u32[]{:S(2)}, u32[]{:S(2)}) collective-permute-start(bf16[128,768]{1,0:T(8,128)(2,1)S(1)} %get-tuple-element.683), channel_id=1, source_target_pairs={{1,0},{2,1},{3,2},{4,3},{5,4},{6,5},{7,6},{9,8},{10,9},{11,10},{12... | collective-permute-start | bytes 589832 | tf_op jit(solution)/shard_map/while/body/eval_jaxpr/ppermute | solution.py:15
  363.3 13.7 %all-to-all-start = ((bf16[128,32,24]{0,2,1:T(8,128)(2,1)}), bf16[128,32,24]{0,2,1:T(8,128)(2,1)S(1)}, u32[]{:S(2)}, u32[]{:S(2)}) async-start(bf16[128,32,24]{0,2,1:T(8,128)(2,1)} %bitcast.242), calls=%async_computation | async-start | bytes 393216 | tf_op jit(solution)/shard_map/while/body/eval_jaxpr/all_to_all | solution.py:131
  387.9 12.4 %copy-start.6 = (f32[128,768]{1,0:T(8,128)S(1)}, f32[128,768]{1,0:T(8,128)}, u32[]{:S(2)}) copy-start(f32[128,768]{1,0:T(8,128)} %get-tuple-element.733) | copy-start | bytes 1179652 | tf_op jit(solution)/shard_map/while
  388.0 12.4 %copy-start.7 = (f32[128,768]{1,0:T(8,128)S(1)}, f32[128,768]{1,0:T(8,128)}, u32[]{:S(2)}) copy-start(f32[128,768]{1,0:T(8,128)} %get-tuple-element.734) | copy-start | bytes 1179652 | tf_op jit(solution)/shard_map/while
  400.4 5.1 collective-permute-start
  405.7 12.2 %copy-start.11 = (bf16[1,128,768]{2,1,0:T(8,128)(2,1)S(1)}, bf16[1,128,768]{2,1,0:T(8,128)(2,1)}, u32[]{:S(2)}) copy-start(bf16[1,128,768]{2,1,0:T(8,128)(2,1)} %get-tuple-element.758) | copy-start | bytes 589828 | tf_op jit(solution)/shard_map/while
  405.7 12.2 %copy-start.3 = (f32[24,32,256]{2,1,0:T(8,128)S(1)}, f32[24,32,256]{2,1,0:T(8,128)}, u32[]{:S(2)}) copy-start(f32[24,32,256]{2,1,0:T(8,128)} %copy-done.1) | copy-start | bytes 2359300 | tf_op jit(solution)/shard_map/while
  405.7 12.2 %copy-start.5 = (f32[128,768]{1,0:T(8,128)S(1)}, f32[128,768]{1,0:T(8,128)}, u32[]{:S(2)}) copy-start(f32[128,768]{1,0:T(8,128)} %copy-done.4) | copy-start | bytes 1179652 | tf_op jit(solution)/shard_map/while
  409.7 8.2 %collective-permute-start.1 = (bf16[128,768]{1,0:T(8,128)(2,1)S(1)}, bf16[128,768]{1,0:T(8,128)(2,1)S(1)}, u32[]{:S(2)}, u32[]{:S(2)}) collective-permute-start(bf16[128,768]{1,0:T(8,128)(2,1)S(1)} %get-tuple-element.683), channel_id=1, source_target_pairs={{1,0},{2,1},{3,2},{4,3},{5,4},{6,5},{7,6},{9,8},{10,9},{11,10},{12... | collective-permute-start | bytes 589832 | tf_op jit(solution)/shard_map/while/body/eval_jaxpr/ppermute | solution.py:15
  421.1 13.7 %all-to-all-start = ((bf16[128,32,24]{0,2,1:T(8,128)(2,1)}), bf16[128,32,24]{0,2,1:T(8,128)(2,1)S(1)}, u32[]{:S(2)}, u32[]{:S(2)}) async-start(bf16[128,32,24]{0,2,1:T(8,128)(2,1)} %bitcast.242), calls=%async_computation | async-start | bytes 393216 | tf_op jit(solution)/shard_map/while/body/eval_jaxpr/all_to_all | solution.py:131
  445.8 12.4 %copy-start.6 = (f32[128,768]{1,0:T(8,128)S(1)}, f32[128,768]{1,0:T(8,128)}, u32[]{:S(2)}) copy-start(f32[128,768]{1,0:T(8,128)} %get-tuple-element.733) | copy-start | bytes 1179652 | tf_op jit(solution)/shard_map/while
  445.8 12.4 %copy-start.7 = (f32[128,768]{1,0:T(8,128)S(1)}, f32[128,768]{1,0:T(8,128)}, u32[]{:S(2)}) copy-start(f32[128,768]{1,0:T(8,128)} %get-tuple-element.734) | copy-start | bytes 1179652 | tf_op jit(solution)/shard_map/while
  458.3 5.1 collective-permute-start
  463.5 12.2 %copy-start.11 = (bf16[1,128,768]{2,1,0:T(8,128)(2,1)S(1)}, bf16[1,128,768]{2,1,0:T(8,128)(2,1)}, u32[]{:S(2)}) copy-start(bf16[1,128,768]{2,1,0:T(8,128)(2,1)} %get-tuple-element.758) | copy-start | bytes 589828 | tf_op jit(solution)/shard_map/while
  463.5 12.2 %copy-start.3 = (f32[24,32,256]{2,1,0:T(8,128)S(1)}, f32[24,32,256]{2,1,0:T(8,128)}, u32[]{:S(2)}) copy-start(f32[24,32,256]{2,1,0:T(8,128)} %copy-done.1) | copy-start | bytes 2359300 | tf_op jit(solution)/shard_map/while
  463.5 12.2 %copy-start.5 = (f32[128,768]{1,0:T(8,128)S(1)}, f32[128,768]{1,0:T(8,128)}, u32[]{:S(2)}) copy-start(f32[128,768]{1,0:T(8,128)} %copy-done.4) | copy-start | bytes 1179652 | tf_op jit(solution)/shard_map/while
  467.6 8.2 %collective-permute-start.1 = (bf16[128,768]{1,0:T(8,128)(2,1)S(1)}, bf16[128,768]{1,0:T(8,128)(2,1)S(1)}, u32[]{:S(2)}, u32[]{:S(2)}) collective-permute-start(bf16[128,768]{1,0:T(8,128)(2,1)S(1)} %get-tuple-element.683), channel_id=1, source_target_pairs={{1,0},{2,1},{3,2},{4,3},{5,4},{6,5},{7,6},{9,8},{10,9},{11,10},{12... | collective-permute-start | bytes 589832 | tf_op jit(solution)/shard_map/while/body/eval_jaxpr/ppermute | solution.py:15
  479.0 13.7 %all-to-all-start = ((bf16[128,32,24]{0,2,1:T(8,128)(2,1)}), bf16[128,32,24]{0,2,1:T(8,128)(2,1)S(1)}, u32[]{:S(2)}, u32[]{:S(2)}) async-start(bf16[128,32,24]{0,2,1:T(8,128)(2,1)} %bitcast.242), calls=%async_computation | async-start | bytes 393216 | tf_op jit(solution)/shard_map/while/body/eval_jaxpr/all_to_all | solution.py:131
  503.7 12.4 %copy-start.6 = (f32[128,768]{1,0:T(8,128)S(1)}, f32[128,768]{1,0:T(8,128)}, u32[]{:S(2)}) copy-start(f32[128,768]{1,0:T(8,128)} %get-tuple-element.733) | copy-start | bytes 1179652 | tf_op jit(solution)/shard_map/while
  503.7 12.4 %copy-start.7 = (f32[128,768]{1,0:T(8,128)S(1)}, f32[128,768]{1,0:T(8,128)}, u32[]{:S(2)}) copy-start(f32[128,768]{1,0:T(8,128)} %get-tuple-element.734) | copy-start | bytes 1179652 | tf_op jit(solution)/shard_map/while
  516.2 5.1 collective-permute-start
  521.4 12.2 %copy-start.11 = (bf16[1,128,768]{2,1,0:T(8,128)(2,1)S(1)}, bf16[1,128,768]{2,1,0:T(8,128)(2,1)}, u32[]{:S(2)}) copy-start(bf16[1,128,768]{2,1,0:T(8,128)(2,1)} %get-tuple-element.758) | copy-start | bytes 589828 | tf_op jit(solution)/shard_map/while
  521.4 12.2 %copy-start.3 = (f32[24,32,256]{2,1,0:T(8,128)S(1)}, f32[24,32,256]{2,1,0:T(8,128)}, u32[]{:S(2)}) copy-start(f32[24,32,256]{2,1,0:T(8,128)} %copy-done.1) | copy-start | bytes 2359300 | tf_op jit(solution)/shard_map/while
  521.4 12.2 %copy-start.5 = (f32[128,768]{1,0:T(8,128)S(1)}, f32[128,768]{1,0:T(8,128)}, u32[]{:S(2)}) copy-start(f32[128,768]{1,0:T(8,128)} %copy-done.4) | copy-start | bytes 1179652 | tf_op jit(solution)/shard_map/while
  525.4 8.2 %collective-permute-start.1 = (bf16[128,768]{1,0:T(8,128)(2,1)S(1)}, bf16[128,768]{1,0:T(8,128)(2,1)S(1)}, u32[]{:S(2)}, u32[]{:S(2)}) collective-permute-start(bf16[128,768]{1,0:T(8,128)(2,1)S(1)} %get-tuple-element.683), channel_id=1, source_target_pairs={{1,0},{2,1},{3,2},{4,3},{5,4},{6,5},{7,6},{9,8},{10,9},{11,10},{12... | collective-permute-start | bytes 589832 | tf_op jit(solution)/shard_map/while/body/eval_jaxpr/ppermute | solution.py:15
  (76 other events, 267.2 us)

commit v2 on v1

--- a/solution.py
+++ b/solution.py
@@ -4,6 +4,8 @@
 import jax
 import jax.numpy as jnp
 from jax import lax
+from jax.experimental import pallas as pl
+from jax.experimental.pallas import tpu as pltpu
 from jax.sharding import PartitionSpec as P
 
 accuracy = lax.Precision.HIGH
@@ -75,6 +77,62 @@
     return (inverse_spectrum(prod_real, prod_imag, inner) + bias_part * values).astype(jnp.bfloat16)
 
 
+def exchange_kernel(x_ref, o_ref, landed, send_sems, recv_sems):
+    count = x_ref.shape[0]
+    me = lax.axis_index("seq")
+    section = lax.axis_index("section")
+    mesh_ids = pl.DeviceIdType.MESH
+    barrier = pltpu.get_barrier_semaphore()
+
+    def greet(k, _):
+        peer = lax.rem(me + k, count)
+        pl.semaphore_signal(barrier, inc=1, device_id=(peer, section), device_id_type=mesh_ids)
+        return 0
+
+    lax.fori_loop(1, count, greet, 0)
+    pl.semaphore_wait(barrier, count - 1)
+
+    def describe(k):
+        peer = lax.rem(me + k, count)
+        return pltpu.make_async_remote_copy(
+            src_ref=x_ref.at[peer],
+            dst_ref=landed.at[me],
+            send_sem=send_sems.at[k],
+            recv_sem=recv_sems.at[k],
+            device_id=(peer, section),
+            device_id_type=mesh_ids,
+        )
+
+    def send(k, _):
+        describe(k).start()
+        return 0
+
+    def finish(k, _):
+        describe(k).wait()
+        return 0
+
+    lax.fori_loop(1, count, send, 0)
+    lax.fori_loop(1, count, finish, 0)
+    o_ref[...] = landed[...]
+    o_ref[pl.ds(me, 1)] = x_ref[pl.ds(me, 1)]
+
+
+def seq_exchange(blocks):
+    count = blocks.shape[0]
+    return pl.pallas_call(
+        exchange_kernel,
+        out_shape=jax.ShapeDtypeStruct(blocks.shape, blocks.dtype),
+        in_specs=[pl.BlockSpec(memory_space=pltpu.VMEM)],
+        out_specs=pl.BlockSpec(memory_space=pltpu.VMEM),
+        scratch_shapes=[
+            pltpu.VMEM(blocks.shape, blocks.dtype),
+            pltpu.SemaphoreType.DMA((count,)),
+            pltpu.SemaphoreType.DMA((count,)),
+        ],
+        compiler_params=pltpu.CompilerParams(collective_id=0, has_side_effects=True),
+    )(blocks)
+
+
 def when(active, action, *operands):
 
     def skipped(*inputs):
@@ -94,21 +152,19 @@
     length = height * seq_count
     inner = math.gcd(length, 32)
     chans = width // seq_count
-    filter_local = lax.all_to_all(
-        long_filter[0].astype(jnp.bfloat16), "seq", split_axis=1, concat_axis=0, tiled=True
-    ).astype(jnp.float32)
-    spectrum = forward_spectrum(filter_local, inner)
     bias_part = lax.dynamic_slice_in_dim(filter_bias[0], seq_place * chans, chans, 0)
     weight_in = w_in[0]
     weight_out = w_out[0]
     taps = short_filter[0]
     contract = (((1,), (1,)), ((), ()))
 
+    held = {}
+
     def causal(series):
-        return channel_conv(series, spectrum, bias_part, False, inner)
+        return channel_conv(series, held["spectrum"], bias_part, False, inner)
 
     def adjoint(series):
-        return channel_conv(series, spectrum, bias_part, True, inner)
+        return channel_conv(series, held["spectrum"], bias_part, True, inner)
 
     forward = []
     for slot in range(micro):
@@ -120,7 +176,13 @@
         keys = mixed[:, width : 2 * width]
         values = mixed[:, 2 * width :]
         product = (keys * values).astype(jnp.bfloat16)
-        product_local = lax.all_to_all(product, "seq", split_axis=1, concat_axis=0, tiled=True)
+        if slot == 0:
+            both = jnp.stack([long_filter[0].astype(jnp.bfloat16), product])
+            both = lax.all_to_all(both, "seq", split_axis=2, concat_axis=1, tiled=True)
+            held["spectrum"] = forward_spectrum(both[0].astype(jnp.float32), inner)
+            product_local = both[1]
+        else:
+            product_local = lax.all_to_all(product, "seq", split_axis=1, concat_axis=0, tiled=True)
         conv = lax.all_to_all(causal(product_local), "seq", split_axis=0, concat_axis=1, tiled=True)
         forward.append((query, keys, values, conv.astype(jnp.float32)))
 
@@ -128,8 +190,11 @@
         query, keys, values, conv_wide = forward[slot]
         d_out = lax.dot_general(grad_out, weight_out, contract, preferred_element_type=jnp.float32)
         d_conv = (d_out * query).astype(jnp.bfloat16)
-        d_conv_local = lax.all_to_all(d_conv, "seq", split_axis=1, concat_axis=0, tiled=True)
-        d_prod = lax.all_to_all(adjoint(d_conv_local), "seq", split_axis=0, concat_axis=1, tiled=True)
+        sent = seq_exchange(d_conv.reshape(height, seq_count, chans).transpose(1, 2, 0))
+        d_conv_local = sent.transpose(0, 2, 1).reshape(length, chans)
+        d_prod_local = adjoint(d_conv_local)
+        back = seq_exchange(d_prod_local.reshape(seq_count, height, chans).transpose(0, 2, 1))
+        d_prod = back.transpose(2, 0, 1).reshape(height, width)
         d_prod_wide = d_prod.astype(jnp.float32)
         d_mixed = jnp.concatenate(
             [d_out * conv_wide, d_prod_wide * values, d_prod_wide * keys], axis=1

time: 540 us -> 534 us (0.989)
  Pallas kernels: 0 us -> 181 us
  blocking collectives: 95 us -> 0 us
  waiting for transfers between devices: 159 us -> 91.7 us
  starting transfers between devices: 89.4 us -> 45.4 us
  other arithmetic: 10.4 us -> 23.1 us
  local copies, waits for them, and re-layouts: 42.8 us -> 52 us
    pallas_call x0 -> x16, Pallas kernels: none -> 181 us  [seq_exchange(): pl.pallas_call(exchange_kernel, out_shape=jax.ShapeDtypeStruct(blocks.sha...]
    all_to_all x8 -> x0, blocking collectives: 95 us -> none  [stage(): lax.all_to_all(adjoint(d_conv_local), 'seq', split_axis=0, concat_axis=1,...]
    all_to_all x10 -> x1, waiting for transfers between devices: 78.5 us -> 9.3 us  [shards(): both = lax.all_to_all(both, 'seq', split_axis=2, concat_axis=1, tiled=True)]
    all_to_all x10 -> x1, starting transfers between devices: 52.5 us -> 7.21 us  [shards(): both = lax.all_to_all(both, 'seq', split_axis=2, concat_axis=1, tiled=True)]
    transpose x0 -> x8, local copies, waits for them, and re-layouts: none -> 7.64 us  [stage(): d_conv_local = sent.transpose(0, 2, 1).reshape(length, chans)]
    transpose x0 -> x8, other arithmetic: none -> 7.48 us  [stage(): d_prod_local.reshape(seq_count, height, chans).transpose(0, 2, 1)]
    convert_element_type x8, other arithmetic: 0.22 us -> 7.64 us  [stage(): d_prod_wide = d_prod.astype(jnp.float32)]
    while x208 -> x224, local copies, waits for them, and re-layouts: 9.13 us -> 13.4 us
  transfers between devices with their start and end apart: 28 -> 19, of which waited for: 27 -> 18; matrix products, arithmetic and copies ran while one was open for 2% -> 1% of each run, Pallas kernels for 0% -> 0%
where the time goes in v2:
time: 534 us; the launch traced here: 529 us
  Pallas kernels  181 us (34%)
  matrix products  132 us (25%)
  waiting for transfers between devices  91.7 us (17%)
  local copies, waits for them, and re-layouts  52 us (10%)
  starting transfers between devices  45.4 us (9%)
  other arithmetic  23.1 us (4%)
    pallas_call x16, Pallas kernels, seq_exchange(): pl.pallas_call(exchange_kernel, out_shape=jax.ShapeDtypeStruct(blocks.sha...  181 us
    ppermute x17, waiting for transfers between devices, shifted(): return lax.ppermute(value, axis, pairs)  74.7 us
    ppermute x17, starting transfers between devices, shifted(): return lax.ppermute(value, axis, pairs)  34.3 us
    dot_general x8, matrix products, stage(): lax.dot_general(d_proj, weight_in, contract, preferred_element_type=jnp.f...  26.7 us
    dot_general x8, matrix products, stage(): lax.dot_general(grad_out, weight_out, contract, preferred_element_type=jn...  17.1 us
    while x224, local copies, waits for them, and re-layouts  13.4 us
    div x18, local copies, waits for them, and re-layouts, inverse_spectrum(): return series.reshape(length, chans) / (2.0 * length)  11.3 us
    dot_general x10, matrix products, forward_spectrum(): real_one = jnp.einsum('kn,nbc->cbk', cos_outer, blocks, precision=accuracy)  10.8 us
  transfers between devices with their start and end apart: 19, of which 18 were waited for; matrix products, arithmetic and copies ran while one was open for 1% of the time, Pallas kernels for 0%

profile of v2, /device:TPU:1, one launch (start us, length us, event | category | flops | bytes accessed | tf_op | source)
XLA Modules:
  0.0 528.7 jit_solution(10760363456250345630)
XLA Ops:
  0.8 4.5 collective-permute-start.2
  10.8 7.2 %all-to-all-start = ((bf16[2,128,768]{1,0,2:T(2,128)(2,1)}), bf16[2,128,768]{1,0,2:T(2,128)(2,1)S(1)}, u32[]{:S(2)}, u32[]{:S(2)}) async-start(bf16[2,128,768]{1,0,2:T(2,128)(2,1)} %copy.146), calls=%async_computation | async-start | bytes 786432 | tf_op jit(solution)/shard_map/all_to_all | solution.py:181
  18.9 9.3 %all-to-all-done = bf16[2,128,768]{1,0,2:T(2,128)(2,1)S(1)} async-done(((bf16[2,128,768]{1,0,2:T(2,128)(2,1)}), bf16[2,128,768]{1,0,2:T(2,128)(2,1)S(1)}, u32[]{:S(2)}, u32[]{:S(2)}) %all-to-all-start) | async-done | bytes 393248 | tf_op jit(solution)/shard_map/all_to_all | solution.py:181
  34.2 2.0 subtract_bitcast_fusion.1
  47.5 2.7 copy.170
  53.0 3.9 all-to-all-start.1
  57.5 7.7 %all-to-all-done.1 = bf16[32,128,24]{1,2,0:T(8,128)(2,1)S(1)} async-done(((bf16[32,128,24]{1,2,0:T(8,128)(2,1)}), bf16[32,128,24]{1,2,0:T(8,128)(2,1)S(1)}, u32[]{:S(2)}, u32[]{:S(2)}) %all-to-all-start.1) | async-done | bytes 196640 | tf_op jit(solution)/shard_map/all_to_all | solution.py:186
  65.5 463.1 %while.19 = (s32[]{:T(128)}, bf16[128,768]{1,0:T(8,128)(2,1)S(1)}, bf16[1,128,768]{2,1,0:T(8,128)(2,1)}, pred[]{:T(512)}, bf16[1,128,768]{2,1,0:T(8,128)(2,1)S(1...) while((s32[]{:T(128)}, bf16[128,768]{1,0:T(8,128)(2,1)S(1)}, ...), condition=%wide.region_1.2_spmd.clone, body=%wide.region_0.1_spmd.clone.sunk | while | flops 1522793472 | bytes 68762376 | solution.py:231
  65.6 2.1 multiply_convert_fusion.7
  68.6 10.4 %eval_jaxpr.18 = bf16[32,24,128]{2,1,0:T(8,128)(2,1)} custom-call(bf16[32,24,128]{2,1,0:T(8,128)(2,1)} %bitcast.261), custom_call_target="tpu_custom_call" | custom-call | tf_op jit(solution)/shard_map/while/body/eval_jaxpr/pallas_call | solution.py:122
  92.4 10.7 %eval_jaxpr.19 = bf16[32,24,128]{2,1,0:T(8,128)(2,1)} custom-call(bf16[32,24,128]{2,1,0:T(8,128)(2,1)} %fusion.398.x_ref), custom_call_target="tpu_custom_call" | custom-call | tf_op jit(solution)/shard_map/while/body/eval_jaxpr/pallas_call | solution.py:122
  104.4 2.4 collective-permute-start
  106.9 2.6 collective-permute-done
  109.6 3.3 bitcast_select_fusion.4
  115.0 6.2 %collective-permute-done.1 = bf16[128,768]{1,0:T(8,128)(2,1)S(1)} collective-permute-done((bf16[128,768]{1,0:T(8,128)(2,1)S(1)}, bf16[128,768]{1,0:T(8,128)(2,1)S(1)}, u32[]{:S(2)}, u32[]{:S(2)}) %collective-permute-start.1) | collective-permute-done | bytes 196640 | tf_op jit(solution)/shard_map/while/body/eval_jaxpr/ppermute | solution.py:17
  121.4 2.1 multiply_convert_fusion.7
  124.4 11.9 %eval_jaxpr.18 = bf16[32,24,128]{2,1,0:T(8,128)(2,1)} custom-call(bf16[32,24,128]{2,1,0:T(8,128)(2,1)} %bitcast.261), custom_call_target="tpu_custom_call" | custom-call | tf_op jit(solution)/shard_map/while/body/eval_jaxpr/pallas_call | solution.py:122
  149.6 10.7 %eval_jaxpr.19 = bf16[32,24,128]{2,1,0:T(8,128)(2,1)} custom-call(bf16[32,24,128]{2,1,0:T(8,128)(2,1)} %fusion.398.x_ref), custom_call_target="tpu_custom_call" | custom-call | tf_op jit(solution)/shard_map/while/body/eval_jaxpr/pallas_call | solution.py:122
  161.6 2.4 collective-permute-start
  164.1 2.6 collective-permute-done
  166.8 3.3 bitcast_select_fusion.4
  172.1 6.2 %collective-permute-done.1 = bf16[128,768]{1,0:T(8,128)(2,1)S(1)} collective-permute-done((bf16[128,768]{1,0:T(8,128)(2,1)S(1)}, bf16[128,768]{1,0:T(8,128)(2,1)S(1)}, u32[]{:S(2)}, u32[]{:S(2)}) %collective-permute-start.1) | collective-permute-done | bytes 196640 | tf_op jit(solution)/shard_map/while/body/eval_jaxpr/ppermute | solution.py:17
  178.5 2.1 multiply_convert_fusion.7
  181.5 12.2 %eval_jaxpr.18 = bf16[32,24,128]{2,1,0:T(8,128)(2,1)} custom-call(bf16[32,24,128]{2,1,0:T(8,128)(2,1)} %bitcast.261), custom_call_target="tpu_custom_call" | custom-call | tf_op jit(solution)/shard_map/while/body/eval_jaxpr/pallas_call | solution.py:122
  207.1 10.7 %eval_jaxpr.19 = bf16[32,24,128]{2,1,0:T(8,128)(2,1)} custom-call(bf16[32,24,128]{2,1,0:T(8,128)(2,1)} %fusion.398.x_ref), custom_call_target="tpu_custom_call" | custom-call | tf_op jit(solution)/shard_map/while/body/eval_jaxpr/pallas_call | solution.py:122
  219.1 2.4 collective-permute-start
  221.6 2.6 collective-permute-done
  224.3 3.3 bitcast_select_fusion.4
  229.6 6.2 %collective-permute-done.1 = bf16[128,768]{1,0:T(8,128)(2,1)S(1)} collective-permute-done((bf16[128,768]{1,0:T(8,128)(2,1)S(1)}, bf16[128,768]{1,0:T(8,128)(2,1)S(1)}, u32[]{:S(2)}, u32[]{:S(2)}) %collective-permute-start.1) | collective-permute-done | bytes 196640 | tf_op jit(solution)/shard_map/while/body/eval_jaxpr/ppermute | solution.py:17
  236.0 2.1 multiply_convert_fusion.7
  239.0 12.2 %eval_jaxpr.18 = bf16[32,24,128]{2,1,0:T(8,128)(2,1)} custom-call(bf16[32,24,128]{2,1,0:T(8,128)(2,1)} %bitcast.261), custom_call_target="tpu_custom_call" | custom-call | tf_op jit(solution)/shard_map/while/body/eval_jaxpr/pallas_call | solution.py:122
  264.6 10.7 %eval_jaxpr.19 = bf16[32,24,128]{2,1,0:T(8,128)(2,1)} custom-call(bf16[32,24,128]{2,1,0:T(8,128)(2,1)} %fusion.398.x_ref), custom_call_target="tpu_custom_call" | custom-call | tf_op jit(solution)/shard_map/while/body/eval_jaxpr/pallas_call | solution.py:122
  276.5 2.4 collective-permute-start
  279.1 2.6 collective-permute-done
  281.8 3.3 bitcast_select_fusion.4
  287.1 7.3 %collective-permute-done.1 = bf16[128,768]{1,0:T(8,128)(2,1)S(1)} collective-permute-done((bf16[128,768]{1,0:T(8,128)(2,1)S(1)}, bf16[128,768]{1,0:T(8,128)(2,1)S(1)}, u32[]{:S(2)}, u32[]{:S(2)}) %collective-permute-start.1) | collective-permute-done | bytes 196640 | tf_op jit(solution)/shard_map/while/body/eval_jaxpr/ppermute | solution.py:17
  294.6 2.1 multiply_convert_fusion.7
  297.6 12.3 %eval_jaxpr.18 = bf16[32,24,128]{2,1,0:T(8,128)(2,1)} custom-call(bf16[32,24,128]{2,1,0:T(8,128)(2,1)} %bitcast.261), custom_call_target="tpu_custom_call" | custom-call | tf_op jit(solution)/shard_map/while/body/eval_jaxpr/pallas_call | solution.py:122
  323.3 10.7 %eval_jaxpr.19 = bf16[32,24,128]{2,1,0:T(8,128)(2,1)} custom-call(bf16[32,24,128]{2,1,0:T(8,128)(2,1)} %fusion.398.x_ref), custom_call_target="tpu_custom_call" | custom-call | tf_op jit(solution)/shard_map/while/body/eval_jaxpr/pallas_call | solution.py:122
  335.2 2.4 collective-permute-start
  337.8 2.6 collective-permute-done
  340.5 3.3 bitcast_select_fusion.4
  345.8 7.1 %collective-permute-done.1 = bf16[128,768]{1,0:T(8,128)(2,1)S(1)} collective-permute-done((bf16[128,768]{1,0:T(8,128)(2,1)S(1)}, bf16[128,768]{1,0:T(8,128)(2,1)S(1)}, u32[]{:S(2)}, u32[]{:S(2)}) %collective-permute-start.1) | collective-permute-done | bytes 196640 | tf_op jit(solution)/shard_map/while/body/eval_jaxpr/ppermute | solution.py:17
  353.2 2.1 multiply_convert_fusion.7
  356.1 12.3 %eval_jaxpr.18 = bf16[32,24,128]{2,1,0:T(8,128)(2,1)} custom-call(bf16[32,24,128]{2,1,0:T(8,128)(2,1)} %bitcast.261), custom_call_target="tpu_custom_call" | custom-call | tf_op jit(solution)/shard_map/while/body/eval_jaxpr/pallas_call | solution.py:122
  381.8 10.7 %eval_jaxpr.19 = bf16[32,24,128]{2,1,0:T(8,128)(2,1)} custom-call(bf16[32,24,128]{2,1,0:T(8,128)(2,1)} %fusion.398.x_ref), custom_call_target="tpu_custom_call" | custom-call | tf_op jit(solution)/shard_map/while/body/eval_jaxpr/pallas_call | solution.py:122
  393.8 2.4 collective-permute-start
  396.3 2.6 collective-permute-done
  399.0 3.3 bitcast_select_fusion.4
  404.3 7.1 %collective-permute-done.1 = bf16[128,768]{1,0:T(8,128)(2,1)S(1)} collective-permute-done((bf16[128,768]{1,0:T(8,128)(2,1)S(1)}, bf16[128,768]{1,0:T(8,128)(2,1)S(1)}, u32[]{:S(2)}, u32[]{:S(2)}) %collective-permute-start.1) | collective-permute-done | bytes 196640 | tf_op jit(solution)/shard_map/while/body/eval_jaxpr/ppermute | solution.py:17
  411.7 2.1 multiply_convert_fusion.7
  414.7 12.3 %eval_jaxpr.18 = bf16[32,24,128]{2,1,0:T(8,128)(2,1)} custom-call(bf16[32,24,128]{2,1,0:T(8,128)(2,1)} %bitcast.261), custom_call_target="tpu_custom_call" | custom-call | tf_op jit(solution)/shard_map/while/body/eval_jaxpr/pallas_call | solution.py:122
  440.4 10.7 %eval_jaxpr.19 = bf16[32,24,128]{2,1,0:T(8,128)(2,1)} custom-call(bf16[32,24,128]{2,1,0:T(8,128)(2,1)} %fusion.398.x_ref), custom_call_target="tpu_custom_call" | custom-call | tf_op jit(solution)/shard_map/while/body/eval_jaxpr/pallas_call | solution.py:122
  452.3 2.4 collective-permute-start
  454.8 2.6 collective-permute-done
  457.5 3.3 bitcast_select_fusion.4
  462.9 7.1 %collective-permute-done.1 = bf16[128,768]{1,0:T(8,128)(2,1)S(1)} collective-permute-done((bf16[128,768]{1,0:T(8,128)(2,1)S(1)}, bf16[128,768]{1,0:T(8,128)(2,1)S(1)}, u32[]{:S(2)}, u32[]{:S(2)}) %collective-permute-start.1) | collective-permute-done | bytes 196640 | tf_op jit(solution)/shard_map/while/body/eval_jaxpr/ppermute | solution.py:17
  470.2 2.1 multiply_convert_fusion.7
  473.2 12.3 %eval_jaxpr.18 = bf16[32,24,128]{2,1,0:T(8,128)(2,1)} custom-call(bf16[32,24,128]{2,1,0:T(8,128)(2,1)} %bitcast.261), custom_call_target="tpu_custom_call" | custom-call | tf_op jit(solution)/shard_map/while/body/eval_jaxpr/pallas_call | solution.py:122
  498.9 10.7 %eval_jaxpr.19 = bf16[32,24,128]{2,1,0:T(8,128)(2,1)} custom-call(bf16[32,24,128]{2,1,0:T(8,128)(2,1)} %fusion.398.x_ref), custom_call_target="tpu_custom_call" | custom-call | tf_op jit(solution)/shard_map/while/body/eval_jaxpr/pallas_call | solution.py:122
  510.8 2.4 collective-permute-start
  513.4 2.6 collective-permute-done
  516.1 3.3 bitcast_select_fusion.4
  521.4 7.1 %collective-permute-done.1 = bf16[128,768]{1,0:T(8,128)(2,1)S(1)} collective-permute-done((bf16[128,768]{1,0:T(8,128)(2,1)S(1)}, bf16[128,768]{1,0:T(8,128)(2,1)S(1)}, u32[]{:S(2)}, u32[]{:S(2)}) %collective-permute-start.1) | collective-permute-done | bytes 196640 | tf_op jit(solution)/shard_map/while/body/eval_jaxpr/ppermute | solution.py:17
  (509 shorter events, 168.5 us)
Async XLA Ops:
  0.0 18.0 %copy-start = (f32[1,768]{1,0:T(1,128)S(1)}, f32[1,768]{1,0:T(1,128)}, u32[]{:S(2)}) copy-start(f32[1,768]{1,0:T(1,128)} %param.15) | copy-start | bytes 9220
  0.8 6.4 %collective-permute-start.2 = (bf16[2,2304]{1,0:T(2,128)(2,1)S(1)}, bf16[2,2304]{1,0:T(2,128)(2,1)S(1)}, u32[]{:S(2)}, u32[]{:S(2)}) collective-permute-start(bf16[2,2304]{1,0:T(2,128)(2,1)S(1)} %slice_bitcast_fusion), channel_id=1, source_target_pairs={{0,8},{8,16},{16,24},{24,32},{32,40},{40,48},{48,56},{56,64},{64,7... | collective-permute-start | bytes 27656 | tf_op jit(solution)/shard_map/ppermute | solution.py:17
  10.8 17.4 %all-to-all-start = ((bf16[2,128,768]{1,0,2:T(2,128)(2,1)}), bf16[2,128,768]{1,0,2:T(2,128)(2,1)S(1)}, u32[]{:S(2)}, u32[]{:S(2)}) async-start(bf16[2,128,768]{1,0,2:T(2,128)(2,1)} %copy.146), calls=%async_computation | async-start | bytes 786432 | tf_op jit(solution)/shard_map/all_to_all | solution.py:181
  50.2 6.7 %copy-start.20 = (f32[1,3,2304]{2,0,1:T(1,128)S(1)}, f32[1,3,2304]{2,0,1:T(1,128)}, u32[]{:S(2)}) copy-start(f32[1,3,2304]{2,0,1:T(1,128)} %param.13) | copy-start | bytes 82948
  50.2 7.3 %copy-start.11 = (bf16[1,128,768]{2,1,0:T(8,128)(2,1)S(1)}, bf16[1,128,768]{2,1,0:T(8,128)(2,1)}, u32[]{:S(2)}) copy-start(bf16[1,128,768]{2,1,0:T(8,128)(2,1)} %param.9) | copy-start | bytes 589828
  53.0 12.3 %all-to-all-start.1 = ((bf16[32,128,24]{1,2,0:T(8,128)(2,1)}), bf16[32,128,24]{1,2,0:T(8,128)(2,1)S(1)}, u32[]{:S(2)}, u32[]{:S(2)}) async-start(bf16[32,128,24]{1,2,0:T(8,128)(2,1)} %fusion.162), calls=%async_computation.1 | async-start | bytes 393216 | tf_op jit(solution)/shard_map/all_to_all | solution.py:186
  91.5 12.8 %copy-start.7 = (f32[128,768]{1,0:T(8,128)S(1)}, f32[128,768]{1,0:T(8,128)}, u32[]{:S(2)}) copy-start(f32[128,768]{1,0:T(8,128)} %get-tuple-element.756) | copy-start | bytes 1179652 | tf_op jit(solution)/shard_map/while
  91.5 12.8 %copy-start.8 = (f32[128,768]{1,0:T(8,128)S(1)}, f32[128,768]{1,0:T(8,128)}, u32[]{:S(2)}) copy-start(f32[128,768]{1,0:T(8,128)} %get-tuple-element.755) | copy-start | bytes 1179652 | tf_op jit(solution)/shard_map/while
  104.4 5.2 copy-start.10
  104.4 5.2 copy-start.21
  104.4 5.1 collective-permute-start
  109.6 11.5 %copy-start.12 = (bf16[1,128,768]{2,1,0:T(8,128)(2,1)S(1)}, bf16[1,128,768]{2,1,0:T(8,128)(2,1)}, u32[]{:S(2)}) copy-start(bf16[1,128,768]{2,1,0:T(8,128)(2,1)} %get-tuple-element.779) | copy-start | bytes 589828 | tf_op jit(solution)/shard_map/while
  109.6 11.5 %copy-start.4 = (f32[24,32,256]{2,1,0:T(8,128)S(1)}, f32[24,32,256]{2,1,0:T(8,128)}, u32[]{:S(2)}) copy-start(f32[24,32,256]{2,1,0:T(8,128)} %copy-done.2) | copy-start | bytes 2359300 | tf_op jit(solution)/shard_map/while
  109.6 11.5 %copy-start.6 = (f32[128,768]{1,0:T(8,128)S(1)}, f32[128,768]{1,0:T(8,128)}, u32[]{:S(2)}) copy-start(f32[128,768]{1,0:T(8,128)} %copy-done.5) | copy-start | bytes 1179652 | tf_op jit(solution)/shard_map/while
  113.7 7.5 %collective-permute-start.1 = (bf16[128,768]{1,0:T(8,128)(2,1)S(1)}, bf16[128,768]{1,0:T(8,128)(2,1)S(1)}, u32[]{:S(2)}, u32[]{:S(2)}) collective-permute-start(bf16[128,768]{1,0:T(8,128)(2,1)S(1)} %get-tuple-element.705), channel_id=1, source_target_pairs={{1,0},{2,1},{3,2},{4,3},{5,4},{6,5},{7,6},{9,8},{10,9},{11,10},{12... | collective-permute-start | bytes 589832 | tf_op jit(solution)/shard_map/while/body/eval_jaxpr/ppermute | solution.py:17
  148.7 12.7 %copy-start.7 = (f32[128,768]{1,0:T(8,128)S(1)}, f32[128,768]{1,0:T(8,128)}, u32[]{:S(2)}) copy-start(f32[128,768]{1,0:T(8,128)} %get-tuple-element.756) | copy-start | bytes 1179652 | tf_op jit(solution)/shard_map/while
  148.7 12.8 %copy-start.8 = (f32[128,768]{1,0:T(8,128)S(1)}, f32[128,768]{1,0:T(8,128)}, u32[]{:S(2)}) copy-start(f32[128,768]{1,0:T(8,128)} %get-tuple-element.755) | copy-start | bytes 1179652 | tf_op jit(solution)/shard_map/while
  161.6 5.1 collective-permute-start
  166.8 11.5 %copy-start.12 = (bf16[1,128,768]{2,1,0:T(8,128)(2,1)S(1)}, bf16[1,128,768]{2,1,0:T(8,128)(2,1)}, u32[]{:S(2)}) copy-start(bf16[1,128,768]{2,1,0:T(8,128)(2,1)} %get-tuple-element.779) | copy-start | bytes 589828 | tf_op jit(solution)/shard_map/while
  166.8 11.5 %copy-start.4 = (f32[24,32,256]{2,1,0:T(8,128)S(1)}, f32[24,32,256]{2,1,0:T(8,128)}, u32[]{:S(2)}) copy-start(f32[24,32,256]{2,1,0:T(8,128)} %copy-done.2) | copy-start | bytes 2359300 | tf_op jit(solution)/shard_map/while
  166.8 11.5 %copy-start.6 = (f32[128,768]{1,0:T(8,128)S(1)}, f32[128,768]{1,0:T(8,128)}, u32[]{:S(2)}) copy-start(f32[128,768]{1,0:T(8,128)} %copy-done.5) | copy-start | bytes 1179652 | tf_op jit(solution)/shard_map/while
  170.8 7.5 %collective-permute-start.1 = (bf16[128,768]{1,0:T(8,128)(2,1)S(1)}, bf16[128,768]{1,0:T(8,128)(2,1)S(1)}, u32[]{:S(2)}, u32[]{:S(2)}) collective-permute-start(bf16[128,768]{1,0:T(8,128)(2,1)S(1)} %get-tuple-element.705), channel_id=1, source_target_pairs={{1,0},{2,1},{3,2},{4,3},{5,4},{6,5},{7,6},{9,8},{10,9},{11,10},{12... | collective-permute-start | bytes 589832 | tf_op jit(solution)/shard_map/while/body/eval_jaxpr/ppermute | solution.py:17
  206.2 12.7 %copy-start.7 = (f32[128,768]{1,0:T(8,128)S(1)}, f32[128,768]{1,0:T(8,128)}, u32[]{:S(2)}) copy-start(f32[128,768]{1,0:T(8,128)} %get-tuple-element.756) | copy-start | bytes 1179652 | tf_op jit(solution)/shard_map/while
  206.2 12.8 %copy-start.8 = (f32[128,768]{1,0:T(8,128)S(1)}, f32[128,768]{1,0:T(8,128)}, u32[]{:S(2)}) copy-start(f32[128,768]{1,0:T(8,128)} %get-tuple-element.755) | copy-start | bytes 1179652 | tf_op jit(solution)/shard_map/while
  219.1 5.1 collective-permute-start
  224.3 11.5 %copy-start.12 = (bf16[1,128,768]{2,1,0:T(8,128)(2,1)S(1)}, bf16[1,128,768]{2,1,0:T(8,128)(2,1)}, u32[]{:S(2)}) copy-start(bf16[1,128,768]{2,1,0:T(8,128)(2,1)} %get-tuple-element.779) | copy-start | bytes 589828 | tf_op jit(solution)/shard_map/while
  224.3 11.5 %copy-start.4 = (f32[24,32,256]{2,1,0:T(8,128)S(1)}, f32[24,32,256]{2,1,0:T(8,128)}, u32[]{:S(2)}) copy-start(f32[24,32,256]{2,1,0:T(8,128)} %copy-done.2) | copy-start | bytes 2359300 | tf_op jit(solution)/shard_map/while
  224.3 11.5 %copy-start.6 = (f32[128,768]{1,0:T(8,128)S(1)}, f32[128,768]{1,0:T(8,128)}, u32[]{:S(2)}) copy-start(f32[128,768]{1,0:T(8,128)} %copy-done.5) | copy-start | bytes 1179652 | tf_op jit(solution)/shard_map/while
  228.3 7.5 %collective-permute-start.1 = (bf16[128,768]{1,0:T(8,128)(2,1)S(1)}, bf16[128,768]{1,0:T(8,128)(2,1)S(1)}, u32[]{:S(2)}, u32[]{:S(2)}) collective-permute-start(bf16[128,768]{1,0:T(8,128)(2,1)S(1)} %get-tuple-element.705), channel_id=1, source_target_pairs={{1,0},{2,1},{3,2},{4,3},{5,4},{6,5},{7,6},{9,8},{10,9},{11,10},{12... | collective-permute-start | bytes 589832 | tf_op jit(solution)/shard_map/while/body/eval_jaxpr/ppermute | solution.py:17
  263.7 12.7 %copy-start.7 = (f32[128,768]{1,0:T(8,128)S(1)}, f32[128,768]{1,0:T(8,128)}, u32[]{:S(2)}) copy-start(f32[128,768]{1,0:T(8,128)} %get-tuple-element.756) | copy-start | bytes 1179652 | tf_op jit(solution)/shard_map/while
  263.7 12.8 %copy-start.8 = (f32[128,768]{1,0:T(8,128)S(1)}, f32[128,768]{1,0:T(8,128)}, u32[]{:S(2)}) copy-start(f32[128,768]{1,0:T(8,128)} %get-tuple-element.755) | copy-start | bytes 1179652 | tf_op jit(solution)/shard_map/while
  276.5 5.1 collective-permute-start
  281.8 12.6 %copy-start.12 = (bf16[1,128,768]{2,1,0:T(8,128)(2,1)S(1)}, bf16[1,128,768]{2,1,0:T(8,128)(2,1)}, u32[]{:S(2)}) copy-start(bf16[1,128,768]{2,1,0:T(8,128)(2,1)} %get-tuple-element.779) | copy-start | bytes 589828 | tf_op jit(solution)/shard_map/while
  281.8 12.6 %copy-start.4 = (f32[24,32,256]{2,1,0:T(8,128)S(1)}, f32[24,32,256]{2,1,0:T(8,128)}, u32[]{:S(2)}) copy-start(f32[24,32,256]{2,1,0:T(8,128)} %copy-done.2) | copy-start | bytes 2359300 | tf_op jit(solution)/shard_map/while
  281.8 12.6 %copy-start.6 = (f32[128,768]{1,0:T(8,128)S(1)}, f32[128,768]{1,0:T(8,128)}, u32[]{:S(2)}) copy-start(f32[128,768]{1,0:T(8,128)} %copy-done.5) | copy-start | bytes 1179652 | tf_op jit(solution)/shard_map/while
  285.8 8.6 %collective-permute-start.1 = (bf16[128,768]{1,0:T(8,128)(2,1)S(1)}, bf16[128,768]{1,0:T(8,128)(2,1)S(1)}, u32[]{:S(2)}, u32[]{:S(2)}) collective-permute-start(bf16[128,768]{1,0:T(8,128)(2,1)S(1)} %get-tuple-element.705), channel_id=1, source_target_pairs={{1,0},{2,1},{3,2},{4,3},{5,4},{6,5},{7,6},{9,8},{10,9},{11,10},{12... | collective-permute-start | bytes 589832 | tf_op jit(solution)/shard_map/while/body/eval_jaxpr/ppermute | solution.py:17
  322.4 12.7 %copy-start.7 = (f32[128,768]{1,0:T(8,128)S(1)}, f32[128,768]{1,0:T(8,128)}, u32[]{:S(2)}) copy-start(f32[128,768]{1,0:T(8,128)} %get-tuple-element.756) | copy-start | bytes 1179652 | tf_op jit(solution)/shard_map/while
  322.4 12.8 %copy-start.8 = (f32[128,768]{1,0:T(8,128)S(1)}, f32[128,768]{1,0:T(8,128)}, u32[]{:S(2)}) copy-start(f32[128,768]{1,0:T(8,128)} %get-tuple-element.755) | copy-start | bytes 1179652 | tf_op jit(solution)/shard_map/while
  335.2 5.1 collective-permute-start
  340.5 12.5 %copy-start.12 = (bf16[1,128,768]{2,1,0:T(8,128)(2,1)S(1)}, bf16[1,128,768]{2,1,0:T(8,128)(2,1)}, u32[]{:S(2)}) copy-start(bf16[1,128,768]{2,1,0:T(8,128)(2,1)} %get-tuple-element.779) | copy-start | bytes 589828 | tf_op jit(solution)/shard_map/while
  340.5 12.5 %copy-start.4 = (f32[24,32,256]{2,1,0:T(8,128)S(1)}, f32[24,32,256]{2,1,0:T(8,128)}, u32[]{:S(2)}) copy-start(f32[24,32,256]{2,1,0:T(8,128)} %copy-done.2) | copy-start | bytes 2359300 | tf_op jit(solution)/shard_map/while
  340.5 12.5 %copy-start.6 = (f32[128,768]{1,0:T(8,128)S(1)}, f32[128,768]{1,0:T(8,128)}, u32[]{:S(2)}) copy-start(f32[128,768]{1,0:T(8,128)} %copy-done.5) | copy-start | bytes 1179652 | tf_op jit(solution)/shard_map/while
  344.5 8.4 %collective-permute-start.1 = (bf16[128,768]{1,0:T(8,128)(2,1)S(1)}, bf16[128,768]{1,0:T(8,128)(2,1)S(1)}, u32[]{:S(2)}, u32[]{:S(2)}) collective-permute-start(bf16[128,768]{1,0:T(8,128)(2,1)S(1)} %get-tuple-element.705), channel_id=1, source_target_pairs={{1,0},{2,1},{3,2},{4,3},{5,4},{6,5},{7,6},{9,8},{10,9},{11,10},{12... | collective-permute-start | bytes 589832 | tf_op jit(solution)/shard_map/while/body/eval_jaxpr/ppermute | solution.py:17
  380.9 12.7 %copy-start.7 = (f32[128,768]{1,0:T(8,128)S(1)}, f32[128,768]{1,0:T(8,128)}, u32[]{:S(2)}) copy-start(f32[128,768]{1,0:T(8,128)} %get-tuple-element.756) | copy-start | bytes 1179652 | tf_op jit(solution)/shard_map/while
  380.9 12.8 %copy-start.8 = (f32[128,768]{1,0:T(8,128)S(1)}, f32[128,768]{1,0:T(8,128)}, u32[]{:S(2)}) copy-start(f32[128,768]{1,0:T(8,128)} %get-tuple-element.755) | copy-start | bytes 1179652 | tf_op jit(solution)/shard_map/while
  393.8 5.1 collective-permute-start
  399.0 12.5 %copy-start.12 = (bf16[1,128,768]{2,1,0:T(8,128)(2,1)S(1)}, bf16[1,128,768]{2,1,0:T(8,128)(2,1)}, u32[]{:S(2)}) copy-start(bf16[1,128,768]{2,1,0:T(8,128)(2,1)} %get-tuple-element.779) | copy-start | bytes 589828 | tf_op jit(solution)/shard_map/while
  399.0 12.5 %copy-start.4 = (f32[24,32,256]{2,1,0:T(8,128)S(1)}, f32[24,32,256]{2,1,0:T(8,128)}, u32[]{:S(2)}) copy-start(f32[24,32,256]{2,1,0:T(8,128)} %copy-done.2) | copy-start | bytes 2359300 | tf_op jit(solution)/shard_map/while
  399.0 12.5 %copy-start.6 = (f32[128,768]{1,0:T(8,128)S(1)}, f32[128,768]{1,0:T(8,128)}, u32[]{:S(2)}) copy-start(f32[128,768]{1,0:T(8,128)} %copy-done.5) | copy-start | bytes 1179652 | tf_op jit(solution)/shard_map/while
  403.0 8.4 %collective-permute-start.1 = (bf16[128,768]{1,0:T(8,128)(2,1)S(1)}, bf16[128,768]{1,0:T(8,128)(2,1)S(1)}, u32[]{:S(2)}, u32[]{:S(2)}) collective-permute-start(bf16[128,768]{1,0:T(8,128)(2,1)S(1)} %get-tuple-element.705), channel_id=1, source_target_pairs={{1,0},{2,1},{3,2},{4,3},{5,4},{6,5},{7,6},{9,8},{10,9},{11,10},{12... | collective-permute-start | bytes 589832 | tf_op jit(solution)/shard_map/while/body/eval_jaxpr/ppermute | solution.py:17
  439.4 12.7 %copy-start.7 = (f32[128,768]{1,0:T(8,128)S(1)}, f32[128,768]{1,0:T(8,128)}, u32[]{:S(2)}) copy-start(f32[128,768]{1,0:T(8,128)} %get-tuple-element.756) | copy-start | bytes 1179652 | tf_op jit(solution)/shard_map/while
  439.4 12.8 %copy-start.8 = (f32[128,768]{1,0:T(8,128)S(1)}, f32[128,768]{1,0:T(8,128)}, u32[]{:S(2)}) copy-start(f32[128,768]{1,0:T(8,128)} %get-tuple-element.755) | copy-start | bytes 1179652 | tf_op jit(solution)/shard_map/while
  452.3 5.1 collective-permute-start
  457.5 12.5 %copy-start.12 = (bf16[1,128,768]{2,1,0:T(8,128)(2,1)S(1)}, bf16[1,128,768]{2,1,0:T(8,128)(2,1)}, u32[]{:S(2)}) copy-start(bf16[1,128,768]{2,1,0:T(8,128)(2,1)} %get-tuple-element.779) | copy-start | bytes 589828 | tf_op jit(solution)/shard_map/while
  457.5 12.5 %copy-start.4 = (f32[24,32,256]{2,1,0:T(8,128)S(1)}, f32[24,32,256]{2,1,0:T(8,128)}, u32[]{:S(2)}) copy-start(f32[24,32,256]{2,1,0:T(8,128)} %copy-done.2) | copy-start | bytes 2359300 | tf_op jit(solution)/shard_map/while
  457.5 12.5 %copy-start.6 = (f32[128,768]{1,0:T(8,128)S(1)}, f32[128,768]{1,0:T(8,128)}, u32[]{:S(2)}) copy-start(f32[128,768]{1,0:T(8,128)} %copy-done.5) | copy-start | bytes 1179652 | tf_op jit(solution)/shard_map/while
  461.6 8.4 %collective-permute-start.1 = (bf16[128,768]{1,0:T(8,128)(2,1)S(1)}, bf16[128,768]{1,0:T(8,128)(2,1)S(1)}, u32[]{:S(2)}, u32[]{:S(2)}) collective-permute-start(bf16[128,768]{1,0:T(8,128)(2,1)S(1)} %get-tuple-element.705), channel_id=1, source_target_pairs={{1,0},{2,1},{3,2},{4,3},{5,4},{6,5},{7,6},{9,8},{10,9},{11,10},{12... | collective-permute-start | bytes 589832 | tf_op jit(solution)/shard_map/while/body/eval_jaxpr/ppermute | solution.py:17
  497.9 12.7 %copy-start.7 = (f32[128,768]{1,0:T(8,128)S(1)}, f32[128,768]{1,0:T(8,128)}, u32[]{:S(2)}) copy-start(f32[128,768]{1,0:T(8,128)} %get-tuple-element.756) | copy-start | bytes 1179652 | tf_op jit(solution)/shard_map/while
  497.9 12.8 %copy-start.8 = (f32[128,768]{1,0:T(8,128)S(1)}, f32[128,768]{1,0:T(8,128)}, u32[]{:S(2)}) copy-start(f32[128,768]{1,0:T(8,128)} %get-tuple-element.755) | copy-start | bytes 1179652 | tf_op jit(solution)/shard_map/while
  510.8 5.1 collective-permute-start
  516.0 12.5 %copy-start.12 = (bf16[1,128,768]{2,1,0:T(8,128)(2,1)S(1)}, bf16[1,128,768]{2,1,0:T(8,128)(2,1)}, u32[]{:S(2)}) copy-start(bf16[1,128,768]{2,1,0:T(8,128)(2,1)} %get-tuple-element.779) | copy-start | bytes 589828 | tf_op jit(solution)/shard_map/while
  516.1 12.5 %copy-start.4 = (f32[24,32,256]{2,1,0:T(8,128)S(1)}, f32[24,32,256]{2,1,0:T(8,128)}, u32[]{:S(2)}) copy-start(f32[24,32,256]{2,1,0:T(8,128)} %copy-done.2) | copy-start | bytes 2359300 | tf_op jit(solution)/shard_map/while
  516.1 12.5 %copy-start.6 = (f32[128,768]{1,0:T(8,128)S(1)}, f32[128,768]{1,0:T(8,128)}, u32[]{:S(2)}) copy-start(f32[128,768]{1,0:T(8,128)} %copy-done.5) | copy-start | bytes 1179652 | tf_op jit(solution)/shard_map/while
  520.1 8.4 %collective-permute-start.1 = (bf16[128,768]{1,0:T(8,128)(2,1)S(1)}, bf16[128,768]{1,0:T(8,128)(2,1)S(1)}, u32[]{:S(2)}, u32[]{:S(2)}) collective-permute-start(bf16[128,768]{1,0:T(8,128)(2,1)S(1)} %get-tuple-element.705), channel_id=1, source_target_pairs={{1,0},{2,1},{3,2},{4,3},{5,4},{6,5},{7,6},{9,8},{10,9},{11,10},{12... | collective-permute-start | bytes 589832 | tf_op jit(solution)/shard_map/while/body/eval_jaxpr/ppermute | solution.py:17
  (76 other events, 178.0 us)

commit v3 on v2

--- a/solution.py
+++ b/solution.py
@@ -131,6 +131,120 @@
         ],
         compiler_params=pltpu.CompilerParams(collective_id=0, has_side_effects=True),
     )(blocks)
+
+
+def finish_kernel(
+    sent_ref, d_out_ref, conv_ref, values_ref, keys_ref, grad_ref, taps_ref, weight_ref,
+    o_ref, landed, extended, head, send_sems, recv_sems, rim_sems,
+):
+    count = lax.axis_size("seq")
+    rows, width = d_out_ref.shape
+    chans = sent_ref.shape[0] // count
+    me = lax.axis_index("seq")
+    section = lax.axis_index("section")
+    mesh_ids = pl.DeviceIdType.MESH
+    barrier = pltpu.get_barrier_semaphore()
+
+    def greet(k, _):
+        peer = lax.rem(me + k, count)
+        pl.semaphore_signal(barrier, inc=1, device_id=(peer, section), device_id_type=mesh_ids)
+        return 0
+
+    lax.fori_loop(1, count, greet, 0)
+    pl.semaphore_wait(barrier, count - 1)
+
+    def describe(k):
+        peer = lax.rem(me + k, count)
+        return pltpu.make_async_remote_copy(
+            src_ref=sent_ref.at[pl.ds(pl.multiple_of(peer * chans, 8), chans)],
+            dst_ref=landed.at[pl.ds(pl.multiple_of(me * chans, 8), chans)],
+            send_sem=send_sems.at[k],
+            recv_sem=recv_sems.at[k],
+            device_id=(peer, section),
+            device_id_type=mesh_ids,
+        )
+
+    def send(k, _):
+        describe(k).start()
+        return 0
+
+    def finish(k, _):
+        describe(k).wait()
+        return 0
+
+    lax.fori_loop(1, count, send, 0)
+    own = pl.ds(pl.multiple_of(me * chans, 8), chans)
+    landed[own] = sent_ref[own]
+    lax.fori_loop(1, count, finish, 0)
+
+    d_prod = landed[...].T
+    d_mixed = jnp.concatenate(
+        [
+            (d_out_ref[...] * conv_ref[...]).astype(jnp.bfloat16),
+            (d_prod * values_ref[...]).astype(jnp.bfloat16),
+            (d_prod * keys_ref[...]).astype(jnp.bfloat16),
+        ],
+        axis=1,
+    ).astype(jnp.float32)
+    head[...] = d_mixed[:8]
+    rim = pltpu.make_async_remote_copy(
+        src_ref=head,
+        dst_ref=extended.at[pl.ds(rows, 8)],
+        send_sem=rim_sems.at[0],
+        recv_sem=rim_sems.at[1],
+        device_id=(jnp.maximum(me - 1, 0), section),
+        device_id_type=mesh_ids,
+    )
+
+    @pl.when(me > 0)
+    def _():
+        rim.start()
+
+    extended[pl.ds(0, rows)] = d_mixed
+
+    @pl.when(me == count - 1)
+    def _():
+        extended[pl.ds(rows, 8)] = jnp.zeros((8, extended.shape[1]), jnp.float32)
+
+    @pl.when(me < count - 1)
+    def _():
+        rim.wait_recv()
+
+    taps = taps_ref[...]
+    d_proj = (
+        taps[0:1] * extended[pl.ds(0, rows)]
+        + taps[1:2] * extended[pl.ds(1, rows)]
+        + taps[2:3] * extended[pl.ds(2, rows)]
+    ).astype(jnp.bfloat16)
+    total = grad_ref[...].astype(jnp.float32) + lax.dot_general(
+        d_proj, weight_ref[...], (((1,), (1,)), ((), ())), preferred_element_type=jnp.float32
+    )
+    o_ref[...] = total.astype(o_ref.dtype)
+
+    @pl.when(me > 0)
+    def _():
+        rim.wait_send()
+
+
+def exchange_and_finish(sent, d_out, conv_wide, values, keys, grad_out, taps, weight_in):
+    count = lax.axis_size("seq")
+    rows, width = d_out.shape
+    vmem = pl.BlockSpec(memory_space=pltpu.VMEM)
+    return pl.pallas_call(
+        finish_kernel,
+        out_shape=jax.ShapeDtypeStruct(grad_out.shape, grad_out.dtype),
+        in_specs=[vmem] * 8,
+        out_specs=vmem,
+        scratch_shapes=[
+            pltpu.VMEM(sent.shape, jnp.float32),
+            pltpu.VMEM((rows + 8, taps.shape[1]), jnp.float32),
+            pltpu.VMEM((8, taps.shape[1]), jnp.float32),
+            pltpu.SemaphoreType.DMA((count,)),
+            pltpu.SemaphoreType.DMA((count,)),
+            pltpu.SemaphoreType.DMA((2,)),
+        ],
+        compiler_params=pltpu.CompilerParams(collective_id=1, has_side_effects=True),
+    )(sent, d_out, conv_wide, values, keys, grad_out, taps, weight_in)
 
 
 def when(active, action, *operands):
@@ -193,21 +307,11 @@
         sent = seq_exchange(d_conv.reshape(height, seq_count, chans).transpose(1, 2, 0))
         d_conv_local = sent.transpose(0, 2, 1).reshape(length, chans)
         d_prod_local = adjoint(d_conv_local)
-        back = seq_exchange(d_prod_local.reshape(seq_count, height, chans).transpose(0, 2, 1))
-        d_prod = back.transpose(2, 0, 1).reshape(height, width)
-        d_prod_wide = d_prod.astype(jnp.float32)
-        d_mixed = jnp.concatenate(
-            [d_out * conv_wide, d_prod_wide * values, d_prod_wide * keys], axis=1
-        ).astype(jnp.bfloat16)
-        rim_below = shifted(d_mixed[:2], "seq", -1)
-        padded = jnp.concatenate([d_mixed, rim_below], axis=0).astype(jnp.float32)
-        d_proj = (taps[0] * padded[:-2] + taps[1] * padded[1:-1] + taps[2] * padded[2:]).astype(
-            jnp.bfloat16
+        sent_back = d_prod_local.reshape(seq_count, height, chans).transpose(0, 2, 1)
+        sent_back = sent_back.reshape(seq_count * chans, height).astype(jnp.float32)
+        return exchange_and_finish(
+            sent_back, d_out, conv_wide, values, keys, grad_out, taps, weight_in
         )
-        total = grad_out.astype(jnp.float32) + lax.dot_general(
-            d_proj, weight_in, contract, preferred_element_type=jnp.float32
-        )
-        return total.astype(jnp.bfloat16)
 
     def tick(step, carry):
         incoming, grads = carry

time: 534 us -> 513 us (0.961)
  Pallas kernels: 181 us -> 234 us
  matrix products: 132 us -> 97.5 us
  waiting for transfers between devices: 91.7 us -> 59.9 us
  other arithmetic: 23.1 us -> 44 us
  starting transfers between devices: 45.4 us -> 27.1 us
  local copies, waits for them, and re-layouts: 52 us -> 41.7 us
    pallas_call x0 -> x8, Pallas kernels: none -> 150 us  [exchange_and_finish(): pl.pallas_call(finish_kernel, out_shape=jax.ShapeDtypeStruct(grad_out.sha...]
    pallas_call x16 -> x8, Pallas kernels: 181 us -> 84.4 us  [seq_exchange(): pl.pallas_call(exchange_kernel, out_shape=jax.ShapeDtypeStruct(blocks.sha...]
    ppermute x17 -> x9, waiting for transfers between devices: 74.7 us -> 43.8 us  [shifted(): return lax.ppermute(value, axis, pairs)]
    dot_general x8 -> x0, matrix products: 26.7 us -> none  [stage(): lax.dot_general(d_proj, weight_in, contract, preferred_element_type=jnp.f...]
    ppermute x17 -> x9, starting transfers between devices: 34.3 us -> 15.9 us  [shifted(): return lax.ppermute(value, axis, pairs)]
    select_n x0 -> x8, other arithmetic: none -> 13.7 us  [tick(): jnp.where(active, lax.dynamic_update_index_in_dim(grads, d_input, slot, 0...]
    while x224 -> x192, local copies, waits for them, and re-layouts: 13.4 us -> 4.41 us
    select_n x8, other arithmetic: 0.18 us -> 7.68 us  [tick(): jnp.where(section_place == section_count - 1, top, shifted(d_input, 'sect...]
  transfers between devices with their start and end apart: 19 -> 11, of which waited for: 18 -> 10; matrix products, arithmetic and copies ran while one was open for 1% -> 4% of each run, Pallas kernels for 0% -> 0%
where the time goes in v3:
time: 513 us; the launch traced here: 508 us
  Pallas kernels  234 us (46%)
  matrix products  97.5 us (19%)
  waiting for transfers between devices  59.9 us (12%)
  other arithmetic  44 us (9%)
  local copies, waits for them, and re-layouts  41.7 us (8%)
  starting transfers between devices  27.1 us (5%)
    pallas_call x8, Pallas kernels, exchange_and_finish(): pl.pallas_call(finish_kernel, out_shape=jax.ShapeDtypeStruct(grad_out.sha...  150 us
    pallas_call x8, Pallas kernels, seq_exchange(): pl.pallas_call(exchange_kernel, out_shape=jax.ShapeDtypeStruct(blocks.sha...  84.4 us
    ppermute x9, waiting for transfers between devices, shifted(): return lax.ppermute(value, axis, pairs)  43.8 us
    ppermute x9, starting transfers between devices, shifted(): return lax.ppermute(value, axis, pairs)  15.9 us
    select_n x8, other arithmetic, tick(): jnp.where(active, lax.dynamic_update_index_in_dim(grads, d_input, slot, 0...  13.7 us
    dot_general x8, matrix products, stage(): lax.dot_general(grad_out, weight_out, contract, preferred_element_type=jn...  10.5 us
  transfers between devices with their start and end apart: 11, of which 10 were waited for; matrix products, arithmetic and copies ran while one was open for 4% of the time, Pallas kernels for 0%

profile of v3, /device:TPU:1, one launch (start us, length us, event | category | flops | bytes accessed | tf_op | source)
XLA Modules:
  0.0 507.7 jit_solution(13128886136842878679)
XLA Ops:
  0.8 4.5 collective-permute-start.1
  6.1 1.0 convert_element_type.232
  7.2 1.2 maximum_convert_fusion
  8.7 1.0 fusion.296
  9.8 1.1 copy.138
  10.9 7.2 %all-to-all-start = ((bf16[2,128,768]{1,0,2:T(2,128)(2,1)}), bf16[2,128,768]{1,0,2:T(2,128)(2,1)S(1)}, u32[]{:S(2)}, u32[]{:S(2)}) async-start(bf16[2,128,768]{1,0,2:T(2,128)(2,1)} %copy.138), calls=%async_computation | async-start | bytes 786432 | tf_op jit(solution)/shard_map/all_to_all | solution.py:295
  19.0 9.3 %all-to-all-done = bf16[2,128,768]{1,0,2:T(2,128)(2,1)S(1)} async-done(((bf16[2,128,768]{1,0,2:T(2,128)(2,1)}), bf16[2,128,768]{1,0,2:T(2,128)(2,1)S(1)}, u32[]{:S(2)}, u32[]{:S(2)}) %all-to-all-start) | async-done | bytes 393248 | tf_op jit(solution)/shard_map/all_to_all | solution.py:295
  33.0 2.0 add_bitcast_fusion.1
  44.5 1.7 fusion.131
  46.3 1.5 copy.162
  47.7 1.1 div.18
  48.9 2.0 fusion.154
  50.9 4.0 all-to-all-start.1
  56.4 6.8 %all-to-all-done.1 = bf16[32,128,24]{1,2,0:T(8,128)(2,1)S(1)} async-done(((bf16[32,128,24]{1,2,0:T(8,128)(2,1)}), bf16[32,128,24]{1,2,0:T(8,128)(2,1)S(1)}, u32[]{:S(2)}, u32[]{:S(2)}) %all-to-all-start.1) | async-done | bytes 196640 | tf_op jit(solution)/shard_map/all_to_all | solution.py:300
  64.0 2.0 copy.164
  66.0 441.6 %while.19 = (s32[]{:T(128)}, bf16[128,768]{1,0:T(8,128)(2,1)S(1)}, bf16[1,128,768]{2,1,0:T(8,128)(2,1)}, pred[]{:T(512)}, bf16[1,128,768]{2,1,0:T(8,128)(2,1)}, ...) while((s32[]{:T(128)}, bf16[128,768]{1,0:T(8,128)(2,1)S(1)}, ...), condition=%wide.region_1.2_spmd.clone, body=%wide.region_0.1_spmd.clone.sunk | while | flops 1064730624 | bytes 54702764 | solution.py:335
  66.9 1.3 multiply_convert_fusion.3
  69.1 10.4 %eval_jaxpr.18 = bf16[32,24,128]{2,1,0:T(8,128)(2,1)} custom-call(bf16[32,24,128]{2,1,0:T(8,128)(2,1)} %bitcast.256), custom_call_target="tpu_custom_call" | custom-call | tf_op jit(solution)/shard_map/while/body/eval_jaxpr/pallas_call | solution.py:122
  92.6 18.0 %eval_jaxpr.19 = bf16[128,768]{1,0:T(8,128)(2,1)} custom-call(f32[768,128]{1,0:T(8,128)} %bitcast.253, f32[128,768]{1,0:T(8,128)} %get-tuple-element.672.d_out_ref, f32[128,768]{1,0:T(8,128)} %get-tuple-element.719.conv_ref, f32[128,768]{1,0:T(8,128)S(1)} %copy-done.8, f32[128,768]{1,0:T(8,128)S(1)} %copy-done.7, bf16[128,768]{1,0:T(8,128)(2,1)} %copy-done.6, ...), custom_call_target="tpu_custom_call" | custom-call | tf_op jit(solution)/shard_map/while/body/eval_jaxpr/pallas_call | solution.py:233
  110.6 1.4 collective-permute-start
  112.1 1.6 bitcast_select_fusion.5
  113.7 4.7 collective-permute-done
  120.4 1.3 multiply_convert_fusion.3
  122.5 10.4 %eval_jaxpr.18 = bf16[32,24,128]{2,1,0:T(8,128)(2,1)} custom-call(bf16[32,24,128]{2,1,0:T(8,128)(2,1)} %bitcast.256), custom_call_target="tpu_custom_call" | custom-call | tf_op jit(solution)/shard_map/while/body/eval_jaxpr/pallas_call | solution.py:122
  146.1 18.8 %eval_jaxpr.19 = bf16[128,768]{1,0:T(8,128)(2,1)} custom-call(f32[768,128]{1,0:T(8,128)} %bitcast.253, f32[128,768]{1,0:T(8,128)} %get-tuple-element.672.d_out_ref, f32[128,768]{1,0:T(8,128)} %get-tuple-element.719.conv_ref, f32[128,768]{1,0:T(8,128)S(1)} %copy-done.8, f32[128,768]{1,0:T(8,128)S(1)} %copy-done.7, bf16[128,768]{1,0:T(8,128)(2,1)} %copy-done.6, ...), custom_call_target="tpu_custom_call" | custom-call | tf_op jit(solution)/shard_map/while/body/eval_jaxpr/pallas_call | solution.py:233
  164.9 1.4 collective-permute-start
  166.4 1.7 bitcast_select_fusion.5
  168.1 4.8 collective-permute-done
  174.9 1.3 multiply_convert_fusion.3
  177.1 10.4 %eval_jaxpr.18 = bf16[32,24,128]{2,1,0:T(8,128)(2,1)} custom-call(bf16[32,24,128]{2,1,0:T(8,128)(2,1)} %bitcast.256), custom_call_target="tpu_custom_call" | custom-call | tf_op jit(solution)/shard_map/while/body/eval_jaxpr/pallas_call | solution.py:122
  200.6 18.8 %eval_jaxpr.19 = bf16[128,768]{1,0:T(8,128)(2,1)} custom-call(f32[768,128]{1,0:T(8,128)} %bitcast.253, f32[128,768]{1,0:T(8,128)} %get-tuple-element.672.d_out_ref, f32[128,768]{1,0:T(8,128)} %get-tuple-element.719.conv_ref, f32[128,768]{1,0:T(8,128)S(1)} %copy-done.8, f32[128,768]{1,0:T(8,128)S(1)} %copy-done.7, bf16[128,768]{1,0:T(8,128)(2,1)} %copy-done.6, ...), custom_call_target="tpu_custom_call" | custom-call | tf_op jit(solution)/shard_map/while/body/eval_jaxpr/pallas_call | solution.py:233
  219.5 1.4 collective-permute-start
  220.9 1.7 bitcast_select_fusion.5
  222.6 4.8 collective-permute-done
  229.4 1.3 multiply_convert_fusion.3
  231.6 10.6 %eval_jaxpr.18 = bf16[32,24,128]{2,1,0:T(8,128)(2,1)} custom-call(bf16[32,24,128]{2,1,0:T(8,128)(2,1)} %bitcast.256), custom_call_target="tpu_custom_call" | custom-call | tf_op jit(solution)/shard_map/while/body/eval_jaxpr/pallas_call | solution.py:122
  255.3 18.8 %eval_jaxpr.19 = bf16[128,768]{1,0:T(8,128)(2,1)} custom-call(f32[768,128]{1,0:T(8,128)} %bitcast.253, f32[128,768]{1,0:T(8,128)} %get-tuple-element.672.d_out_ref, f32[128,768]{1,0:T(8,128)} %get-tuple-element.719.conv_ref, f32[128,768]{1,0:T(8,128)S(1)} %copy-done.8, f32[128,768]{1,0:T(8,128)S(1)} %copy-done.7, bf16[128,768]{1,0:T(8,128)(2,1)} %copy-done.6, ...), custom_call_target="tpu_custom_call" | custom-call | tf_op jit(solution)/shard_map/while/body/eval_jaxpr/pallas_call | solution.py:233
  274.1 1.4 collective-permute-start
  275.6 1.7 bitcast_select_fusion.5
  277.3 5.8 %collective-permute-done = bf16[128,768]{1,0:T(8,128)(2,1)S(1)} collective-permute-done((bf16[128,768]{1,0:T(8,128)(2,1)}, bf16[128,768]{1,0:T(8,128)(2,1)S(1)}, u32[]{:S(2)}, u32[]{:S(2)}) %collective-permute-start) | collective-permute-done | bytes 196640 | tf_op jit(solution)/shard_map/while/body/eval_jaxpr/ppermute | solution.py:17
  285.0 1.3 multiply_convert_fusion.3
  287.2 10.6 %eval_jaxpr.18 = bf16[32,24,128]{2,1,0:T(8,128)(2,1)} custom-call(bf16[32,24,128]{2,1,0:T(8,128)(2,1)} %bitcast.256), custom_call_target="tpu_custom_call" | custom-call | tf_op jit(solution)/shard_map/while/body/eval_jaxpr/pallas_call | solution.py:122
  310.9 18.9 %eval_jaxpr.19 = bf16[128,768]{1,0:T(8,128)(2,1)} custom-call(f32[768,128]{1,0:T(8,128)} %bitcast.253, f32[128,768]{1,0:T(8,128)} %get-tuple-element.672.d_out_ref, f32[128,768]{1,0:T(8,128)} %get-tuple-element.719.conv_ref, f32[128,768]{1,0:T(8,128)S(1)} %copy-done.8, f32[128,768]{1,0:T(8,128)S(1)} %copy-done.7, bf16[128,768]{1,0:T(8,128)(2,1)} %copy-done.6, ...), custom_call_target="tpu_custom_call" | custom-call | tf_op jit(solution)/shard_map/while/body/eval_jaxpr/pallas_call | solution.py:233
  329.8 1.4 collective-permute-start
  331.3 1.7 bitcast_select_fusion.5
  333.0 5.9 %collective-permute-done = bf16[128,768]{1,0:T(8,128)(2,1)S(1)} collective-permute-done((bf16[128,768]{1,0:T(8,128)(2,1)}, bf16[128,768]{1,0:T(8,128)(2,1)S(1)}, u32[]{:S(2)}, u32[]{:S(2)}) %collective-permute-start) | collective-permute-done | bytes 196640 | tf_op jit(solution)/shard_map/while/body/eval_jaxpr/ppermute | solution.py:17
  340.9 1.3 multiply_convert_fusion.3
  343.0 10.6 %eval_jaxpr.18 = bf16[32,24,128]{2,1,0:T(8,128)(2,1)} custom-call(bf16[32,24,128]{2,1,0:T(8,128)(2,1)} %bitcast.256), custom_call_target="tpu_custom_call" | custom-call | tf_op jit(solution)/shard_map/while/body/eval_jaxpr/pallas_call | solution.py:122
  366.8 18.9 %eval_jaxpr.19 = bf16[128,768]{1,0:T(8,128)(2,1)} custom-call(f32[768,128]{1,0:T(8,128)} %bitcast.253, f32[128,768]{1,0:T(8,128)} %get-tuple-element.672.d_out_ref, f32[128,768]{1,0:T(8,128)} %get-tuple-element.719.conv_ref, f32[128,768]{1,0:T(8,128)S(1)} %copy-done.8, f32[128,768]{1,0:T(8,128)S(1)} %copy-done.7, bf16[128,768]{1,0:T(8,128)(2,1)} %copy-done.6, ...), custom_call_target="tpu_custom_call" | custom-call | tf_op jit(solution)/shard_map/while/body/eval_jaxpr/pallas_call | solution.py:233
  385.7 1.4 collective-permute-start
  387.2 1.7 bitcast_select_fusion.5
  388.9 5.9 %collective-permute-done = bf16[128,768]{1,0:T(8,128)(2,1)S(1)} collective-permute-done((bf16[128,768]{1,0:T(8,128)(2,1)}, bf16[128,768]{1,0:T(8,128)(2,1)S(1)}, u32[]{:S(2)}, u32[]{:S(2)}) %collective-permute-start) | collective-permute-done | bytes 196640 | tf_op jit(solution)/shard_map/while/body/eval_jaxpr/ppermute | solution.py:17
  396.8 1.3 multiply_convert_fusion.3
  398.9 10.6 %eval_jaxpr.18 = bf16[32,24,128]{2,1,0:T(8,128)(2,1)} custom-call(bf16[32,24,128]{2,1,0:T(8,128)(2,1)} %bitcast.256), custom_call_target="tpu_custom_call" | custom-call | tf_op jit(solution)/shard_map/while/body/eval_jaxpr/pallas_call | solution.py:122
  422.7 18.9 %eval_jaxpr.19 = bf16[128,768]{1,0:T(8,128)(2,1)} custom-call(f32[768,128]{1,0:T(8,128)} %bitcast.253, f32[128,768]{1,0:T(8,128)} %get-tuple-element.672.d_out_ref, f32[128,768]{1,0:T(8,128)} %get-tuple-element.719.conv_ref, f32[128,768]{1,0:T(8,128)S(1)} %copy-done.8, f32[128,768]{1,0:T(8,128)S(1)} %copy-done.7, bf16[128,768]{1,0:T(8,128)(2,1)} %copy-done.6, ...), custom_call_target="tpu_custom_call" | custom-call | tf_op jit(solution)/shard_map/while/body/eval_jaxpr/pallas_call | solution.py:233
  441.6 1.4 collective-permute-start
  443.0 1.7 bitcast_select_fusion.5
  444.8 5.9 %collective-permute-done = bf16[128,768]{1,0:T(8,128)(2,1)S(1)} collective-permute-done((bf16[128,768]{1,0:T(8,128)(2,1)}, bf16[128,768]{1,0:T(8,128)(2,1)S(1)}, u32[]{:S(2)}, u32[]{:S(2)}) %collective-permute-start) | collective-permute-done | bytes 196640 | tf_op jit(solution)/shard_map/while/body/eval_jaxpr/ppermute | solution.py:17
  452.6 1.3 multiply_convert_fusion.3
  454.8 10.6 %eval_jaxpr.18 = bf16[32,24,128]{2,1,0:T(8,128)(2,1)} custom-call(bf16[32,24,128]{2,1,0:T(8,128)(2,1)} %bitcast.256), custom_call_target="tpu_custom_call" | custom-call | tf_op jit(solution)/shard_map/while/body/eval_jaxpr/pallas_call | solution.py:122
  478.5 18.9 %eval_jaxpr.19 = bf16[128,768]{1,0:T(8,128)(2,1)} custom-call(f32[768,128]{1,0:T(8,128)} %bitcast.253, f32[128,768]{1,0:T(8,128)} %get-tuple-element.672.d_out_ref, f32[128,768]{1,0:T(8,128)} %get-tuple-element.719.conv_ref, f32[128,768]{1,0:T(8,128)S(1)} %copy-done.8, f32[128,768]{1,0:T(8,128)S(1)} %copy-done.7, bf16[128,768]{1,0:T(8,128)(2,1)} %copy-done.6, ...), custom_call_target="tpu_custom_call" | custom-call | tf_op jit(solution)/shard_map/while/body/eval_jaxpr/pallas_call | solution.py:233
  497.5 1.4 collective-permute-start
  498.9 1.7 bitcast_select_fusion.5
  500.6 5.9 %collective-permute-done = bf16[128,768]{1,0:T(8,128)(2,1)S(1)} collective-permute-done((bf16[128,768]{1,0:T(8,128)(2,1)}, bf16[128,768]{1,0:T(8,128)(2,1)S(1)}, u32[]{:S(2)}, u32[]{:S(2)}) %collective-permute-start) | collective-permute-done | bytes 196640 | tf_op jit(solution)/shard_map/while/body/eval_jaxpr/ppermute | solution.py:17
  (409 shorter events, 144.5 us)
Async XLA Ops:
  0.0 18.1 %copy-start = (f32[1,768]{1,0:T(1,128)S(1)}, f32[1,768]{1,0:T(1,128)}, u32[]{:S(2)}) copy-start(f32[1,768]{1,0:T(1,128)} %param.15) | copy-start | bytes 9220
  0.8 6.4 %collective-permute-start.1 = (bf16[2,2304]{1,0:T(2,128)(2,1)S(1)}, bf16[2,2304]{1,0:T(2,128)(2,1)S(1)}, u32[]{:S(2)}, u32[]{:S(2)}) collective-permute-start(bf16[2,2304]{1,0:T(2,128)(2,1)S(1)} %slice_bitcast_fusion), channel_id=1, source_target_pairs={{0,8},{8,16},{16,24},{24,32},{32,40},{40,48},{48,56},{56,64},{64,7... | collective-permute-start | bytes 27656 | tf_op jit(solution)/shard_map/ppermute | solution.py:17
  10.9 17.4 %all-to-all-start = ((bf16[2,128,768]{1,0,2:T(2,128)(2,1)}), bf16[2,128,768]{1,0,2:T(2,128)(2,1)S(1)}, u32[]{:S(2)}, u32[]{:S(2)}) async-start(bf16[2,128,768]{1,0,2:T(2,128)(2,1)} %copy.138), calls=%async_computation | async-start | bytes 786432 | tf_op jit(solution)/shard_map/all_to_all | solution.py:295
  48.9 6.0 %copy-start.18 = (f32[1,3,2304]{2,0,1:T(1,128)S(1)}, f32[1,3,2304]{2,0,1:T(1,128)}, u32[]{:S(2)}) copy-start(f32[1,3,2304]{2,0,1:T(1,128)} %param.13) | copy-start | bytes 82948
  50.9 15.1 %copy-start.4 = (bf16[1,768,768]{2,1,0:T(8,128)(2,1)S(1)}, bf16[1,768,768]{2,1,0:T(8,128)(2,1)}, u32[]{:S(2)}) copy-start(bf16[1,768,768]{2,1,0:T(8,128)(2,1)} %param.12) | copy-start | bytes 3538948
  50.9 12.4 %all-to-all-start.1 = ((bf16[32,128,24]{1,2,0:T(8,128)(2,1)}), bf16[32,128,24]{1,2,0:T(8,128)(2,1)S(1)}, u32[]{:S(2)}, u32[]{:S(2)}) async-start(bf16[32,128,24]{1,2,0:T(8,128)(2,1)} %fusion.154), calls=%async_computation.1 | async-start | bytes 393216 | tf_op jit(solution)/shard_map/all_to_all | solution.py:300
  66.0 2.3 copy-start.9
  66.0 17.0 %copy-start.6 = (bf16[128,768]{1,0:T(8,128)(2,1)}, bf16[128,768]{1,0:T(8,128)(2,1)S(1)}, u32[]{:S(2)}) copy-start(bf16[128,768]{1,0:T(8,128)(2,1)S(1)} %get-tuple-element.692.grad_ref) | copy-start | bytes 589828 | tf_op jit(solution)/shard_map/while
  66.0 19.1 %copy-start.2 = (f32[24,32,256]{2,1,0:T(8,128)}, f32[24,32,256]{2,1,0:T(8,128)S(1)}, u32[]{:S(2)}) copy-start(f32[24,32,256]{2,1,0:T(8,128)S(1)} %get-tuple-element.716) | copy-start | bytes 2359300 | tf_op jit(solution)/shard_map/while
  92.6 26.8 %copy-start.5 = (bf16[1,768,768]{2,1,0:T(8,128)(2,1)S(1)}, bf16[1,768,768]{2,1,0:T(8,128)(2,1)}, u32[]{:S(2)}) copy-start(bf16[1,768,768]{2,1,0:T(8,128)(2,1)} %get-tuple-element.745) | copy-start | bytes 3538948 | tf_op jit(solution)/shard_map/while
  110.6 8.8 %copy-start.3 = (f32[24,32,256]{2,1,0:T(8,128)S(1)}, f32[24,32,256]{2,1,0:T(8,128)}, u32[]{:S(2)}) copy-start(f32[24,32,256]{2,1,0:T(8,128)} %copy-done.2) | copy-start | bytes 2359300 | tf_op jit(solution)/shard_map/while
  110.6 8.8 %copy-start.10 = (f32[128,768]{1,0:T(8,128)S(1)}, f32[128,768]{1,0:T(8,128)}, u32[]{:S(2)}) copy-start(f32[128,768]{1,0:T(8,128)} %copy-done.9) | copy-start | bytes 1179652 | tf_op jit(solution)/shard_map/while
  110.6 7.8 %collective-permute-start = (bf16[128,768]{1,0:T(8,128)(2,1)}, bf16[128,768]{1,0:T(8,128)(2,1)S(1)}, u32[]{:S(2)}, u32[]{:S(2)}) collective-permute-start(bf16[128,768]{1,0:T(8,128)(2,1)} %eval_jaxpr.19), channel_id=1, source_target_pairs={{1,0},{2,1},{3,2},{4,3},{5,4},{6,5},{7,6},{9,8},{10,9},{11,10},{12... | collective-permute-start | bytes 589832 | tf_op jit(solution)/shard_map/while/body/eval_jaxpr/ppermute | solution.py:17
  119.4 2.3 copy-start.9
  119.4 16.9 %copy-start.6 = (bf16[128,768]{1,0:T(8,128)(2,1)}, bf16[128,768]{1,0:T(8,128)(2,1)S(1)}, u32[]{:S(2)}) copy-start(bf16[128,768]{1,0:T(8,128)(2,1)S(1)} %get-tuple-element.692.grad_ref) | copy-start | bytes 589828 | tf_op jit(solution)/shard_map/while
  119.5 19.1 %copy-start.2 = (f32[24,32,256]{2,1,0:T(8,128)}, f32[24,32,256]{2,1,0:T(8,128)S(1)}, u32[]{:S(2)}) copy-start(f32[24,32,256]{2,1,0:T(8,128)S(1)} %get-tuple-element.716) | copy-start | bytes 2359300 | tf_op jit(solution)/shard_map/while
  146.1 27.8 %copy-start.5 = (bf16[1,768,768]{2,1,0:T(8,128)(2,1)S(1)}, bf16[1,768,768]{2,1,0:T(8,128)(2,1)}, u32[]{:S(2)}) copy-start(bf16[1,768,768]{2,1,0:T(8,128)(2,1)} %get-tuple-element.745) | copy-start | bytes 3538948 | tf_op jit(solution)/shard_map/while
  164.9 9.0 %copy-start.3 = (f32[24,32,256]{2,1,0:T(8,128)S(1)}, f32[24,32,256]{2,1,0:T(8,128)}, u32[]{:S(2)}) copy-start(f32[24,32,256]{2,1,0:T(8,128)} %copy-done.2) | copy-start | bytes 2359300 | tf_op jit(solution)/shard_map/while
  164.9 9.0 %copy-start.10 = (f32[128,768]{1,0:T(8,128)S(1)}, f32[128,768]{1,0:T(8,128)}, u32[]{:S(2)}) copy-start(f32[128,768]{1,0:T(8,128)} %copy-done.9) | copy-start | bytes 1179652 | tf_op jit(solution)/shard_map/while
  164.9 8.0 %collective-permute-start = (bf16[128,768]{1,0:T(8,128)(2,1)}, bf16[128,768]{1,0:T(8,128)(2,1)S(1)}, u32[]{:S(2)}, u32[]{:S(2)}) collective-permute-start(bf16[128,768]{1,0:T(8,128)(2,1)} %eval_jaxpr.19), channel_id=1, source_target_pairs={{1,0},{2,1},{3,2},{4,3},{5,4},{6,5},{7,6},{9,8},{10,9},{11,10},{12... | collective-permute-start | bytes 589832 | tf_op jit(solution)/shard_map/while/body/eval_jaxpr/ppermute | solution.py:17
  173.9 2.3 copy-start.9
  174.0 17.0 %copy-start.6 = (bf16[128,768]{1,0:T(8,128)(2,1)}, bf16[128,768]{1,0:T(8,128)(2,1)S(1)}, u32[]{:S(2)}) copy-start(bf16[128,768]{1,0:T(8,128)(2,1)S(1)} %get-tuple-element.692.grad_ref) | copy-start | bytes 589828 | tf_op jit(solution)/shard_map/while
  174.0 19.1 %copy-start.2 = (f32[24,32,256]{2,1,0:T(8,128)}, f32[24,32,256]{2,1,0:T(8,128)S(1)}, u32[]{:S(2)}) copy-start(f32[24,32,256]{2,1,0:T(8,128)S(1)} %get-tuple-element.716) | copy-start | bytes 2359300 | tf_op jit(solution)/shard_map/while
  200.6 27.8 %copy-start.5 = (bf16[1,768,768]{2,1,0:T(8,128)(2,1)S(1)}, bf16[1,768,768]{2,1,0:T(8,128)(2,1)}, u32[]{:S(2)}) copy-start(bf16[1,768,768]{2,1,0:T(8,128)(2,1)} %get-tuple-element.745) | copy-start | bytes 3538948 | tf_op jit(solution)/shard_map/while
  219.4 9.0 %copy-start.3 = (f32[24,32,256]{2,1,0:T(8,128)S(1)}, f32[24,32,256]{2,1,0:T(8,128)}, u32[]{:S(2)}) copy-start(f32[24,32,256]{2,1,0:T(8,128)} %copy-done.2) | copy-start | bytes 2359300 | tf_op jit(solution)/shard_map/while
  219.4 9.0 %copy-start.10 = (f32[128,768]{1,0:T(8,128)S(1)}, f32[128,768]{1,0:T(8,128)}, u32[]{:S(2)}) copy-start(f32[128,768]{1,0:T(8,128)} %copy-done.9) | copy-start | bytes 1179652 | tf_op jit(solution)/shard_map/while
  219.5 8.0 %collective-permute-start = (bf16[128,768]{1,0:T(8,128)(2,1)}, bf16[128,768]{1,0:T(8,128)(2,1)S(1)}, u32[]{:S(2)}, u32[]{:S(2)}) collective-permute-start(bf16[128,768]{1,0:T(8,128)(2,1)} %eval_jaxpr.19), channel_id=1, source_target_pairs={{1,0},{2,1},{3,2},{4,3},{5,4},{6,5},{7,6},{9,8},{10,9},{11,10},{12... | collective-permute-start | bytes 589832 | tf_op jit(solution)/shard_map/while/body/eval_jaxpr/ppermute | solution.py:17
  228.4 2.3 copy-start.9
  228.5 17.2 %copy-start.6 = (bf16[128,768]{1,0:T(8,128)(2,1)}, bf16[128,768]{1,0:T(8,128)(2,1)S(1)}, u32[]{:S(2)}) copy-start(bf16[128,768]{1,0:T(8,128)(2,1)S(1)} %get-tuple-element.692.grad_ref) | copy-start | bytes 589828 | tf_op jit(solution)/shard_map/while
  228.5 19.3 %copy-start.2 = (f32[24,32,256]{2,1,0:T(8,128)}, f32[24,32,256]{2,1,0:T(8,128)S(1)}, u32[]{:S(2)}) copy-start(f32[24,32,256]{2,1,0:T(8,128)S(1)} %get-tuple-element.716) | copy-start | bytes 2359300 | tf_op jit(solution)/shard_map/while
  255.3 28.7 %copy-start.5 = (bf16[1,768,768]{2,1,0:T(8,128)(2,1)S(1)}, bf16[1,768,768]{2,1,0:T(8,128)(2,1)}, u32[]{:S(2)}) copy-start(bf16[1,768,768]{2,1,0:T(8,128)(2,1)} %get-tuple-element.745) | copy-start | bytes 3538948 | tf_op jit(solution)/shard_map/while
  274.1 9.9 %copy-start.3 = (f32[24,32,256]{2,1,0:T(8,128)S(1)}, f32[24,32,256]{2,1,0:T(8,128)}, u32[]{:S(2)}) copy-start(f32[24,32,256]{2,1,0:T(8,128)} %copy-done.2) | copy-start | bytes 2359300 | tf_op jit(solution)/shard_map/while
  274.1 9.9 %copy-start.10 = (f32[128,768]{1,0:T(8,128)S(1)}, f32[128,768]{1,0:T(8,128)}, u32[]{:S(2)}) copy-start(f32[128,768]{1,0:T(8,128)} %copy-done.9) | copy-start | bytes 1179652 | tf_op jit(solution)/shard_map/while
  274.1 8.9 %collective-permute-start = (bf16[128,768]{1,0:T(8,128)(2,1)}, bf16[128,768]{1,0:T(8,128)(2,1)S(1)}, u32[]{:S(2)}, u32[]{:S(2)}) collective-permute-start(bf16[128,768]{1,0:T(8,128)(2,1)} %eval_jaxpr.19), channel_id=1, source_target_pairs={{1,0},{2,1},{3,2},{4,3},{5,4},{6,5},{7,6},{9,8},{10,9},{11,10},{12... | collective-permute-start | bytes 589832 | tf_op jit(solution)/shard_map/while/body/eval_jaxpr/ppermute | solution.py:17
  284.0 2.3 copy-start.9
  284.1 17.1 %copy-start.6 = (bf16[128,768]{1,0:T(8,128)(2,1)}, bf16[128,768]{1,0:T(8,128)(2,1)S(1)}, u32[]{:S(2)}) copy-start(bf16[128,768]{1,0:T(8,128)(2,1)S(1)} %get-tuple-element.692.grad_ref) | copy-start | bytes 589828 | tf_op jit(solution)/shard_map/while
  284.1 19.3 %copy-start.2 = (f32[24,32,256]{2,1,0:T(8,128)}, f32[24,32,256]{2,1,0:T(8,128)S(1)}, u32[]{:S(2)}) copy-start(f32[24,32,256]{2,1,0:T(8,128)S(1)} %get-tuple-element.716) | copy-start | bytes 2359300 | tf_op jit(solution)/shard_map/while
  309.0 1.9 copy-start.7
  310.9 29.0 %copy-start.5 = (bf16[1,768,768]{2,1,0:T(8,128)(2,1)S(1)}, bf16[1,768,768]{2,1,0:T(8,128)(2,1)}, u32[]{:S(2)}) copy-start(bf16[1,768,768]{2,1,0:T(8,128)(2,1)} %get-tuple-element.745) | copy-start | bytes 3538948 | tf_op jit(solution)/shard_map/while
  329.8 10.1 %copy-start.3 = (f32[24,32,256]{2,1,0:T(8,128)S(1)}, f32[24,32,256]{2,1,0:T(8,128)}, u32[]{:S(2)}) copy-start(f32[24,32,256]{2,1,0:T(8,128)} %copy-done.2) | copy-start | bytes 2359300 | tf_op jit(solution)/shard_map/while
  329.8 10.1 %copy-start.10 = (f32[128,768]{1,0:T(8,128)S(1)}, f32[128,768]{1,0:T(8,128)}, u32[]{:S(2)}) copy-start(f32[128,768]{1,0:T(8,128)} %copy-done.9) | copy-start | bytes 1179652 | tf_op jit(solution)/shard_map/while
  329.8 9.1 %collective-permute-start = (bf16[128,768]{1,0:T(8,128)(2,1)}, bf16[128,768]{1,0:T(8,128)(2,1)S(1)}, u32[]{:S(2)}, u32[]{:S(2)}) collective-permute-start(bf16[128,768]{1,0:T(8,128)(2,1)} %eval_jaxpr.19), channel_id=1, source_target_pairs={{1,0},{2,1},{3,2},{4,3},{5,4},{6,5},{7,6},{9,8},{10,9},{11,10},{12... | collective-permute-start | bytes 589832 | tf_op jit(solution)/shard_map/while/body/eval_jaxpr/ppermute | solution.py:17
  339.9 2.3 copy-start.9
  339.9 17.1 %copy-start.6 = (bf16[128,768]{1,0:T(8,128)(2,1)}, bf16[128,768]{1,0:T(8,128)(2,1)S(1)}, u32[]{:S(2)}) copy-start(bf16[128,768]{1,0:T(8,128)(2,1)S(1)} %get-tuple-element.692.grad_ref) | copy-start | bytes 589828 | tf_op jit(solution)/shard_map/while
  339.9 19.3 %copy-start.2 = (f32[24,32,256]{2,1,0:T(8,128)}, f32[24,32,256]{2,1,0:T(8,128)S(1)}, u32[]{:S(2)}) copy-start(f32[24,32,256]{2,1,0:T(8,128)S(1)} %get-tuple-element.716) | copy-start | bytes 2359300 | tf_op jit(solution)/shard_map/while
  364.8 1.9 copy-start.7
  366.7 29.0 %copy-start.5 = (bf16[1,768,768]{2,1,0:T(8,128)(2,1)S(1)}, bf16[1,768,768]{2,1,0:T(8,128)(2,1)}, u32[]{:S(2)}) copy-start(bf16[1,768,768]{2,1,0:T(8,128)(2,1)} %get-tuple-element.745) | copy-start | bytes 3538948 | tf_op jit(solution)/shard_map/while
  385.7 10.1 %copy-start.3 = (f32[24,32,256]{2,1,0:T(8,128)S(1)}, f32[24,32,256]{2,1,0:T(8,128)}, u32[]{:S(2)}) copy-start(f32[24,32,256]{2,1,0:T(8,128)} %copy-done.2) | copy-start | bytes 2359300 | tf_op jit(solution)/shard_map/while
  385.7 10.1 %copy-start.10 = (f32[128,768]{1,0:T(8,128)S(1)}, f32[128,768]{1,0:T(8,128)}, u32[]{:S(2)}) copy-start(f32[128,768]{1,0:T(8,128)} %copy-done.9) | copy-start | bytes 1179652 | tf_op jit(solution)/shard_map/while
  385.7 9.1 %collective-permute-start = (bf16[128,768]{1,0:T(8,128)(2,1)}, bf16[128,768]{1,0:T(8,128)(2,1)S(1)}, u32[]{:S(2)}, u32[]{:S(2)}) collective-permute-start(bf16[128,768]{1,0:T(8,128)(2,1)} %eval_jaxpr.19), channel_id=1, source_target_pairs={{1,0},{2,1},{3,2},{4,3},{5,4},{6,5},{7,6},{9,8},{10,9},{11,10},{12... | collective-permute-start | bytes 589832 | tf_op jit(solution)/shard_map/while/body/eval_jaxpr/ppermute | solution.py:17
  395.8 2.3 copy-start.9
  395.8 17.1 %copy-start.6 = (bf16[128,768]{1,0:T(8,128)(2,1)}, bf16[128,768]{1,0:T(8,128)(2,1)S(1)}, u32[]{:S(2)}) copy-start(bf16[128,768]{1,0:T(8,128)(2,1)S(1)} %get-tuple-element.692.grad_ref) | copy-start | bytes 589828 | tf_op jit(solution)/shard_map/while
  395.8 19.3 %copy-start.2 = (f32[24,32,256]{2,1,0:T(8,128)}, f32[24,32,256]{2,1,0:T(8,128)S(1)}, u32[]{:S(2)}) copy-start(f32[24,32,256]{2,1,0:T(8,128)S(1)} %get-tuple-element.716) | copy-start | bytes 2359300 | tf_op jit(solution)/shard_map/while
  422.7 29.0 %copy-start.5 = (bf16[1,768,768]{2,1,0:T(8,128)(2,1)S(1)}, bf16[1,768,768]{2,1,0:T(8,128)(2,1)}, u32[]{:S(2)}) copy-start(bf16[1,768,768]{2,1,0:T(8,128)(2,1)} %get-tuple-element.745) | copy-start | bytes 3538948 | tf_op jit(solution)/shard_map/while
  441.6 10.1 %copy-start.3 = (f32[24,32,256]{2,1,0:T(8,128)S(1)}, f32[24,32,256]{2,1,0:T(8,128)}, u32[]{:S(2)}) copy-start(f32[24,32,256]{2,1,0:T(8,128)} %copy-done.2) | copy-start | bytes 2359300 | tf_op jit(solution)/shard_map/while
  441.6 10.1 %copy-start.10 = (f32[128,768]{1,0:T(8,128)S(1)}, f32[128,768]{1,0:T(8,128)}, u32[]{:S(2)}) copy-start(f32[128,768]{1,0:T(8,128)} %copy-done.9) | copy-start | bytes 1179652 | tf_op jit(solution)/shard_map/while
  441.6 9.1 %collective-permute-start = (bf16[128,768]{1,0:T(8,128)(2,1)}, bf16[128,768]{1,0:T(8,128)(2,1)S(1)}, u32[]{:S(2)}, u32[]{:S(2)}) collective-permute-start(bf16[128,768]{1,0:T(8,128)(2,1)} %eval_jaxpr.19), channel_id=1, source_target_pairs={{1,0},{2,1},{3,2},{4,3},{5,4},{6,5},{7,6},{9,8},{10,9},{11,10},{12... | collective-permute-start | bytes 589832 | tf_op jit(solution)/shard_map/while/body/eval_jaxpr/ppermute | solution.py:17
  451.7 2.3 copy-start.9
  451.7 17.1 %copy-start.6 = (bf16[128,768]{1,0:T(8,128)(2,1)}, bf16[128,768]{1,0:T(8,128)(2,1)S(1)}, u32[]{:S(2)}) copy-start(bf16[128,768]{1,0:T(8,128)(2,1)S(1)} %get-tuple-element.692.grad_ref) | copy-start | bytes 589828 | tf_op jit(solution)/shard_map/while
  451.7 19.3 %copy-start.2 = (f32[24,32,256]{2,1,0:T(8,128)}, f32[24,32,256]{2,1,0:T(8,128)S(1)}, u32[]{:S(2)}) copy-start(f32[24,32,256]{2,1,0:T(8,128)S(1)} %get-tuple-element.716) | copy-start | bytes 2359300 | tf_op jit(solution)/shard_map/while
  478.5 29.0 %copy-start.5 = (bf16[1,768,768]{2,1,0:T(8,128)(2,1)S(1)}, bf16[1,768,768]{2,1,0:T(8,128)(2,1)}, u32[]{:S(2)}) copy-start(bf16[1,768,768]{2,1,0:T(8,128)(2,1)} %get-tuple-element.745) | copy-start | bytes 3538948 | tf_op jit(solution)/shard_map/while
  497.5 10.1 %copy-start.3 = (f32[24,32,256]{2,1,0:T(8,128)S(1)}, f32[24,32,256]{2,1,0:T(8,128)}, u32[]{:S(2)}) copy-start(f32[24,32,256]{2,1,0:T(8,128)} %copy-done.2) | copy-start | bytes 2359300 | tf_op jit(solution)/shard_map/while
  497.5 10.1 %copy-start.10 = (f32[128,768]{1,0:T(8,128)S(1)}, f32[128,768]{1,0:T(8,128)}, u32[]{:S(2)}) copy-start(f32[128,768]{1,0:T(8,128)} %copy-done.9) | copy-start | bytes 1179652 | tf_op jit(solution)/shard_map/while
  497.5 9.1 %collective-permute-start = (bf16[128,768]{1,0:T(8,128)(2,1)}, bf16[128,768]{1,0:T(8,128)(2,1)S(1)}, u32[]{:S(2)}, u32[]{:S(2)}) collective-permute-start(bf16[128,768]{1,0:T(8,128)(2,1)} %eval_jaxpr.19), channel_id=1, source_target_pairs={{1,0},{2,1},{3,2},{4,3},{5,4},{6,5},{7,6},{9,8},{10,9},{11,10},{12... | collective-permute-start | bytes 589832 | tf_op jit(solution)/shard_map/while/body/eval_jaxpr/ppermute | solution.py:17
  (50 other events, 68.7 us)

commit v4 on v3

--- a/solution.py
+++ b/solution.py
@@ -135,7 +135,7 @@
 
 def finish_kernel(
     sent_ref, d_out_ref, conv_ref, values_ref, keys_ref, grad_ref, taps_ref, weight_ref,
-    o_ref, landed, extended, head, send_sems, recv_sems, rim_sems,
+    o_ref, next_ref, landed, extended, head, from_above, send_sems, recv_sems, rim_sems, hand_sems, acks,
 ):
     count = lax.axis_size("seq")
     rows, width = d_out_ref.shape
@@ -151,7 +151,30 @@
         return 0
 
     lax.fori_loop(1, count, greet, 0)
-    pl.semaphore_wait(barrier, count - 1)
+    sections = lax.axis_size("section")
+    has_up = section < sections - 1
+    has_down = section > 0
+    up = (me, jnp.minimum(section + 1, sections - 1))
+    down = (me, jnp.maximum(section - 1, 0))
+    neighbours = has_up.astype(jnp.int32) + has_down.astype(jnp.int32)
+
+    @pl.when(has_up)
+    def _():
+        pl.semaphore_signal(barrier, inc=1, device_id=up, device_id_type=mesh_ids)
+
+    @pl.when(has_down)
+    def _():
+        pl.semaphore_signal(barrier, inc=1, device_id=down, device_id_type=mesh_ids)
+
+    pl.semaphore_wait(barrier, count - 1 + neighbours)
+
+    @pl.when(has_up)
+    def _():
+        pl.semaphore_signal(acks, inc=1, device_id=up, device_id_type=mesh_ids)
+
+    @pl.when(has_down)
+    def _():
+        pl.semaphore_signal(acks, inc=1, device_id=down, device_id_type=mesh_ids)
 
     def describe(k):
         peer = lax.rem(me + k, count)
@@ -220,10 +243,37 @@
         d_proj, weight_ref[...], (((1,), (1,)), ((), ())), preferred_element_type=jnp.float32
     )
     o_ref[...] = total.astype(o_ref.dtype)
+    hand = pltpu.make_async_remote_copy(
+        src_ref=o_ref,
+        dst_ref=from_above,
+        send_sem=hand_sems.at[0],
+        recv_sem=hand_sems.at[1],
+        device_id=down,
+        device_id_type=mesh_ids,
+    )
+
+    @pl.when(has_down)
+    def _():
+        hand.start()
 
     @pl.when(me > 0)
     def _():
         rim.wait_send()
+
+    @pl.when(has_up)
+    def _():
+        hand.wait_recv()
+        next_ref[...] = from_above[...]
+
+    @pl.when(jnp.logical_not(has_up))
+    def _():
+        next_ref[...] = jnp.zeros(next_ref.shape, next_ref.dtype)
+
+    @pl.when(has_down)
+    def _():
+        hand.wait_send()
+
+    pl.semaphore_wait(acks, neighbours)
 
 
 def exchange_and_finish(sent, d_out, conv_wide, values, keys, grad_out, taps, weight_in):
@@ -232,16 +282,22 @@
     vmem = pl.BlockSpec(memory_space=pltpu.VMEM)
     return pl.pallas_call(
         finish_kernel,
-        out_shape=jax.ShapeDtypeStruct(grad_out.shape, grad_out.dtype),
+        out_shape=(
+            jax.ShapeDtypeStruct(grad_out.shape, grad_out.dtype),
+            jax.ShapeDtypeStruct(grad_out.shape, grad_out.dtype),
+        ),
         in_specs=[vmem] * 8,
-        out_specs=vmem,
+        out_specs=(vmem, vmem),
         scratch_shapes=[
             pltpu.VMEM(sent.shape, jnp.float32),
             pltpu.VMEM((rows + 8, taps.shape[1]), jnp.float32),
             pltpu.VMEM((8, taps.shape[1]), jnp.float32),
+            pltpu.VMEM(grad_out.shape, grad_out.dtype),
             pltpu.SemaphoreType.DMA((count,)),
             pltpu.SemaphoreType.DMA((count,)),
             pltpu.SemaphoreType.DMA((2,)),
+            pltpu.SemaphoreType.DMA((2,)),
+            pltpu.SemaphoreType.REGULAR,
         ],
         compiler_params=pltpu.CompilerParams(collective_id=1, has_side_effects=True),
     )(sent, d_out, conv_wide, values, keys, grad_out, taps, weight_in)
@@ -319,13 +375,15 @@
         active = (index >= 0) & (index < micro)
         slot = jnp.clip(index, 0, micro - 1)
         if micro == 1:
-            d_input = stage(incoming, 0)
+            d_input, arrived = stage(incoming, 0)
         else:
-            d_input = lax.switch(slot, [functools.partial(stage, slot=m) for m in range(micro)], incoming)
+            d_input, arrived = lax.switch(
+                slot, [functools.partial(stage, slot=m) for m in range(micro)], incoming
+            )
         grads = jnp.where(active, lax.dynamic_update_index_in_dim(grads, d_input, slot, 0), grads)
         later = jnp.clip(index + 1, 0, micro - 1)
         top = lax.dynamic_index_in_dim(cotangent, later, 0, keepdims=False)
-        incoming = jnp.where(section_place == section_count - 1, top, shifted(d_input, "section", -1))
+        incoming = jnp.where(section_place == section_count - 1, top, arrived)
         return (incoming, grads)
 
     start = (

time: 513 us -> 492 us (0.959)
  waiting for transfers between devices: 59.9 us -> 16.1 us
  Pallas kernels: 234 us -> 277 us
  starting transfers between devices: 27.1 us -> 15.7 us
    ppermute x9 -> x1, waiting for transfers between devices: 43.8 us -> 0.01 us  [shifted(): return lax.ppermute(value, axis, pairs)]
    pallas_call x8, Pallas kernels: 150 us -> 192 us  [exchange_and_finish(): pl.pallas_call(finish_kernel, out_shape=(jax.ShapeDtypeStruct(grad_out.sh...]
    ppermute x9 -> x1, starting transfers between devices: 15.9 us -> 4.51 us  [shifted(): return lax.ppermute(value, axis, pairs)]
    sin x9, other arithmetic: 8.28 us -> 1.93 us  [phase_table(): return (jnp.cos(angle), jnp.sin(angle))]
  transfers between devices with their start and end apart: 11 -> 3, of which waited for: 10 -> 2; matrix products, arithmetic and copies ran while one was open for 4% -> 1% of each run, Pallas kernels for 0% -> 0%
where the time goes in v4:
time: 492 us; the launch traced here: 490 us
  Pallas kernels  277 us (56%)
  matrix products  97.4 us (20%)
  local copies, waits for them, and re-layouts  41.6 us (8%)
  other arithmetic  39.1 us (8%)
  waiting for transfers between devices  16.1 us (3%)
  starting transfers between devices  15.7 us (3%)
    pallas_call x8, Pallas kernels, exchange_and_finish(): pl.pallas_call(finish_kernel, out_shape=(jax.ShapeDtypeStruct(grad_out.sh...  192 us
    pallas_call x8, Pallas kernels, seq_exchange(): pl.pallas_call(exchange_kernel, out_shape=jax.ShapeDtypeStruct(blocks.sha...  84.9 us
    select_n x8, other arithmetic, tick(): jnp.where(active, lax.dynamic_update_index_in_dim(grads, d_input, slot, 0...  14.4 us
    dot_general x8, matrix products, stage(): lax.dot_general(grad_out, weight_out, contract, preferred_element_type=jn...  10.4 us
    dot_general x10, matrix products, forward_spectrum(): real_one = jnp.einsum('kn,nbc->cbk', cos_outer, blocks, precision=accuracy)  9.96 us
  transfers between devices with their start and end apart: 3, of which 2 were waited for; matrix products, arithmetic and copies ran while one was open for 1% of the time, Pallas kernels for 0%

profile of v4, /device:TPU:1, one launch (start us, length us, event | category | flops | bytes accessed | tf_op | source)
XLA Modules:
  0.0 490.0 jit_solution(12076054058713938686)
XLA Ops:
  0.8 4.5 collective-permute-start
  6.1 1.0 convert_element_type.232
  7.2 1.2 maximum_convert_fusion
  8.7 1.0 fusion.296
  9.8 1.1 copy.138
  10.9 7.2 %all-to-all-start = ((bf16[2,128,768]{1,0,2:T(2,128)(2,1)}), bf16[2,128,768]{1,0,2:T(2,128)(2,1)S(1)}, u32[]{:S(2)}, u32[]{:S(2)}) async-start(bf16[2,128,768]{1,0,2:T(2,128)(2,1)} %copy.138), calls=%async_computation | async-start | bytes 786432 | tf_op jit(solution)/shard_map/all_to_all | solution.py:351
  18.9 9.3 %all-to-all-done = bf16[2,128,768]{1,0,2:T(2,128)(2,1)S(1)} async-done(((bf16[2,128,768]{1,0,2:T(2,128)(2,1)}), bf16[2,128,768]{1,0,2:T(2,128)(2,1)S(1)}, u32[]{:S(2)}, u32[]{:S(2)}) %all-to-all-start) | async-done | bytes 393248 | tf_op jit(solution)/shard_map/all_to_all | solution.py:351
  33.0 2.0 add_bitcast_fusion.1
  44.5 1.7 fusion.131
  46.3 1.5 copy.162
  47.7 1.1 div.18
  48.8 2.0 fusion.154
  50.8 4.0 all-to-all-start.1
  56.4 6.8 %all-to-all-done.1 = bf16[32,128,24]{1,2,0:T(8,128)(2,1)S(1)} async-done(((bf16[32,128,24]{1,2,0:T(8,128)(2,1)}), bf16[32,128,24]{1,2,0:T(8,128)(2,1)S(1)}, u32[]{:S(2)}, u32[]{:S(2)}) %all-to-all-start.1) | async-done | bytes 196640 | tf_op jit(solution)/shard_map/all_to_all | solution.py:356
  64.0 1.9 copy.164
  66.0 423.9 %while.19 = (s32[]{:T(128)}, bf16[128,768]{1,0:T(8,128)(2,1)S(1)}, bf16[1,128,768]{2,1,0:T(8,128)(2,1)}, pred[]{:T(512)}, bf16[1,128,768]{2,1,0:T(8,128)(2,1)}, ...) while((s32[]{:T(128)}, bf16[128,768]{1,0:T(8,128)(2,1)S(1)}, ...), condition=%wide.region_1.2_spmd.clone, body=%wide.region_0.1_spmd.clone.sunk | while | flops 1064730624 | bytes 53654092 | solution.py:393
  66.0 1.3 multiply_convert_fusion.3
  68.1 10.4 %eval_jaxpr.18 = bf16[32,24,128]{2,1,0:T(8,128)(2,1)} custom-call(bf16[32,24,128]{2,1,0:T(8,128)(2,1)} %bitcast.256), custom_call_target="tpu_custom_call" | custom-call | tf_op jit(solution)/shard_map/while/body/eval_jaxpr/pallas_call | solution.py:122
  90.8 1.0 fusion.387
  91.8 23.5 %eval_jaxpr.19 = (bf16[128,768]{1,0:T(8,128)(2,1)}, bf16[128,768]{1,0:T(8,128)(2,1)}) custom-call(f32[768,128]{1,0:T(8,128)} %bitcast.253, f32[128,768]{1,0:T(8,128)} %get-tuple-element.678.d_out_ref, f32[128,768]{1,0:T(8,128)} %get-tuple-element.727.conv_ref, f32[128,768]{1,0:T(8,128)S(1)} %copy-done.8, f32[128,768]{1,0:T(8,128)S(1)} %copy-done.7, ...), custom_call_target="tpu_custom_call" | custom-call | tf_op jit(solution)/shard_map/while/body/eval_jaxpr/pallas_call | solution.py:283
  115.3 1.7 bitcast_select_fusion.5
  117.1 1.0 bitcast_select_fusion.4
  118.2 1.3 multiply_convert_fusion.3
  120.3 10.4 %eval_jaxpr.18 = bf16[32,24,128]{2,1,0:T(8,128)(2,1)} custom-call(bf16[32,24,128]{2,1,0:T(8,128)(2,1)} %bitcast.256), custom_call_target="tpu_custom_call" | custom-call | tf_op jit(solution)/shard_map/while/body/eval_jaxpr/pallas_call | solution.py:122
  142.9 1.0 fusion.387
  143.9 24.7 %eval_jaxpr.19 = (bf16[128,768]{1,0:T(8,128)(2,1)}, bf16[128,768]{1,0:T(8,128)(2,1)}) custom-call(f32[768,128]{1,0:T(8,128)} %bitcast.253, f32[128,768]{1,0:T(8,128)} %get-tuple-element.678.d_out_ref, f32[128,768]{1,0:T(8,128)} %get-tuple-element.727.conv_ref, f32[128,768]{1,0:T(8,128)S(1)} %copy-done.8, f32[128,768]{1,0:T(8,128)S(1)} %copy-done.7, ...), custom_call_target="tpu_custom_call" | custom-call | tf_op jit(solution)/shard_map/while/body/eval_jaxpr/pallas_call | solution.py:283
  168.6 1.8 bitcast_select_fusion.5
  170.5 1.0 bitcast_select_fusion.4
  171.6 1.3 multiply_convert_fusion.3
  173.7 10.6 %eval_jaxpr.18 = bf16[32,24,128]{2,1,0:T(8,128)(2,1)} custom-call(bf16[32,24,128]{2,1,0:T(8,128)(2,1)} %bitcast.256), custom_call_target="tpu_custom_call" | custom-call | tf_op jit(solution)/shard_map/while/body/eval_jaxpr/pallas_call | solution.py:122
  196.5 1.0 fusion.387
  197.5 24.9 %eval_jaxpr.19 = (bf16[128,768]{1,0:T(8,128)(2,1)}, bf16[128,768]{1,0:T(8,128)(2,1)}) custom-call(f32[768,128]{1,0:T(8,128)} %bitcast.253, f32[128,768]{1,0:T(8,128)} %get-tuple-element.678.d_out_ref, f32[128,768]{1,0:T(8,128)} %get-tuple-element.727.conv_ref, f32[128,768]{1,0:T(8,128)S(1)} %copy-done.8, f32[128,768]{1,0:T(8,128)S(1)} %copy-done.7, ...), custom_call_target="tpu_custom_call" | custom-call | tf_op jit(solution)/shard_map/while/body/eval_jaxpr/pallas_call | solution.py:283
  222.4 1.8 bitcast_select_fusion.5
  224.2 1.0 bitcast_select_fusion.4
  225.4 1.3 multiply_convert_fusion.3
  227.5 10.7 %eval_jaxpr.18 = bf16[32,24,128]{2,1,0:T(8,128)(2,1)} custom-call(bf16[32,24,128]{2,1,0:T(8,128)(2,1)} %bitcast.256), custom_call_target="tpu_custom_call" | custom-call | tf_op jit(solution)/shard_map/while/body/eval_jaxpr/pallas_call | solution.py:122
  250.4 1.0 fusion.387
  251.4 25.4 %eval_jaxpr.19 = (bf16[128,768]{1,0:T(8,128)(2,1)}, bf16[128,768]{1,0:T(8,128)(2,1)}) custom-call(f32[768,128]{1,0:T(8,128)} %bitcast.253, f32[128,768]{1,0:T(8,128)} %get-tuple-element.678.d_out_ref, f32[128,768]{1,0:T(8,128)} %get-tuple-element.727.conv_ref, f32[128,768]{1,0:T(8,128)S(1)} %copy-done.8, f32[128,768]{1,0:T(8,128)S(1)} %copy-done.7, ...), custom_call_target="tpu_custom_call" | custom-call | tf_op jit(solution)/shard_map/while/body/eval_jaxpr/pallas_call | solution.py:283
  276.9 1.8 bitcast_select_fusion.5
  278.7 1.0 bitcast_select_fusion.4
  279.8 1.3 multiply_convert_fusion.3
  281.9 10.6 %eval_jaxpr.18 = bf16[32,24,128]{2,1,0:T(8,128)(2,1)} custom-call(bf16[32,24,128]{2,1,0:T(8,128)(2,1)} %bitcast.256), custom_call_target="tpu_custom_call" | custom-call | tf_op jit(solution)/shard_map/while/body/eval_jaxpr/pallas_call | solution.py:122
  304.8 1.0 fusion.387
  305.8 23.7 %eval_jaxpr.19 = (bf16[128,768]{1,0:T(8,128)(2,1)}, bf16[128,768]{1,0:T(8,128)(2,1)}) custom-call(f32[768,128]{1,0:T(8,128)} %bitcast.253, f32[128,768]{1,0:T(8,128)} %get-tuple-element.678.d_out_ref, f32[128,768]{1,0:T(8,128)} %get-tuple-element.727.conv_ref, f32[128,768]{1,0:T(8,128)S(1)} %copy-done.8, f32[128,768]{1,0:T(8,128)S(1)} %copy-done.7, ...), custom_call_target="tpu_custom_call" | custom-call | tf_op jit(solution)/shard_map/while/body/eval_jaxpr/pallas_call | solution.py:283
  329.5 1.8 bitcast_select_fusion.5
  331.3 1.0 bitcast_select_fusion.4
  332.5 1.3 multiply_convert_fusion.3
  334.6 10.6 %eval_jaxpr.18 = bf16[32,24,128]{2,1,0:T(8,128)(2,1)} custom-call(bf16[32,24,128]{2,1,0:T(8,128)(2,1)} %bitcast.256), custom_call_target="tpu_custom_call" | custom-call | tf_op jit(solution)/shard_map/while/body/eval_jaxpr/pallas_call | solution.py:122
  357.4 1.0 fusion.387
  358.5 23.7 %eval_jaxpr.19 = (bf16[128,768]{1,0:T(8,128)(2,1)}, bf16[128,768]{1,0:T(8,128)(2,1)}) custom-call(f32[768,128]{1,0:T(8,128)} %bitcast.253, f32[128,768]{1,0:T(8,128)} %get-tuple-element.678.d_out_ref, f32[128,768]{1,0:T(8,128)} %get-tuple-element.727.conv_ref, f32[128,768]{1,0:T(8,128)S(1)} %copy-done.8, f32[128,768]{1,0:T(8,128)S(1)} %copy-done.7, ...), custom_call_target="tpu_custom_call" | custom-call | tf_op jit(solution)/shard_map/while/body/eval_jaxpr/pallas_call | solution.py:283
  382.2 1.8 bitcast_select_fusion.5
  384.0 1.0 bitcast_select_fusion.4
  385.1 1.3 multiply_convert_fusion.3
  387.2 10.6 %eval_jaxpr.18 = bf16[32,24,128]{2,1,0:T(8,128)(2,1)} custom-call(bf16[32,24,128]{2,1,0:T(8,128)(2,1)} %bitcast.256), custom_call_target="tpu_custom_call" | custom-call | tf_op jit(solution)/shard_map/while/body/eval_jaxpr/pallas_call | solution.py:122
  410.1 1.0 fusion.387
  411.1 24.2 %eval_jaxpr.19 = (bf16[128,768]{1,0:T(8,128)(2,1)}, bf16[128,768]{1,0:T(8,128)(2,1)}) custom-call(f32[768,128]{1,0:T(8,128)} %bitcast.253, f32[128,768]{1,0:T(8,128)} %get-tuple-element.678.d_out_ref, f32[128,768]{1,0:T(8,128)} %get-tuple-element.727.conv_ref, f32[128,768]{1,0:T(8,128)S(1)} %copy-done.8, f32[128,768]{1,0:T(8,128)S(1)} %copy-done.7, ...), custom_call_target="tpu_custom_call" | custom-call | tf_op jit(solution)/shard_map/while/body/eval_jaxpr/pallas_call | solution.py:283
  435.4 1.8 bitcast_select_fusion.5
  437.2 1.0 bitcast_select_fusion.4
  438.3 1.3 multiply_convert_fusion.3
  440.4 10.9 %eval_jaxpr.18 = bf16[32,24,128]{2,1,0:T(8,128)(2,1)} custom-call(bf16[32,24,128]{2,1,0:T(8,128)(2,1)} %bitcast.256), custom_call_target="tpu_custom_call" | custom-call | tf_op jit(solution)/shard_map/while/body/eval_jaxpr/pallas_call | solution.py:122
  463.6 1.0 fusion.387
  464.6 22.3 %eval_jaxpr.19 = (bf16[128,768]{1,0:T(8,128)(2,1)}, bf16[128,768]{1,0:T(8,128)(2,1)}) custom-call(f32[768,128]{1,0:T(8,128)} %bitcast.253, f32[128,768]{1,0:T(8,128)} %get-tuple-element.678.d_out_ref, f32[128,768]{1,0:T(8,128)} %get-tuple-element.727.conv_ref, f32[128,768]{1,0:T(8,128)S(1)} %copy-done.8, f32[128,768]{1,0:T(8,128)S(1)} %copy-done.7, ...), custom_call_target="tpu_custom_call" | custom-call | tf_op jit(solution)/shard_map/while/body/eval_jaxpr/pallas_call | solution.py:283
  486.9 1.8 bitcast_select_fusion.5
  488.7 1.0 bitcast_select_fusion.4
  (361 shorter events, 122.3 us)
Async XLA Ops:
  0.0 18.1 %copy-start = (f32[1,768]{1,0:T(1,128)S(1)}, f32[1,768]{1,0:T(1,128)}, u32[]{:S(2)}) copy-start(f32[1,768]{1,0:T(1,128)} %param.15) | copy-start | bytes 9220
  0.8 6.4 %collective-permute-start = (bf16[2,2304]{1,0:T(2,128)(2,1)S(1)}, bf16[2,2304]{1,0:T(2,128)(2,1)S(1)}, u32[]{:S(2)}, u32[]{:S(2)}) collective-permute-start(bf16[2,2304]{1,0:T(2,128)(2,1)S(1)} %slice_bitcast_fusion), channel_id=1, source_target_pairs={{0,8},{8,16},{16,24},{24,32},{32,40},{40,48},{48,56},{56,64},{64,7... | collective-permute-start | bytes 27656 | tf_op jit(solution)/shard_map/ppermute | solution.py:17
  10.9 17.4 %all-to-all-start = ((bf16[2,128,768]{1,0,2:T(2,128)(2,1)}), bf16[2,128,768]{1,0,2:T(2,128)(2,1)S(1)}, u32[]{:S(2)}, u32[]{:S(2)}) async-start(bf16[2,128,768]{1,0,2:T(2,128)(2,1)} %copy.138), calls=%async_computation | async-start | bytes 786432 | tf_op jit(solution)/shard_map/all_to_all | solution.py:351
  48.8 6.0 %copy-start.16 = (f32[1,3,2304]{2,0,1:T(1,128)S(1)}, f32[1,3,2304]{2,0,1:T(1,128)}, u32[]{:S(2)}) copy-start(f32[1,3,2304]{2,0,1:T(1,128)} %param.13) | copy-start | bytes 82948
  50.8 15.1 %copy-start.4 = (bf16[1,768,768]{2,1,0:T(8,128)(2,1)S(1)}, bf16[1,768,768]{2,1,0:T(8,128)(2,1)}, u32[]{:S(2)}) copy-start(bf16[1,768,768]{2,1,0:T(8,128)(2,1)} %param.12) | copy-start | bytes 3538948
  50.8 12.4 %all-to-all-start.1 = ((bf16[32,128,24]{1,2,0:T(8,128)(2,1)}), bf16[32,128,24]{1,2,0:T(8,128)(2,1)S(1)}, u32[]{:S(2)}, u32[]{:S(2)}) async-start(bf16[32,128,24]{1,2,0:T(8,128)(2,1)} %fusion.154), calls=%async_computation.1 | async-start | bytes 393216 | tf_op jit(solution)/shard_map/all_to_all | solution.py:356
  66.0 16.1 %copy-start.6 = (bf16[128,768]{1,0:T(8,128)(2,1)}, bf16[128,768]{1,0:T(8,128)(2,1)S(1)}, u32[]{:S(2)}) copy-start(bf16[128,768]{1,0:T(8,128)(2,1)S(1)} %get-tuple-element.700.grad_ref) | copy-start | bytes 589828 | tf_op jit(solution)/shard_map/while
  66.0 18.2 %copy-start.2 = (f32[24,32,256]{2,1,0:T(8,128)}, f32[24,32,256]{2,1,0:T(8,128)S(1)}, u32[]{:S(2)}) copy-start(f32[24,32,256]{2,1,0:T(8,128)S(1)} %get-tuple-element.724) | copy-start | bytes 2359300 | tf_op jit(solution)/shard_map/while
  89.8 1.9 copy-start.7
  89.8 1.9 copy-start.13
  90.2 1.5 copy-start.8
  91.8 26.4 %copy-start.5 = (bf16[1,768,768]{2,1,0:T(8,128)(2,1)S(1)}, bf16[1,768,768]{2,1,0:T(8,128)(2,1)}, u32[]{:S(2)}) copy-start(bf16[1,768,768]{2,1,0:T(8,128)(2,1)} %get-tuple-element.753) | copy-start | bytes 3538948 | tf_op jit(solution)/shard_map/while
  115.3 2.8 copy-start.3
  115.3 2.8 copy-start.10
  118.2 16.1 %copy-start.6 = (bf16[128,768]{1,0:T(8,128)(2,1)}, bf16[128,768]{1,0:T(8,128)(2,1)S(1)}, u32[]{:S(2)}) copy-start(bf16[128,768]{1,0:T(8,128)(2,1)S(1)} %get-tuple-element.700.grad_ref) | copy-start | bytes 589828 | tf_op jit(solution)/shard_map/while
  118.2 18.2 %copy-start.2 = (f32[24,32,256]{2,1,0:T(8,128)}, f32[24,32,256]{2,1,0:T(8,128)S(1)}, u32[]{:S(2)}) copy-start(f32[24,32,256]{2,1,0:T(8,128)S(1)} %get-tuple-element.724) | copy-start | bytes 2359300 | tf_op jit(solution)/shard_map/while
  142.0 1.9 copy-start.7
  142.0 1.9 copy-start.13
  143.9 27.6 %copy-start.5 = (bf16[1,768,768]{2,1,0:T(8,128)(2,1)S(1)}, bf16[1,768,768]{2,1,0:T(8,128)(2,1)}, u32[]{:S(2)}) copy-start(bf16[1,768,768]{2,1,0:T(8,128)(2,1)} %get-tuple-element.753) | copy-start | bytes 3538948 | tf_op jit(solution)/shard_map/while
  168.6 2.9 copy-start.3
  168.6 2.9 copy-start.10
  171.6 16.2 %copy-start.6 = (bf16[128,768]{1,0:T(8,128)(2,1)}, bf16[128,768]{1,0:T(8,128)(2,1)S(1)}, u32[]{:S(2)}) copy-start(bf16[128,768]{1,0:T(8,128)(2,1)S(1)} %get-tuple-element.700.grad_ref) | copy-start | bytes 589828 | tf_op jit(solution)/shard_map/while
  171.6 18.4 %copy-start.2 = (f32[24,32,256]{2,1,0:T(8,128)}, f32[24,32,256]{2,1,0:T(8,128)S(1)}, u32[]{:S(2)}) copy-start(f32[24,32,256]{2,1,0:T(8,128)S(1)} %get-tuple-element.724) | copy-start | bytes 2359300 | tf_op jit(solution)/shard_map/while
  195.6 1.9 copy-start.7
  195.6 1.9 copy-start.13
  197.5 27.8 %copy-start.5 = (bf16[1,768,768]{2,1,0:T(8,128)(2,1)S(1)}, bf16[1,768,768]{2,1,0:T(8,128)(2,1)}, u32[]{:S(2)}) copy-start(bf16[1,768,768]{2,1,0:T(8,128)(2,1)} %get-tuple-element.753) | copy-start | bytes 3538948 | tf_op jit(solution)/shard_map/while
  222.4 2.9 copy-start.3
  222.4 2.9 copy-start.10
  225.3 16.4 %copy-start.6 = (bf16[128,768]{1,0:T(8,128)(2,1)}, bf16[128,768]{1,0:T(8,128)(2,1)S(1)}, u32[]{:S(2)}) copy-start(bf16[128,768]{1,0:T(8,128)(2,1)S(1)} %get-tuple-element.700.grad_ref) | copy-start | bytes 589828 | tf_op jit(solution)/shard_map/while
  225.4 18.5 %copy-start.2 = (f32[24,32,256]{2,1,0:T(8,128)}, f32[24,32,256]{2,1,0:T(8,128)S(1)}, u32[]{:S(2)}) copy-start(f32[24,32,256]{2,1,0:T(8,128)S(1)} %get-tuple-element.724) | copy-start | bytes 2359300 | tf_op jit(solution)/shard_map/while
  249.5 1.9 copy-start.7
  249.5 1.9 copy-start.13
  249.9 1.5 copy-start.8
  251.4 28.3 %copy-start.5 = (bf16[1,768,768]{2,1,0:T(8,128)(2,1)S(1)}, bf16[1,768,768]{2,1,0:T(8,128)(2,1)}, u32[]{:S(2)}) copy-start(bf16[1,768,768]{2,1,0:T(8,128)(2,1)} %get-tuple-element.753) | copy-start | bytes 3538948 | tf_op jit(solution)/shard_map/while
  276.8 2.9 copy-start.3
  276.8 2.9 copy-start.10
  279.8 16.3 %copy-start.6 = (bf16[128,768]{1,0:T(8,128)(2,1)}, bf16[128,768]{1,0:T(8,128)(2,1)S(1)}, u32[]{:S(2)}) copy-start(bf16[128,768]{1,0:T(8,128)(2,1)S(1)} %get-tuple-element.700.grad_ref) | copy-start | bytes 589828 | tf_op jit(solution)/shard_map/while
  279.8 18.4 %copy-start.2 = (f32[24,32,256]{2,1,0:T(8,128)}, f32[24,32,256]{2,1,0:T(8,128)S(1)}, u32[]{:S(2)}) copy-start(f32[24,32,256]{2,1,0:T(8,128)S(1)} %get-tuple-element.724) | copy-start | bytes 2359300 | tf_op jit(solution)/shard_map/while
  303.9 1.9 copy-start.7
  303.9 1.9 copy-start.13
  305.8 26.6 %copy-start.5 = (bf16[1,768,768]{2,1,0:T(8,128)(2,1)S(1)}, bf16[1,768,768]{2,1,0:T(8,128)(2,1)}, u32[]{:S(2)}) copy-start(bf16[1,768,768]{2,1,0:T(8,128)(2,1)} %get-tuple-element.753) | copy-start | bytes 3538948 | tf_op jit(solution)/shard_map/while
  329.5 2.9 copy-start.3
  329.5 2.9 copy-start.10
  332.4 16.3 %copy-start.6 = (bf16[128,768]{1,0:T(8,128)(2,1)}, bf16[128,768]{1,0:T(8,128)(2,1)S(1)}, u32[]{:S(2)}) copy-start(bf16[128,768]{1,0:T(8,128)(2,1)S(1)} %get-tuple-element.700.grad_ref) | copy-start | bytes 589828 | tf_op jit(solution)/shard_map/while
  332.5 18.4 %copy-start.2 = (f32[24,32,256]{2,1,0:T(8,128)}, f32[24,32,256]{2,1,0:T(8,128)S(1)}, u32[]{:S(2)}) copy-start(f32[24,32,256]{2,1,0:T(8,128)S(1)} %get-tuple-element.724) | copy-start | bytes 2359300 | tf_op jit(solution)/shard_map/while
  356.5 1.9 copy-start.7
  356.5 1.9 copy-start.13
  358.5 26.6 %copy-start.5 = (bf16[1,768,768]{2,1,0:T(8,128)(2,1)S(1)}, bf16[1,768,768]{2,1,0:T(8,128)(2,1)}, u32[]{:S(2)}) copy-start(bf16[1,768,768]{2,1,0:T(8,128)(2,1)} %get-tuple-element.753) | copy-start | bytes 3538948 | tf_op jit(solution)/shard_map/while
  382.1 2.9 copy-start.3
  382.2 2.9 copy-start.10
  385.1 16.3 %copy-start.6 = (bf16[128,768]{1,0:T(8,128)(2,1)}, bf16[128,768]{1,0:T(8,128)(2,1)S(1)}, u32[]{:S(2)}) copy-start(bf16[128,768]{1,0:T(8,128)(2,1)S(1)} %get-tuple-element.700.grad_ref) | copy-start | bytes 589828 | tf_op jit(solution)/shard_map/while
  385.1 18.4 %copy-start.2 = (f32[24,32,256]{2,1,0:T(8,128)}, f32[24,32,256]{2,1,0:T(8,128)S(1)}, u32[]{:S(2)}) copy-start(f32[24,32,256]{2,1,0:T(8,128)S(1)} %get-tuple-element.724) | copy-start | bytes 2359300 | tf_op jit(solution)/shard_map/while
  409.2 1.9 copy-start.7
  409.2 1.9 copy-start.13
  411.1 27.1 %copy-start.5 = (bf16[1,768,768]{2,1,0:T(8,128)(2,1)S(1)}, bf16[1,768,768]{2,1,0:T(8,128)(2,1)}, u32[]{:S(2)}) copy-start(bf16[1,768,768]{2,1,0:T(8,128)(2,1)} %get-tuple-element.753) | copy-start | bytes 3538948 | tf_op jit(solution)/shard_map/while
  435.3 2.9 copy-start.3
  435.3 2.9 copy-start.10
  438.3 16.6 %copy-start.6 = (bf16[128,768]{1,0:T(8,128)(2,1)}, bf16[128,768]{1,0:T(8,128)(2,1)S(1)}, u32[]{:S(2)}) copy-start(bf16[128,768]{1,0:T(8,128)(2,1)S(1)} %get-tuple-element.700.grad_ref) | copy-start | bytes 589828 | tf_op jit(solution)/shard_map/while
  438.3 18.7 %copy-start.2 = (f32[24,32,256]{2,1,0:T(8,128)}, f32[24,32,256]{2,1,0:T(8,128)S(1)}, u32[]{:S(2)}) copy-start(f32[24,32,256]{2,1,0:T(8,128)S(1)} %get-tuple-element.724) | copy-start | bytes 2359300 | tf_op jit(solution)/shard_map/while
  462.6 1.9 copy-start.7
  462.7 1.9 copy-start.13
  464.6 25.2 %copy-start.5 = (bf16[1,768,768]{2,1,0:T(8,128)(2,1)S(1)}, bf16[1,768,768]{2,1,0:T(8,128)(2,1)}, u32[]{:S(2)}) copy-start(bf16[1,768,768]{2,1,0:T(8,128)(2,1)} %get-tuple-element.753) | copy-start | bytes 3538948 | tf_op jit(solution)/shard_map/while
  486.9 2.9 copy-start.3
  486.9 2.9 copy-start.10
  (26 other events, 30.3 us)

commit v5 on v4

--- a/solution.py
+++ b/solution.py
@@ -29,37 +29,53 @@
     outer = 2 * length // inner
     blocks = series.reshape(length // inner, inner, chans)
     cos_outer, sin_outer = phase_table(outer, length // inner, outer)
-    real_one = jnp.einsum("kn,nbc->cbk", cos_outer, blocks, precision=accuracy)
-    imag_one = -jnp.einsum("kn,nbc->cbk", sin_outer, blocks, precision=accuracy)
+    one = jnp.einsum(
+        "kn,nbc->cbk", jnp.concatenate([cos_outer, -sin_outer], axis=0), blocks, precision=accuracy
+    )
+    real_one = one[:, :, :outer]
+    imag_one = one[:, :, outer:]
     cos_twist, sin_twist = phase_table(inner, outer, 2 * length)
     real_two = real_one * cos_twist + imag_one * sin_twist
     imag_two = imag_one * cos_twist - real_one * sin_twist
     cos_inner, sin_inner = phase_table(inner, inner, inner)
-    real = jnp.einsum("jb,cbk->cjk", cos_inner, real_two, precision=accuracy) + jnp.einsum(
-        "jb,cbk->cjk", sin_inner, imag_two, precision=accuracy
-    )
-    imag = jnp.einsum("jb,cbk->cjk", cos_inner, imag_two, precision=accuracy) - jnp.einsum(
-        "jb,cbk->cjk", sin_inner, real_two, precision=accuracy
-    )
-    return (real, imag)
+    mixer = jnp.concatenate(
+        [
+            jnp.concatenate([cos_inner, sin_inner], axis=1),
+            jnp.concatenate([-sin_inner, cos_inner], axis=1),
+        ],
+        axis=0,
+    )
+    both = jnp.einsum(
+        "jb,cbk->cjk", mixer, jnp.concatenate([real_two, imag_two], axis=1), precision=accuracy
+    )
+    return (both[:, :inner], both[:, inner:])
 
 
 def inverse_spectrum(real, imag, inner):
     chans, _, outer = real.shape
     length = outer * inner // 2
     cos_inner, sin_inner = phase_table(inner, inner, inner)
-    real_one = jnp.einsum("jb,cjk->cbk", cos_inner, real, precision=accuracy) - jnp.einsum(
-        "jb,cjk->cbk", sin_inner, imag, precision=accuracy
-    )
-    imag_one = jnp.einsum("jb,cjk->cbk", cos_inner, imag, precision=accuracy) + jnp.einsum(
-        "jb,cjk->cbk", sin_inner, real, precision=accuracy
-    )
+    mixer = jnp.concatenate(
+        [
+            jnp.concatenate([cos_inner, -sin_inner], axis=1),
+            jnp.concatenate([sin_inner, cos_inner], axis=1),
+        ],
+        axis=0,
+    )
+    both = jnp.einsum(
+        "jb,cjk->cbk", mixer.T, jnp.concatenate([real, imag], axis=1), precision=accuracy
+    )
+    real_one = both[:, :inner]
+    imag_one = both[:, inner:]
     cos_twist, sin_twist = phase_table(inner, outer, 2 * length)
     real_two = real_one * cos_twist - imag_one * sin_twist
     imag_two = imag_one * cos_twist + real_one * sin_twist
     cos_outer, sin_outer = phase_table(outer, length // inner, outer)
-    series = jnp.einsum("kn,cbk->nbc", cos_outer, real_two, precision=accuracy) - jnp.einsum(
-        "kn,cbk->nbc", sin_outer, imag_two, precision=accuracy
+    series = jnp.einsum(
+        "kn,cbk->nbc",
+        jnp.concatenate([cos_outer, -sin_outer], axis=0),
+        jnp.concatenate([real_two, imag_two], axis=2),
+        precision=accuracy,
     )
     return series.reshape(length, chans) / (2.0 * length)
 
@@ -134,7 +150,7 @@
 
 
 def finish_kernel(
-    sent_ref, d_out_ref, conv_ref, values_ref, keys_ref, grad_ref, taps_ref, weight_ref,
+    sent_ref, d_out_ref, conv_ref, values_ref, keys_ref, grad_ref, taps_ref, weight_ref, top_ref,
     o_ref, next_ref, landed, extended, head, from_above, send_sems, recv_sems, rim_sems, hand_sems, acks,
 ):
     count = lax.axis_size("seq")
@@ -267,7 +283,7 @@
 
     @pl.when(jnp.logical_not(has_up))
     def _():
-        next_ref[...] = jnp.zeros(next_ref.shape, next_ref.dtype)
+        next_ref[...] = top_ref[...]
 
     @pl.when(has_down)
     def _():
@@ -276,7 +292,7 @@
     pl.semaphore_wait(acks, neighbours)
 
 
-def exchange_and_finish(sent, d_out, conv_wide, values, keys, grad_out, taps, weight_in):
+def exchange_and_finish(sent, d_out, conv_wide, values, keys, grad_out, taps, weight_in, top):
     count = lax.axis_size("seq")
     rows, width = d_out.shape
     vmem = pl.BlockSpec(memory_space=pltpu.VMEM)
@@ -286,7 +302,7 @@
             jax.ShapeDtypeStruct(grad_out.shape, grad_out.dtype),
             jax.ShapeDtypeStruct(grad_out.shape, grad_out.dtype),
         ),
-        in_specs=[vmem] * 8,
+        in_specs=[vmem] * 9,
         out_specs=(vmem, vmem),
         scratch_shapes=[
             pltpu.VMEM(sent.shape, jnp.float32),
@@ -300,7 +316,7 @@
             pltpu.SemaphoreType.REGULAR,
         ],
         compiler_params=pltpu.CompilerParams(collective_id=1, has_side_effects=True),
-    )(sent, d_out, conv_wide, values, keys, grad_out, taps, weight_in)
+    )(sent, d_out, conv_wide, values, keys, grad_out, taps, weight_in, top)
 
 
 def when(active, action, *operands):
@@ -356,7 +372,7 @@
         conv = lax.all_to_all(causal(product_local), "seq", split_axis=0, concat_axis=1, tiled=True)
         forward.append((query, keys, values, conv.astype(jnp.float32)))
 
-    def stage(grad_out, slot):
+    def stage(grad_out, top, slot):
         query, keys, values, conv_wide = forward[slot]
         d_out = lax.dot_general(grad_out, weight_out, contract, preferred_element_type=jnp.float32)
         d_conv = (d_out * query).astype(jnp.bfloat16)
@@ -366,7 +382,7 @@
         sent_back = d_prod_local.reshape(seq_count, height, chans).transpose(0, 2, 1)
         sent_back = sent_back.reshape(seq_count * chans, height).astype(jnp.float32)
         return exchange_and_finish(
-            sent_back, d_out, conv_wide, values, keys, grad_out, taps, weight_in
+            sent_back, d_out, conv_wide, values, keys, grad_out, taps, weight_in, top
         )
 
     def tick(step, carry):
@@ -374,16 +390,15 @@
         index = step - (section_count - 1 - section_place)
         active = (index >= 0) & (index < micro)
         slot = jnp.clip(index, 0, micro - 1)
+        later = jnp.clip(index + 1, 0, micro - 1)
+        top = lax.dynamic_index_in_dim(cotangent, later, 0, keepdims=False)
         if micro == 1:
-            d_input, arrived = stage(incoming, 0)
+            d_input, incoming = stage(incoming, top, 0)
         else:
-            d_input, arrived = lax.switch(
-                slot, [functools.partial(stage, slot=m) for m in range(micro)], incoming
+            d_input, incoming = lax.switch(
+                slot, [functools.partial(stage, slot=m) for m in range(micro)], incoming, top
             )
         grads = jnp.where(active, lax.dynamic_update_index_in_dim(grads, d_input, slot, 0), grads)
-        later = jnp.clip(index + 1, 0, micro - 1)
-        top = lax.dynamic_index_in_dim(cotangent, later, 0, keepdims=False)
-        incoming = jnp.where(section_place == section_count - 1, top, arrived)
         return (incoming, grads)
 
     start = (

time: 492 us -> 479 us (0.974)
  matrix products: 97.4 us -> 52.1 us
  local copies, waits for them, and re-layouts: 41.6 us -> 67.2 us
    dot_general x114 -> x38, matrix products: 87 us -> 40.8 us  [the longest x10 13.2 us: forward_spectrum(): jnp.einsum('kn,nbc->cbk', jnp.concatenate([cos_outer, -sin_outer], axis=0...]
    reshape x20, local copies, waits for them, and re-layouts: 6.34 us -> 19.1 us  [forward_spectrum(): blocks = series.reshape(length // inner, inner, chans)]
    select_n x8 -> x0, other arithmetic: 8.35 us -> none  [tick(): incoming = jnp.where(section_place == section_count - 1, top, arrived)]
    dot_general x0 -> x9, local copies, waits for them, and re-layouts: none -> 8.24 us  [inverse_spectrum(): jnp.einsum('jb,cjk->cbk', mixer.T, jnp.concatenate([real, imag], axis=1),...]
    neg x0 -> x18, other arithmetic: none -> 5.54 us  [the longest x9 4.78 us: forward_spectrum(): -sin_outer]
    transpose x8, local copies, waits for them, and re-layouts: 7.64 us -> 13.1 us  [stage(): d_conv_local = sent.transpose(0, 2, 1).reshape(length, chans)]
where the time goes in v5:
time: 479 us; the launch traced here: 477 us
  Pallas kernels  278 us (58%)
  local copies, waits for them, and re-layouts  67.2 us (14%)
  matrix products  52.1 us (11%)
  other arithmetic  43.8 us (9%)
  waiting for transfers between devices  17 us (4%)
  starting transfers between devices  16.3 us (3%)
    pallas_call x8, Pallas kernels, exchange_and_finish(): pl.pallas_call(finish_kernel, out_shape=(jax.ShapeDtypeStruct(grad_out.sh...  194 us
    pallas_call x8, Pallas kernels, seq_exchange(): pl.pallas_call(exchange_kernel, out_shape=jax.ShapeDtypeStruct(blocks.sha...  84.8 us
    reshape x20, local copies, waits for them, and re-layouts, forward_spectrum(): blocks = series.reshape(length // inner, inner, chans)  19.1 us
    select_n x8, other arithmetic, tick(): jnp.where(active, lax.dynamic_update_index_in_dim(grads, d_input, slot, 0...  13.7 us
    dot_general x10, matrix products, forward_spectrum(): jnp.einsum('kn,nbc->cbk', jnp.concatenate([cos_outer, -sin_outer], axis=0...  13.2 us
    transpose x8, local copies, waits for them, and re-layouts, stage(): d_conv_local = sent.transpose(0, 2, 1).reshape(length, chans)  13.1 us
    dot_general x10, matrix products, forward_spectrum(): jnp.einsum('jb,cbk->cjk', mixer, jnp.concatenate([real_two, imag_two], ax...  12.3 us
    div x18, local copies, waits for them, and re-layouts, inverse_spectrum(): return series.reshape(length, chans) / (2.0 * length)  12.2 us
  transfers between devices with their start and end apart: 3, of which 2 were waited for; matrix products, arithmetic and copies ran while one was open for 1% of the time, Pallas kernels for 0%

profile of v5, /device:TPU:1, one launch (start us, length us, event | category | flops | bytes accessed | tf_op | source)
XLA Modules:
  0.0 477.2 jit_solution(6561630600079654114)
XLA Ops:
  0.8 4.5 collective-permute-start
  10.9 7.1 %all-to-all-start = ((bf16[2,128,768]{1,0,2:T(2,128)(2,1)}), bf16[2,128,768]{1,0,2:T(2,128)(2,1)S(1)}, u32[]{:S(2)}, u32[]{:S(2)}) async-start(bf16[2,128,768]{1,0,2:T(2,128)(2,1)} %copy.72), calls=%async_computation | async-start | bytes 786432 | tf_op jit(solution)/shard_map/all_to_all | solution.py:367
  19.0 9.2 %all-to-all-done = bf16[2,128,768]{1,0,2:T(2,128)(2,1)S(1)} async-done(((bf16[2,128,768]{1,0,2:T(2,128)(2,1)}), bf16[2,128,768]{1,0,2:T(2,128)(2,1)S(1)}, u32[]{:S(2)}, u32[]{:S(2)}) %all-to-all-start) | async-done | bytes 393248 | tf_op jit(solution)/shard_map/all_to_all | solution.py:367
  38.2 1.6 fusion.80
  39.8 2.6 copy.81
  42.4 2.6 div.18
  45.0 2.1 fusion.86
  47.1 4.7 all-to-all-start.1
  52.5 7.8 %all-to-all-done.1 = bf16[32,128,24]{1,2,0:T(8,128)(2,1)} async-done(((bf16[32,128,24]{1,2,0:T(8,128)(2,1)}), bf16[32,128,24]{1,2,0:T(8,128)(2,1)}, u32[]{:S(2)}, u32[]{:S(2)}) %all-to-all-start.1) | async-done | bytes 196640 | tf_op jit(solution)/shard_map/all_to_all | solution.py:372
  60.3 1.7 convert_element_type.227
  62.0 1.9 copy.83
  63.9 413.1 %while.19 = (s32[]{:T(128)}, bf16[128,768]{1,0:T(8,128)(2,1)S(1)}, bf16[1,128,768]{2,1,0:T(8,128)(2,1)}, bf16[768,768]{1,0:T(8,128)(2,1)S(1)}, f32[128,768]{1,0:...) while((s32[]{:T(128)}, bf16[128,768]{1,0:T(8,128)(2,1)S(1)}, ...), condition=%wide.region_1.2_spmd.clone, body=%wide.region_0.1_spmd.clone.sunk | while | flops 1063457792 | bytes 53908012 | solution.py:408
  63.9 1.4 multiply_convert_fusion.3
  66.2 10.4 %eval_jaxpr.18 = bf16[32,24,128]{2,1,0:T(8,128)(2,1)} custom-call(bf16[32,24,128]{2,1,0:T(8,128)(2,1)} %bitcast.136), custom_call_target="tpu_custom_call" | custom-call | tf_op jit(solution)/shard_map/while/body/eval_jaxpr/pallas_call | solution.py:138
  76.6 1.6 copy.119
  78.3 1.2 reshape.155
  81.0 1.5 convolution_bitcast_fusion.4
  89.4 23.7 %eval_jaxpr.19 = (bf16[128,768]{1,0:T(8,128)(2,1)}, bf16[128,768]{1,0:T(8,128)(2,1)S(1)}) custom-call(f32[768,128]{1,0:T(8,128)} %bitcast.134, f32[128,768]{1,0:T(8,128)} %get-tuple-element.689.d_out_ref, f32[128,768]{1,0:T(8,128)} %get-tuple-element.735.conv_ref, f32[128,768]{1,0:T(8,128)} %get-tuple-element.736.values_ref, ...), custom_call_target="tpu_custom_call" | custom-call | tf_op jit(solution)/shard_map/while/body/eval_jaxpr/pallas_call | solution.py:299
  113.1 1.6 bitcast_select_fusion.2
  114.8 1.4 multiply_convert_fusion.3
  117.1 10.4 %eval_jaxpr.18 = bf16[32,24,128]{2,1,0:T(8,128)(2,1)} custom-call(bf16[32,24,128]{2,1,0:T(8,128)(2,1)} %bitcast.136), custom_call_target="tpu_custom_call" | custom-call | tf_op jit(solution)/shard_map/while/body/eval_jaxpr/pallas_call | solution.py:138
  127.4 1.6 copy.119
  131.8 1.5 convolution_bitcast_fusion.4
  140.2 24.8 %eval_jaxpr.19 = (bf16[128,768]{1,0:T(8,128)(2,1)}, bf16[128,768]{1,0:T(8,128)(2,1)S(1)}) custom-call(f32[768,128]{1,0:T(8,128)} %bitcast.134, f32[128,768]{1,0:T(8,128)} %get-tuple-element.689.d_out_ref, f32[128,768]{1,0:T(8,128)} %get-tuple-element.735.conv_ref, f32[128,768]{1,0:T(8,128)} %get-tuple-element.736.values_ref, ...), custom_call_target="tpu_custom_call" | custom-call | tf_op jit(solution)/shard_map/while/body/eval_jaxpr/pallas_call | solution.py:299
  165.0 1.7 bitcast_select_fusion.2
  166.8 1.4 multiply_convert_fusion.3
  169.0 10.6 %eval_jaxpr.18 = bf16[32,24,128]{2,1,0:T(8,128)(2,1)} custom-call(bf16[32,24,128]{2,1,0:T(8,128)(2,1)} %bitcast.136), custom_call_target="tpu_custom_call" | custom-call | tf_op jit(solution)/shard_map/while/body/eval_jaxpr/pallas_call | solution.py:138
  179.7 1.6 copy.119
  184.1 1.5 convolution_bitcast_fusion.4
  192.4 24.9 %eval_jaxpr.19 = (bf16[128,768]{1,0:T(8,128)(2,1)}, bf16[128,768]{1,0:T(8,128)(2,1)S(1)}) custom-call(f32[768,128]{1,0:T(8,128)} %bitcast.134, f32[128,768]{1,0:T(8,128)} %get-tuple-element.689.d_out_ref, f32[128,768]{1,0:T(8,128)} %get-tuple-element.735.conv_ref, f32[128,768]{1,0:T(8,128)} %get-tuple-element.736.values_ref, ...), custom_call_target="tpu_custom_call" | custom-call | tf_op jit(solution)/shard_map/while/body/eval_jaxpr/pallas_call | solution.py:299
  217.3 1.7 bitcast_select_fusion.2
  219.2 1.4 multiply_convert_fusion.3
  221.4 10.7 %eval_jaxpr.18 = bf16[32,24,128]{2,1,0:T(8,128)(2,1)} custom-call(bf16[32,24,128]{2,1,0:T(8,128)(2,1)} %bitcast.136), custom_call_target="tpu_custom_call" | custom-call | tf_op jit(solution)/shard_map/while/body/eval_jaxpr/pallas_call | solution.py:138
  232.1 1.6 copy.119
  233.8 1.2 reshape.155
  236.5 1.5 convolution_bitcast_fusion.4
  244.9 25.6 %eval_jaxpr.19 = (bf16[128,768]{1,0:T(8,128)(2,1)}, bf16[128,768]{1,0:T(8,128)(2,1)S(1)}) custom-call(f32[768,128]{1,0:T(8,128)} %bitcast.134, f32[128,768]{1,0:T(8,128)} %get-tuple-element.689.d_out_ref, f32[128,768]{1,0:T(8,128)} %get-tuple-element.735.conv_ref, f32[128,768]{1,0:T(8,128)} %get-tuple-element.736.values_ref, ...), custom_call_target="tpu_custom_call" | custom-call | tf_op jit(solution)/shard_map/while/body/eval_jaxpr/pallas_call | solution.py:299
  270.6 1.7 bitcast_select_fusion.2
  272.4 1.4 multiply_convert_fusion.3
  274.6 10.6 %eval_jaxpr.18 = bf16[32,24,128]{2,1,0:T(8,128)(2,1)} custom-call(bf16[32,24,128]{2,1,0:T(8,128)(2,1)} %bitcast.136), custom_call_target="tpu_custom_call" | custom-call | tf_op jit(solution)/shard_map/while/body/eval_jaxpr/pallas_call | solution.py:138
  285.2 1.6 copy.119
  289.6 1.5 convolution_bitcast_fusion.4
  298.0 23.8 %eval_jaxpr.19 = (bf16[128,768]{1,0:T(8,128)(2,1)}, bf16[128,768]{1,0:T(8,128)(2,1)S(1)}) custom-call(f32[768,128]{1,0:T(8,128)} %bitcast.134, f32[128,768]{1,0:T(8,128)} %get-tuple-element.689.d_out_ref, f32[128,768]{1,0:T(8,128)} %get-tuple-element.735.conv_ref, f32[128,768]{1,0:T(8,128)} %get-tuple-element.736.values_ref, ...), custom_call_target="tpu_custom_call" | custom-call | tf_op jit(solution)/shard_map/while/body/eval_jaxpr/pallas_call | solution.py:299
  321.8 1.7 bitcast_select_fusion.2
  323.7 1.4 multiply_convert_fusion.3
  325.9 10.6 %eval_jaxpr.18 = bf16[32,24,128]{2,1,0:T(8,128)(2,1)} custom-call(bf16[32,24,128]{2,1,0:T(8,128)(2,1)} %bitcast.136), custom_call_target="tpu_custom_call" | custom-call | tf_op jit(solution)/shard_map/while/body/eval_jaxpr/pallas_call | solution.py:138
  336.5 1.6 copy.119
  338.1 1.2 reshape.155
  340.9 1.5 convolution_bitcast_fusion.4
  349.3 23.8 %eval_jaxpr.19 = (bf16[128,768]{1,0:T(8,128)(2,1)}, bf16[128,768]{1,0:T(8,128)(2,1)S(1)}) custom-call(f32[768,128]{1,0:T(8,128)} %bitcast.134, f32[128,768]{1,0:T(8,128)} %get-tuple-element.689.d_out_ref, f32[128,768]{1,0:T(8,128)} %get-tuple-element.735.conv_ref, f32[128,768]{1,0:T(8,128)} %get-tuple-element.736.values_ref, ...), custom_call_target="tpu_custom_call" | custom-call | tf_op jit(solution)/shard_map/while/body/eval_jaxpr/pallas_call | solution.py:299
  373.1 1.7 bitcast_select_fusion.2
  374.9 1.4 multiply_convert_fusion.3
  377.2 10.6 %eval_jaxpr.18 = bf16[32,24,128]{2,1,0:T(8,128)(2,1)} custom-call(bf16[32,24,128]{2,1,0:T(8,128)(2,1)} %bitcast.136), custom_call_target="tpu_custom_call" | custom-call | tf_op jit(solution)/shard_map/while/body/eval_jaxpr/pallas_call | solution.py:138
  387.8 1.6 copy.119
  392.2 1.5 convolution_bitcast_fusion.4
  400.6 24.3 %eval_jaxpr.19 = (bf16[128,768]{1,0:T(8,128)(2,1)}, bf16[128,768]{1,0:T(8,128)(2,1)S(1)}) custom-call(f32[768,128]{1,0:T(8,128)} %bitcast.134, f32[128,768]{1,0:T(8,128)} %get-tuple-element.689.d_out_ref, f32[128,768]{1,0:T(8,128)} %get-tuple-element.735.conv_ref, f32[128,768]{1,0:T(8,128)} %get-tuple-element.736.values_ref, ...), custom_call_target="tpu_custom_call" | custom-call | tf_op jit(solution)/shard_map/while/body/eval_jaxpr/pallas_call | solution.py:299
  424.9 1.7 bitcast_select_fusion.2
  426.7 1.4 multiply_convert_fusion.3
  428.9 10.9 %eval_jaxpr.18 = bf16[32,24,128]{2,1,0:T(8,128)(2,1)} custom-call(bf16[32,24,128]{2,1,0:T(8,128)(2,1)} %bitcast.136), custom_call_target="tpu_custom_call" | custom-call | tf_op jit(solution)/shard_map/while/body/eval_jaxpr/pallas_call | solution.py:138
  439.8 1.6 copy.119
  441.5 1.2 reshape.155
  444.2 1.5 convolution_bitcast_fusion.4
  452.6 22.7 %eval_jaxpr.19 = (bf16[128,768]{1,0:T(8,128)(2,1)}, bf16[128,768]{1,0:T(8,128)(2,1)S(1)}) custom-call(f32[768,128]{1,0:T(8,128)} %bitcast.134, f32[128,768]{1,0:T(8,128)} %get-tuple-element.689.d_out_ref, f32[128,768]{1,0:T(8,128)} %get-tuple-element.735.conv_ref, f32[128,768]{1,0:T(8,128)} %get-tuple-element.736.values_ref, ...), custom_call_target="tpu_custom_call" | custom-call | tf_op jit(solution)/shard_map/while/body/eval_jaxpr/pallas_call | solution.py:299
  475.3 1.7 bitcast_select_fusion.2
  (366 shorter events, 95.4 us)
Async XLA Ops:
  0.0 18.1 %copy-start = (f32[1,768]{1,0:T(1,128)S(1)}, f32[1,768]{1,0:T(1,128)}, u32[]{:S(2)}) copy-start(f32[1,768]{1,0:T(1,128)} %param.15) | copy-start | bytes 9220
  0.8 6.5 %collective-permute-start = (bf16[2,2304]{1,0:T(2,128)(2,1)S(1)}, bf16[2,2304]{1,0:T(2,128)(2,1)S(1)}, u32[]{:S(2)}, u32[]{:S(2)}) collective-permute-start(bf16[2,2304]{1,0:T(2,128)(2,1)S(1)} %slice_bitcast_fusion), channel_id=1, source_target_pairs={{0,8},{8,16},{16,24},{24,32},{32,40},{40,48},{48,56},{56,64},{64,7... | collective-permute-start | bytes 27656 | tf_op jit(solution)/shard_map/ppermute | solution.py:17
  6.2 27.2 %copy-start.21 = (f32[32,32]{1,0:T(8,128)}, f32[32,32]{1,0:T(8,128)S(1)}, u32[]{:S(2)}) copy-start(f32[32,32]{1,0:T(8,128)S(1)} %fusion.120) | copy-start | bytes 12292
  10.9 17.3 %all-to-all-start = ((bf16[2,128,768]{1,0,2:T(2,128)(2,1)}), bf16[2,128,768]{1,0,2:T(2,128)(2,1)S(1)}, u32[]{:S(2)}, u32[]{:S(2)}) async-start(bf16[2,128,768]{1,0,2:T(2,128)(2,1)} %copy.72), calls=%async_computation | async-start | bytes 786432 | tf_op jit(solution)/shard_map/all_to_all | solution.py:367
  18.2 15.2 %copy-start.23 = (f32[32,32]{1,0:T(8,128)}, f32[32,32]{1,0:T(8,128)S(1)}, u32[]{:S(2)}) copy-start(f32[32,32]{1,0:T(8,128)S(1)} %get-tuple-element.567) | copy-start | bytes 12292
  18.2 15.2 %copy-start.25 = (f32[32,32]{1,0:T(8,128)}, f32[32,32]{1,0:T(8,128)S(1)}, u32[]{:S(2)}) copy-start(f32[32,32]{1,0:T(8,128)S(1)} %get-tuple-element.568) | copy-start | bytes 12292
  18.4 13.2 %copy-start.17 = (f32[32,256]{1,0:T(8,128)}, f32[32,256]{1,0:T(8,128)S(1)}, u32[]{:S(2)}) copy-start(f32[32,256]{1,0:T(8,128)S(1)} %get-tuple-element.565) | copy-start | bytes 98308
  18.4 13.2 %copy-start.19 = (f32[32,256]{1,0:T(8,128)}, f32[32,256]{1,0:T(8,128)S(1)}, u32[]{:S(2)}) copy-start(f32[32,256]{1,0:T(8,128)S(1)} %get-tuple-element.566) | copy-start | bytes 98308
  45.0 18.9 %copy-start.3 = (bf16[1,768,768]{2,1,0:T(8,128)(2,1)S(1)}, bf16[1,768,768]{2,1,0:T(8,128)(2,1)}, u32[]{:S(2)}) copy-start(bf16[1,768,768]{2,1,0:T(8,128)(2,1)} %param.12) | copy-start | bytes 3538948
  47.1 13.2 %all-to-all-start.1 = ((bf16[32,128,24]{1,2,0:T(8,128)(2,1)}), bf16[32,128,24]{1,2,0:T(8,128)(2,1)}, u32[]{:S(2)}, u32[]{:S(2)}) async-start(bf16[32,128,24]{1,2,0:T(8,128)(2,1)} %fusion.86), calls=%async_computation.1 | async-start | bytes 393216 | tf_op jit(solution)/shard_map/all_to_all | solution.py:372
  63.9 20.5 %copy-start.4 = (f32[24,32,256]{2,1,0:T(8,128)}, f32[24,32,256]{2,1,0:T(8,128)S(1)}, u32[]{:S(2)}) copy-start(f32[24,32,256]{2,1,0:T(8,128)S(1)} %get-tuple-element.732) | copy-start | bytes 2359300 | tf_op jit(solution)/shard_map/while
  63.9 20.5 %copy-start.6 = (f32[24,32,256]{2,1,0:T(8,128)}, f32[24,32,256]{2,1,0:T(8,128)S(1)}, u32[]{:S(2)}) copy-start(f32[24,32,256]{2,1,0:T(8,128)S(1)} %get-tuple-element.731) | copy-start | bytes 2359300 | tf_op jit(solution)/shard_map/while
  89.4 25.4 %copy-start.5 = (f32[24,32,256]{2,1,0:T(8,128)S(1)}, f32[24,32,256]{2,1,0:T(8,128)}, u32[]{:S(2)}) copy-start(f32[24,32,256]{2,1,0:T(8,128)} %copy-done.4) | copy-start | bytes 2359300 | tf_op jit(solution)/shard_map/while
  89.4 25.4 %copy-start.7 = (f32[24,32,256]{2,1,0:T(8,128)S(1)}, f32[24,32,256]{2,1,0:T(8,128)}, u32[]{:S(2)}) copy-start(f32[24,32,256]{2,1,0:T(8,128)} %copy-done.6) | copy-start | bytes 2359300 | tf_op jit(solution)/shard_map/while
  89.4 25.4 %copy-start.9 = (f32[128,768]{1,0:T(8,128)S(1)}, f32[128,768]{1,0:T(8,128)}, u32[]{:S(2)}) copy-start(f32[128,768]{1,0:T(8,128)} %copy-done.8) | copy-start | bytes 1179652 | tf_op jit(solution)/shard_map/while
  89.4 25.4 %copy-start.11 = (bf16[1,128,768]{2,1,0:T(8,128)(2,1)S(1)}, bf16[1,128,768]{2,1,0:T(8,128)(2,1)}, u32[]{:S(2)}) copy-start(bf16[1,128,768]{2,1,0:T(8,128)(2,1)} %get-tuple-element.760) | copy-start | bytes 589828 | tf_op jit(solution)/shard_map/while
  114.8 20.4 %copy-start.4 = (f32[24,32,256]{2,1,0:T(8,128)}, f32[24,32,256]{2,1,0:T(8,128)S(1)}, u32[]{:S(2)}) copy-start(f32[24,32,256]{2,1,0:T(8,128)S(1)} %get-tuple-element.732) | copy-start | bytes 2359300 | tf_op jit(solution)/shard_map/while
  114.8 20.4 %copy-start.6 = (f32[24,32,256]{2,1,0:T(8,128)}, f32[24,32,256]{2,1,0:T(8,128)S(1)}, u32[]{:S(2)}) copy-start(f32[24,32,256]{2,1,0:T(8,128)S(1)} %get-tuple-element.731) | copy-start | bytes 2359300 | tf_op jit(solution)/shard_map/while
  140.2 26.5 %copy-start.5 = (f32[24,32,256]{2,1,0:T(8,128)S(1)}, f32[24,32,256]{2,1,0:T(8,128)}, u32[]{:S(2)}) copy-start(f32[24,32,256]{2,1,0:T(8,128)} %copy-done.4) | copy-start | bytes 2359300 | tf_op jit(solution)/shard_map/while
  140.2 26.5 %copy-start.7 = (f32[24,32,256]{2,1,0:T(8,128)S(1)}, f32[24,32,256]{2,1,0:T(8,128)}, u32[]{:S(2)}) copy-start(f32[24,32,256]{2,1,0:T(8,128)} %copy-done.6) | copy-start | bytes 2359300 | tf_op jit(solution)/shard_map/while
  140.2 26.5 %copy-start.9 = (f32[128,768]{1,0:T(8,128)S(1)}, f32[128,768]{1,0:T(8,128)}, u32[]{:S(2)}) copy-start(f32[128,768]{1,0:T(8,128)} %copy-done.8) | copy-start | bytes 1179652 | tf_op jit(solution)/shard_map/while
  140.2 26.5 %copy-start.11 = (bf16[1,128,768]{2,1,0:T(8,128)(2,1)S(1)}, bf16[1,128,768]{2,1,0:T(8,128)(2,1)}, u32[]{:S(2)}) copy-start(bf16[1,128,768]{2,1,0:T(8,128)(2,1)} %get-tuple-element.760) | copy-start | bytes 589828 | tf_op jit(solution)/shard_map/while
  166.7 20.7 %copy-start.4 = (f32[24,32,256]{2,1,0:T(8,128)}, f32[24,32,256]{2,1,0:T(8,128)S(1)}, u32[]{:S(2)}) copy-start(f32[24,32,256]{2,1,0:T(8,128)S(1)} %get-tuple-element.732) | copy-start | bytes 2359300 | tf_op jit(solution)/shard_map/while
  166.8 20.7 %copy-start.6 = (f32[24,32,256]{2,1,0:T(8,128)}, f32[24,32,256]{2,1,0:T(8,128)S(1)}, u32[]{:S(2)}) copy-start(f32[24,32,256]{2,1,0:T(8,128)S(1)} %get-tuple-element.731) | copy-start | bytes 2359300 | tf_op jit(solution)/shard_map/while
  166.8 12.9 %copy-start.1 = (bf16[128,768]{1,0:T(8,128)(2,1)}, bf16[128,768]{1,0:T(8,128)(2,1)S(1)}, u32[]{:S(2)}) copy-start(bf16[128,768]{1,0:T(8,128)(2,1)S(1)} %copy.133.grad_ref) | copy-start | bytes 589828 | tf_op jit(solution)/shard_map/while
  192.4 26.7 %copy-start.5 = (f32[24,32,256]{2,1,0:T(8,128)S(1)}, f32[24,32,256]{2,1,0:T(8,128)}, u32[]{:S(2)}) copy-start(f32[24,32,256]{2,1,0:T(8,128)} %copy-done.4) | copy-start | bytes 2359300 | tf_op jit(solution)/shard_map/while
  192.4 26.7 %copy-start.7 = (f32[24,32,256]{2,1,0:T(8,128)S(1)}, f32[24,32,256]{2,1,0:T(8,128)}, u32[]{:S(2)}) copy-start(f32[24,32,256]{2,1,0:T(8,128)} %copy-done.6) | copy-start | bytes 2359300 | tf_op jit(solution)/shard_map/while
  192.4 26.7 %copy-start.9 = (f32[128,768]{1,0:T(8,128)S(1)}, f32[128,768]{1,0:T(8,128)}, u32[]{:S(2)}) copy-start(f32[128,768]{1,0:T(8,128)} %copy-done.8) | copy-start | bytes 1179652 | tf_op jit(solution)/shard_map/while
  192.4 26.7 %copy-start.11 = (bf16[1,128,768]{2,1,0:T(8,128)(2,1)S(1)}, bf16[1,128,768]{2,1,0:T(8,128)(2,1)}, u32[]{:S(2)}) copy-start(bf16[1,128,768]{2,1,0:T(8,128)(2,1)} %get-tuple-element.760) | copy-start | bytes 589828 | tf_op jit(solution)/shard_map/while
  219.1 20.8 %copy-start.4 = (f32[24,32,256]{2,1,0:T(8,128)}, f32[24,32,256]{2,1,0:T(8,128)S(1)}, u32[]{:S(2)}) copy-start(f32[24,32,256]{2,1,0:T(8,128)S(1)} %get-tuple-element.732) | copy-start | bytes 2359300 | tf_op jit(solution)/shard_map/while
  219.1 20.8 %copy-start.6 = (f32[24,32,256]{2,1,0:T(8,128)}, f32[24,32,256]{2,1,0:T(8,128)S(1)}, u32[]{:S(2)}) copy-start(f32[24,32,256]{2,1,0:T(8,128)S(1)} %get-tuple-element.731) | copy-start | bytes 2359300 | tf_op jit(solution)/shard_map/while
  219.2 13.0 %copy-start.1 = (bf16[128,768]{1,0:T(8,128)(2,1)}, bf16[128,768]{1,0:T(8,128)(2,1)S(1)}, u32[]{:S(2)}) copy-start(bf16[128,768]{1,0:T(8,128)(2,1)S(1)} %copy.133.grad_ref) | copy-start | bytes 589828 | tf_op jit(solution)/shard_map/while
  244.9 27.4 %copy-start.5 = (f32[24,32,256]{2,1,0:T(8,128)S(1)}, f32[24,32,256]{2,1,0:T(8,128)}, u32[]{:S(2)}) copy-start(f32[24,32,256]{2,1,0:T(8,128)} %copy-done.4) | copy-start | bytes 2359300 | tf_op jit(solution)/shard_map/while
  244.9 27.4 %copy-start.7 = (f32[24,32,256]{2,1,0:T(8,128)S(1)}, f32[24,32,256]{2,1,0:T(8,128)}, u32[]{:S(2)}) copy-start(f32[24,32,256]{2,1,0:T(8,128)} %copy-done.6) | copy-start | bytes 2359300 | tf_op jit(solution)/shard_map/while
  244.9 27.4 %copy-start.9 = (f32[128,768]{1,0:T(8,128)S(1)}, f32[128,768]{1,0:T(8,128)}, u32[]{:S(2)}) copy-start(f32[128,768]{1,0:T(8,128)} %copy-done.8) | copy-start | bytes 1179652 | tf_op jit(solution)/shard_map/while
  244.9 27.4 %copy-start.11 = (bf16[1,128,768]{2,1,0:T(8,128)(2,1)S(1)}, bf16[1,128,768]{2,1,0:T(8,128)(2,1)}, u32[]{:S(2)}) copy-start(bf16[1,128,768]{2,1,0:T(8,128)(2,1)} %get-tuple-element.760) | copy-start | bytes 589828 | tf_op jit(solution)/shard_map/while
  272.3 20.7 %copy-start.4 = (f32[24,32,256]{2,1,0:T(8,128)}, f32[24,32,256]{2,1,0:T(8,128)S(1)}, u32[]{:S(2)}) copy-start(f32[24,32,256]{2,1,0:T(8,128)S(1)} %get-tuple-element.732) | copy-start | bytes 2359300 | tf_op jit(solution)/shard_map/while
  272.3 20.7 %copy-start.6 = (f32[24,32,256]{2,1,0:T(8,128)}, f32[24,32,256]{2,1,0:T(8,128)S(1)}, u32[]{:S(2)}) copy-start(f32[24,32,256]{2,1,0:T(8,128)S(1)} %get-tuple-element.731) | copy-start | bytes 2359300 | tf_op jit(solution)/shard_map/while
  272.4 12.9 %copy-start.1 = (bf16[128,768]{1,0:T(8,128)(2,1)}, bf16[128,768]{1,0:T(8,128)(2,1)S(1)}, u32[]{:S(2)}) copy-start(bf16[128,768]{1,0:T(8,128)(2,1)S(1)} %copy.133.grad_ref) | copy-start | bytes 589828 | tf_op jit(solution)/shard_map/while
  298.0 25.6 %copy-start.5 = (f32[24,32,256]{2,1,0:T(8,128)S(1)}, f32[24,32,256]{2,1,0:T(8,128)}, u32[]{:S(2)}) copy-start(f32[24,32,256]{2,1,0:T(8,128)} %copy-done.4) | copy-start | bytes 2359300 | tf_op jit(solution)/shard_map/while
  298.0 25.6 %copy-start.7 = (f32[24,32,256]{2,1,0:T(8,128)S(1)}, f32[24,32,256]{2,1,0:T(8,128)}, u32[]{:S(2)}) copy-start(f32[24,32,256]{2,1,0:T(8,128)} %copy-done.6) | copy-start | bytes 2359300 | tf_op jit(solution)/shard_map/while
  298.0 25.6 %copy-start.9 = (f32[128,768]{1,0:T(8,128)S(1)}, f32[128,768]{1,0:T(8,128)}, u32[]{:S(2)}) copy-start(f32[128,768]{1,0:T(8,128)} %copy-done.8) | copy-start | bytes 1179652 | tf_op jit(solution)/shard_map/while
  298.0 25.6 %copy-start.11 = (bf16[1,128,768]{2,1,0:T(8,128)(2,1)S(1)}, bf16[1,128,768]{2,1,0:T(8,128)(2,1)}, u32[]{:S(2)}) copy-start(bf16[1,128,768]{2,1,0:T(8,128)(2,1)} %get-tuple-element.760) | copy-start | bytes 589828 | tf_op jit(solution)/shard_map/while
  323.6 20.7 %copy-start.4 = (f32[24,32,256]{2,1,0:T(8,128)}, f32[24,32,256]{2,1,0:T(8,128)S(1)}, u32[]{:S(2)}) copy-start(f32[24,32,256]{2,1,0:T(8,128)S(1)} %get-tuple-element.732) | copy-start | bytes 2359300 | tf_op jit(solution)/shard_map/while
  323.6 20.7 %copy-start.6 = (f32[24,32,256]{2,1,0:T(8,128)}, f32[24,32,256]{2,1,0:T(8,128)S(1)}, u32[]{:S(2)}) copy-start(f32[24,32,256]{2,1,0:T(8,128)S(1)} %get-tuple-element.731) | copy-start | bytes 2359300 | tf_op jit(solution)/shard_map/while
  323.6 12.9 %copy-start.1 = (bf16[128,768]{1,0:T(8,128)(2,1)}, bf16[128,768]{1,0:T(8,128)(2,1)S(1)}, u32[]{:S(2)}) copy-start(bf16[128,768]{1,0:T(8,128)(2,1)S(1)} %copy.133.grad_ref) | copy-start | bytes 589828 | tf_op jit(solution)/shard_map/while
  349.3 25.6 %copy-start.5 = (f32[24,32,256]{2,1,0:T(8,128)S(1)}, f32[24,32,256]{2,1,0:T(8,128)}, u32[]{:S(2)}) copy-start(f32[24,32,256]{2,1,0:T(8,128)} %copy-done.4) | copy-start | bytes 2359300 | tf_op jit(solution)/shard_map/while
  349.3 25.6 %copy-start.7 = (f32[24,32,256]{2,1,0:T(8,128)S(1)}, f32[24,32,256]{2,1,0:T(8,128)}, u32[]{:S(2)}) copy-start(f32[24,32,256]{2,1,0:T(8,128)} %copy-done.6) | copy-start | bytes 2359300 | tf_op jit(solution)/shard_map/while
  349.3 25.6 %copy-start.9 = (f32[128,768]{1,0:T(8,128)S(1)}, f32[128,768]{1,0:T(8,128)}, u32[]{:S(2)}) copy-start(f32[128,768]{1,0:T(8,128)} %copy-done.8) | copy-start | bytes 1179652 | tf_op jit(solution)/shard_map/while
  349.3 25.6 %copy-start.11 = (bf16[1,128,768]{2,1,0:T(8,128)(2,1)S(1)}, bf16[1,128,768]{2,1,0:T(8,128)(2,1)}, u32[]{:S(2)}) copy-start(bf16[1,128,768]{2,1,0:T(8,128)(2,1)} %get-tuple-element.760) | copy-start | bytes 589828 | tf_op jit(solution)/shard_map/while
  374.9 20.7 %copy-start.4 = (f32[24,32,256]{2,1,0:T(8,128)}, f32[24,32,256]{2,1,0:T(8,128)S(1)}, u32[]{:S(2)}) copy-start(f32[24,32,256]{2,1,0:T(8,128)S(1)} %get-tuple-element.732) | copy-start | bytes 2359300 | tf_op jit(solution)/shard_map/while
  374.9 20.7 %copy-start.6 = (f32[24,32,256]{2,1,0:T(8,128)}, f32[24,32,256]{2,1,0:T(8,128)S(1)}, u32[]{:S(2)}) copy-start(f32[24,32,256]{2,1,0:T(8,128)S(1)} %get-tuple-element.731) | copy-start | bytes 2359300 | tf_op jit(solution)/shard_map/while
  374.9 12.9 %copy-start.1 = (bf16[128,768]{1,0:T(8,128)(2,1)}, bf16[128,768]{1,0:T(8,128)(2,1)S(1)}, u32[]{:S(2)}) copy-start(bf16[128,768]{1,0:T(8,128)(2,1)S(1)} %copy.133.grad_ref) | copy-start | bytes 589828 | tf_op jit(solution)/shard_map/while
  400.6 26.0 %copy-start.5 = (f32[24,32,256]{2,1,0:T(8,128)S(1)}, f32[24,32,256]{2,1,0:T(8,128)}, u32[]{:S(2)}) copy-start(f32[24,32,256]{2,1,0:T(8,128)} %copy-done.4) | copy-start | bytes 2359300 | tf_op jit(solution)/shard_map/while
  400.6 26.0 %copy-start.7 = (f32[24,32,256]{2,1,0:T(8,128)S(1)}, f32[24,32,256]{2,1,0:T(8,128)}, u32[]{:S(2)}) copy-start(f32[24,32,256]{2,1,0:T(8,128)} %copy-done.6) | copy-start | bytes 2359300 | tf_op jit(solution)/shard_map/while
  400.6 26.0 %copy-start.9 = (f32[128,768]{1,0:T(8,128)S(1)}, f32[128,768]{1,0:T(8,128)}, u32[]{:S(2)}) copy-start(f32[128,768]{1,0:T(8,128)} %copy-done.8) | copy-start | bytes 1179652 | tf_op jit(solution)/shard_map/while
  400.6 26.1 %copy-start.11 = (bf16[1,128,768]{2,1,0:T(8,128)(2,1)S(1)}, bf16[1,128,768]{2,1,0:T(8,128)(2,1)}, u32[]{:S(2)}) copy-start(bf16[1,128,768]{2,1,0:T(8,128)(2,1)} %get-tuple-element.760) | copy-start | bytes 589828 | tf_op jit(solution)/shard_map/while
  426.6 21.0 %copy-start.4 = (f32[24,32,256]{2,1,0:T(8,128)}, f32[24,32,256]{2,1,0:T(8,128)S(1)}, u32[]{:S(2)}) copy-start(f32[24,32,256]{2,1,0:T(8,128)S(1)} %get-tuple-element.732) | copy-start | bytes 2359300 | tf_op jit(solution)/shard_map/while
  426.6 21.0 %copy-start.6 = (f32[24,32,256]{2,1,0:T(8,128)}, f32[24,32,256]{2,1,0:T(8,128)S(1)}, u32[]{:S(2)}) copy-start(f32[24,32,256]{2,1,0:T(8,128)S(1)} %get-tuple-element.731) | copy-start | bytes 2359300 | tf_op jit(solution)/shard_map/while
  426.7 13.1 %copy-start.1 = (bf16[128,768]{1,0:T(8,128)(2,1)}, bf16[128,768]{1,0:T(8,128)(2,1)S(1)}, u32[]{:S(2)}) copy-start(bf16[128,768]{1,0:T(8,128)(2,1)S(1)} %copy.133.grad_ref) | copy-start | bytes 589828 | tf_op jit(solution)/shard_map/while
  452.6 24.4 %copy-start.5 = (f32[24,32,256]{2,1,0:T(8,128)S(1)}, f32[24,32,256]{2,1,0:T(8,128)}, u32[]{:S(2)}) copy-start(f32[24,32,256]{2,1,0:T(8,128)} %copy-done.4) | copy-start | bytes 2359300 | tf_op jit(solution)/shard_map/while
  452.6 24.4 %copy-start.7 = (f32[24,32,256]{2,1,0:T(8,128)S(1)}, f32[24,32,256]{2,1,0:T(8,128)}, u32[]{:S(2)}) copy-start(f32[24,32,256]{2,1,0:T(8,128)} %copy-done.6) | copy-start | bytes 2359300 | tf_op jit(solution)/shard_map/while
  452.6 24.4 %copy-start.9 = (f32[128,768]{1,0:T(8,128)S(1)}, f32[128,768]{1,0:T(8,128)}, u32[]{:S(2)}) copy-start(f32[128,768]{1,0:T(8,128)} %copy-done.8) | copy-start | bytes 1179652 | tf_op jit(solution)/shard_map/while
  452.6 24.4 %copy-start.11 = (bf16[1,128,768]{2,1,0:T(8,128)(2,1)S(1)}, bf16[1,128,768]{2,1,0:T(8,128)(2,1)}, u32[]{:S(2)}) copy-start(bf16[1,128,768]{2,1,0:T(8,128)(2,1)} %get-tuple-element.760) | copy-start | bytes 589828 | tf_op jit(solution)/shard_map/while
  (30 other events, 101.3 us)

commit v6 on v5

--- a/solution.py
+++ b/solution.py
@@ -24,19 +24,10 @@
     return (jnp.cos(angle), jnp.sin(angle))
 
 
-def forward_spectrum(series, inner):
-    length, chans = series.shape
+def spectrum_tables(length, inner):
     outer = 2 * length // inner
-    blocks = series.reshape(length // inner, inner, chans)
     cos_outer, sin_outer = phase_table(outer, length // inner, outer)
-    one = jnp.einsum(
-        "kn,nbc->cbk", jnp.concatenate([cos_outer, -sin_outer], axis=0), blocks, precision=accuracy
-    )
-    real_one = one[:, :, :outer]
-    imag_one = one[:, :, outer:]
     cos_twist, sin_twist = phase_table(inner, outer, 2 * length)
-    real_two = real_one * cos_twist + imag_one * sin_twist
-    imag_two = imag_one * cos_twist - real_one * sin_twist
     cos_inner, sin_inner = phase_table(inner, inner, inner)
     mixer = jnp.concatenate(
         [
@@ -45,44 +36,55 @@
         ],
         axis=0,
     )
+    return {
+        "outer": jnp.concatenate([cos_outer, -sin_outer], axis=0),
+        "twist": (cos_twist, sin_twist),
+        "forward": mixer,
+        "inverse": mixer,
+    }
+
+
+def forward_blocks(blocks, tables):
+    count, chans, inner = blocks.shape
+    outer = 2 * count
+    one = jnp.einsum("kn,ncb->cbk", tables["outer"], blocks, precision=accuracy)
+    real_one = one[:, :, :outer]
+    imag_one = one[:, :, outer:]
+    cos_twist, sin_twist = tables["twist"]
+    real_two = real_one * cos_twist + imag_one * sin_twist
+    imag_two = imag_one * cos_twist - real_one * sin_twist
     both = jnp.einsum(
-        "jb,cbk->cjk", mixer, jnp.concatenate([real_two, imag_two], axis=1), precision=accuracy
+        "jb,cbk->cjk",
+        tables["forward"],
+        jnp.concatenate([real_two, imag_two], axis=1),
+        precision=accuracy,
     )
     return (both[:, :inner], both[:, inner:])
 
 
-def inverse_spectrum(real, imag, inner):
-    chans, _, outer = real.shape
+def inverse_blocks(real, imag, tables):
+    chans, inner, outer = real.shape
     length = outer * inner // 2
-    cos_inner, sin_inner = phase_table(inner, inner, inner)
-    mixer = jnp.concatenate(
-        [
-            jnp.concatenate([cos_inner, -sin_inner], axis=1),
-            jnp.concatenate([sin_inner, cos_inner], axis=1),
-        ],
-        axis=0,
-    )
     both = jnp.einsum(
-        "jb,cjk->cbk", mixer.T, jnp.concatenate([real, imag], axis=1), precision=accuracy
+        "jb,cjk->cbk", tables["inverse"], jnp.concatenate([real, imag], axis=1), precision=accuracy
     )
     real_one = both[:, :inner]
     imag_one = both[:, inner:]
-    cos_twist, sin_twist = phase_table(inner, outer, 2 * length)
+    cos_twist, sin_twist = tables["twist"]
     real_two = real_one * cos_twist - imag_one * sin_twist
     imag_two = imag_one * cos_twist + real_one * sin_twist
-    cos_outer, sin_outer = phase_table(outer, length // inner, outer)
     series = jnp.einsum(
-        "kn,cbk->nbc",
-        jnp.concatenate([cos_outer, -sin_outer], axis=0),
+        "kn,cbk->ncb",
+        tables["outer"],
         jnp.concatenate([real_two, imag_two], axis=2),
         precision=accuracy,
     )
-    return series.reshape(length, chans) / (2.0 * length)
-
-
-def channel_conv(series, spectrum, bias_part, adjoint, inner):
-    values = series.astype(jnp.float32)
-    real, imag = forward_spectrum(values, inner)
+    return series / (2.0 * length)
+
+
+def channel_conv(blocks, spectrum, bias_part, adjoint, tables):
+    values = blocks.astype(jnp.float32)
+    real, imag = forward_blocks(values, tables)
     filter_real, filter_imag = spectrum
     if adjoint:
         prod_real = real * filter_real + imag * filter_imag
@@ -90,7 +92,8 @@
     else:
         prod_real = real * filter_real - imag * filter_imag
         prod_imag = real * filter_imag + imag * filter_real
-    return (inverse_spectrum(prod_real, prod_imag, inner) + bias_part * values).astype(jnp.bfloat16)
+    direct = bias_part[None, :, None] * values
+    return (inverse_blocks(prod_real, prod_imag, tables) + direct).astype(jnp.bfloat16)
 
 
 def exchange_kernel(x_ref, o_ref, landed, send_sems, recv_sems):
@@ -336,7 +339,7 @@
     height = projected.shape[2]
     width = w_out.shape[2]
     length = height * seq_count
-    inner = math.gcd(length, 32)
+    tables = spectrum_tables(length, height)
     chans = width // seq_count
     bias_part = lax.dynamic_slice_in_dim(filter_bias[0], seq_place * chans, chans, 0)
     weight_in = w_in[0]
@@ -346,11 +349,14 @@
 
     held = {}
 
-    def causal(series):
-        return channel_conv(series, held["spectrum"], bias_part, False, inner)
-
-    def adjoint(series):
-        return channel_conv(series, held["spectrum"], bias_part, True, inner)
+    def causal(blocks):
+        return channel_conv(blocks, held["spectrum"], bias_part, False, tables)
+
+    def adjoint(blocks):
+        return channel_conv(blocks, held["spectrum"], bias_part, True, tables)
+
+    def to_blocks(series):
+        return series.reshape(seq_count, height, chans).transpose(0, 2, 1)
 
     forward = []
     for slot in range(micro):
@@ -365,11 +371,12 @@
         if slot == 0:
             both = jnp.stack([long_filter[0].astype(jnp.bfloat16), product])
             both = lax.all_to_all(both, "seq", split_axis=2, concat_axis=1, tiled=True)
-            held["spectrum"] = forward_spectrum(both[0].astype(jnp.float32), inner)
+            held["spectrum"] = forward_blocks(to_blocks(both[0].astype(jnp.float32)), tables)
             product_local = both[1]
         else:
             product_local = lax.all_to_all(product, "seq", split_axis=1, concat_axis=0, tiled=True)
-        conv = lax.all_to_all(causal(product_local), "seq", split_axis=0, concat_axis=1, tiled=True)
+        conv_local = causal(to_blocks(product_local)).transpose(0, 2, 1).reshape(length, chans)
+        conv = lax.all_to_all(conv_local, "seq", split_axis=0, concat_axis=1, tiled=True)
         forward.append((query, keys, values, conv.astype(jnp.float32)))
 
     def stage(grad_out, top, slot):
@@ -377,10 +384,8 @@
         d_out = lax.dot_general(grad_out, weight_out, contract, preferred_element_type=jnp.float32)
         d_conv = (d_out * query).astype(jnp.bfloat16)
         sent = seq_exchange(d_conv.reshape(height, seq_count, chans).transpose(1, 2, 0))
-        d_conv_local = sent.transpose(0, 2, 1).reshape(length, chans)
-        d_prod_local = adjoint(d_conv_local)
-        sent_back = d_prod_local.reshape(seq_count, height, chans).transpose(0, 2, 1)
-        sent_back = sent_back.reshape(seq_count * chans, height).astype(jnp.float32)
+        d_prod_blocks = adjoint(sent)
+        sent_back = d_prod_blocks.reshape(seq_count * chans, height).astype(jnp.float32)
         return exchange_and_finish(
             sent_back, d_out, conv_wide, values, keys, grad_out, taps, weight_in, top
         )

time: 479 us -> 446 us (0.931)
  local copies, waits for them, and re-layouts: 67.2 us -> 49.7 us
  Pallas kernels: 278 us -> 269 us
    while x152 -> x104, local copies, waits for them, and re-layouts: 0.71 us -> 26.6 us
    reshape x20 -> x0, local copies, waits for them, and re-layouts: 19.1 us -> none  [forward_spectrum(): blocks = series.reshape(length // inner, inner, chans)]
    transpose x8 -> x0, local copies, waits for them, and re-layouts: 13.1 us -> none  [stage(): d_conv_local = sent.transpose(0, 2, 1).reshape(length, chans)]
    div x18 -> x0, local copies, waits for them, and re-layouts: 12.2 us -> none  [inverse_spectrum(): return series.reshape(length, chans) / (2.0 * length)]
    dot_general x8, matrix products: 11.3 us -> 21.7 us  [stage(): lax.dot_general(grad_out, weight_out, contract, preferred_element_type=jn...]
    pallas_call x8, Pallas kernels: 194 us -> 184 us  [exchange_and_finish(): pl.pallas_call(finish_kernel, out_shape=(jax.ShapeDtypeStruct(grad_out.sh...]
    dot_general x9 -> x0, local copies, waits for them, and re-layouts: 8.24 us -> none  [inverse_spectrum(): jnp.einsum('jb,cjk->cbk', mixer.T, jnp.concatenate([real, imag], axis=1),...]
    convert_element_type x8, local copies, waits for them, and re-layouts: 6.52 us -> 14 us  [stage(): d_conv = (d_out * query).astype(jnp.bfloat16)]
  transfers between devices with their start and end apart: 3 -> 3, of which waited for: 2 -> 2; matrix products, arithmetic and copies ran while one was open for 1% -> 2% of each run, Pallas kernels for 0% -> 0%
where the time goes in v6:
time: 446 us; the launch traced here: 443 us
  Pallas kernels  269 us (60%)
  matrix products  55 us (12%)
  local copies, waits for them, and re-layouts  49.7 us (11%)
  other arithmetic  39.7 us (9%)
  starting transfers between devices  16.1 us (4%)
  waiting for transfers between devices  13.1 us (3%)
    pallas_call x8, Pallas kernels, exchange_and_finish(): pl.pallas_call(finish_kernel, out_shape=(jax.ShapeDtypeStruct(grad_out.sh...  184 us
    pallas_call x8, Pallas kernels, seq_exchange(): pl.pallas_call(exchange_kernel, out_shape=jax.ShapeDtypeStruct(blocks.sha...  84.8 us
    while x104, local copies, waits for them, and re-layouts  26.6 us
    dot_general x8, matrix products, stage(): lax.dot_general(grad_out, weight_out, contract, preferred_element_type=jn...  21.7 us
    convert_element_type x8, local copies, waits for them, and re-layouts, stage(): d_conv = (d_out * query).astype(jnp.bfloat16)  14 us
    select_n x8, other arithmetic, tick(): jnp.where(active, lax.dynamic_update_index_in_dim(grads, d_input, slot, 0...  13.7 us
    dot_general x10, matrix products, forward_blocks(): one = jnp.einsum('kn,ncb->cbk', tables['outer'], blocks, precision=accuracy)  13.6 us
    all_to_all x1, waiting for transfers between devices, shards(): both = lax.all_to_all(both, 'seq', split_axis=2, concat_axis=1, tiled=True)  9.36 us
  transfers between devices with their start and end apart: 3, of which 2 were waited for; matrix products, arithmetic and copies ran while one was open for 2% of the time, Pallas kernels for 0%

profile of v6, /device:TPU:1, one launch (start us, length us, event | category | flops | bytes accessed | tf_op | source)
XLA Modules:
  0.0 443.5 jit_solution(4915826831680315625)
XLA Ops:
  0.8 4.5 %collective-permute-start = (bf16[2,2304]{1,0:T(2,128)(2,1)S(1)}, bf16[2,2304]{1,0:T(2,128)(2,1)S(1)}, u32[]{:S(2)}, u32[]{:S(2)}) collective-permute-start(bf16[2,2304]{1,0:T(2,128)(2,1)S(1)} %slice_bitcast_fusion.2), channel_id=1, source_target_pairs={{0,8},{8,16},{16,24},{24,32},{32,40},{40,48},{48,56},{56,64},{64,7... | collective-permute-start | bytes 27656 | tf_op jit(solution)/shard_map/ppermute | solution.py:17
  6.3 1.0 convert_element_type.126
  7.3 1.2 maximum_convert_fusion
  8.9 1.1 fusion.118
  10.0 1.1 copy.46
  11.1 7.0 %all-to-all-start = ((bf16[2,128,768]{1,0,2:T(2,128)(2,1)}), bf16[2,128,768]{1,0,2:T(2,128)(2,1)S(1)}, u32[]{:S(2)}, u32[]{:S(2)}) async-start(bf16[2,128,768]{1,0,2:T(2,128)(2,1)} %copy.46), calls=%async_computation | async-start | bytes 786432 | tf_op jit(solution)/shard_map/all_to_all | solution.py:373
  19.0 9.4 %all-to-all-done = bf16[2,128,768]{1,0,2:T(2,128)(2,1)S(1)} async-done(((bf16[2,128,768]{1,0,2:T(2,128)(2,1)}), bf16[2,128,768]{1,0,2:T(2,128)(2,1)S(1)}, u32[]{:S(2)}, u32[]{:S(2)}) %all-to-all-start) | async-done | bytes 393248 | tf_op jit(solution)/shard_map/all_to_all | solution.py:373
  32.0 1.4 multiply_subtract_fusion.4
  36.3 4.5 %all-to-all-start.1 = ((bf16[32,128,24]{1,2,0:T(8,128)(2,1)}), bf16[32,128,24]{1,2,0:T(8,128)(2,1)}, u32[]{:S(2)}, u32[]{:S(2)}) async-start(bf16[32,128,24]{1,2,0:T(8,128)(2,1)} %copy.50), calls=%async_computation.1 | async-start | bytes 393216 | tf_op jit(solution)/shard_map/all_to_all | solution.py:379
  40.8 1.4 copy.65
  42.2 1.6 copy.73
  43.8 1.7 maximum_maximum_fusion
  45.5 3.7 all-to-all-done.1
  49.2 1.7 convert_element_type.140
  50.9 1.9 copy.51
  52.9 390.6 %while.19 = (s32[]{:T(128)}, bf16[128,768]{1,0:T(8,128)(2,1)}, bf16[1,128,768]{2,1,0:T(8,128)(2,1)}, bf16[768,768]{1,0:T(8,128)(2,1)}, f32[128,768]{1,0:T(8,128)...) while((s32[]{:T(128)}, bf16[128,768]{1,0:T(8,128)(2,1)}, ...), condition=%wide.region_1.2_spmd.clone.clone, body=%wide.region_0.1_spmd.clone.clone.sunk | while | flops 1515765760 | bytes 35881440 | solution.py:413
  54.5 2.7 multiply_convert_fusion.3
  57.2 1.8 copy.71
  58.9 10.4 %eval_jaxpr.14 = bf16[32,24,128]{2,1,0:T(8,128)(2,1)} custom-call(bf16[32,24,128]{2,1,0:T(8,128)(2,1)} %bitcast.115), custom_call_target="tpu_custom_call" | custom-call | tf_op jit(solution)/shard_map/while/body/eval_jaxpr/pallas_call | solution.py:141
  69.3 1.5 fusion.147
  76.8 22.5 %eval_jaxpr.15 = (bf16[128,768]{1,0:T(8,128)(2,1)}, bf16[128,768]{1,0:T(8,128)(2,1)}) custom-call(f32[768,128]{1,0:T(8,128)} %bitcast_convert_fusion.2.sent_ref, f32[128,768]{1,0:T(8,128)} %get-tuple-element.794.d_out_ref, f32[128,768]{1,0:T(8,128)} %get-tuple-element.846.conv_ref, f32[128,768]{1,0:T(8,128)} %get-tuple-element.847.values_ref, ...), custom_call_target="tpu_custom_call" | custom-call | tf_op jit(solution)/shard_map/while/body/eval_jaxpr/pallas_call | solution.py:302
  99.3 1.6 bitcast_select_fusion.2
  102.5 2.7 multiply_convert_fusion.3
  105.2 1.8 copy.71
  107.0 10.4 %eval_jaxpr.14 = bf16[32,24,128]{2,1,0:T(8,128)(2,1)} custom-call(bf16[32,24,128]{2,1,0:T(8,128)(2,1)} %bitcast.115), custom_call_target="tpu_custom_call" | custom-call | tf_op jit(solution)/shard_map/while/body/eval_jaxpr/pallas_call | solution.py:141
  117.3 1.5 fusion.147
  124.8 23.5 %eval_jaxpr.15 = (bf16[128,768]{1,0:T(8,128)(2,1)}, bf16[128,768]{1,0:T(8,128)(2,1)}) custom-call(f32[768,128]{1,0:T(8,128)} %bitcast_convert_fusion.2.sent_ref, f32[128,768]{1,0:T(8,128)} %get-tuple-element.794.d_out_ref, f32[128,768]{1,0:T(8,128)} %get-tuple-element.846.conv_ref, f32[128,768]{1,0:T(8,128)} %get-tuple-element.847.values_ref, ...), custom_call_target="tpu_custom_call" | custom-call | tf_op jit(solution)/shard_map/while/body/eval_jaxpr/pallas_call | solution.py:302
  148.3 1.7 bitcast_select_fusion.2
  151.7 2.7 multiply_convert_fusion.3
  154.4 1.8 copy.71
  156.1 10.6 %eval_jaxpr.14 = bf16[32,24,128]{2,1,0:T(8,128)(2,1)} custom-call(bf16[32,24,128]{2,1,0:T(8,128)(2,1)} %bitcast.115), custom_call_target="tpu_custom_call" | custom-call | tf_op jit(solution)/shard_map/while/body/eval_jaxpr/pallas_call | solution.py:141
  166.8 1.5 fusion.147
  174.2 23.7 %eval_jaxpr.15 = (bf16[128,768]{1,0:T(8,128)(2,1)}, bf16[128,768]{1,0:T(8,128)(2,1)}) custom-call(f32[768,128]{1,0:T(8,128)} %bitcast_convert_fusion.2.sent_ref, f32[128,768]{1,0:T(8,128)} %get-tuple-element.794.d_out_ref, f32[128,768]{1,0:T(8,128)} %get-tuple-element.846.conv_ref, f32[128,768]{1,0:T(8,128)} %get-tuple-element.847.values_ref, ...), custom_call_target="tpu_custom_call" | custom-call | tf_op jit(solution)/shard_map/while/body/eval_jaxpr/pallas_call | solution.py:302
  197.9 1.7 bitcast_select_fusion.2
  201.2 2.7 multiply_convert_fusion.3
  203.9 1.8 copy.71
  205.7 10.7 %eval_jaxpr.14 = bf16[32,24,128]{2,1,0:T(8,128)(2,1)} custom-call(bf16[32,24,128]{2,1,0:T(8,128)(2,1)} %bitcast.115), custom_call_target="tpu_custom_call" | custom-call | tf_op jit(solution)/shard_map/while/body/eval_jaxpr/pallas_call | solution.py:141
  216.4 1.5 fusion.147
  223.8 24.4 %eval_jaxpr.15 = (bf16[128,768]{1,0:T(8,128)(2,1)}, bf16[128,768]{1,0:T(8,128)(2,1)}) custom-call(f32[768,128]{1,0:T(8,128)} %bitcast_convert_fusion.2.sent_ref, f32[128,768]{1,0:T(8,128)} %get-tuple-element.794.d_out_ref, f32[128,768]{1,0:T(8,128)} %get-tuple-element.846.conv_ref, f32[128,768]{1,0:T(8,128)} %get-tuple-element.847.values_ref, ...), custom_call_target="tpu_custom_call" | custom-call | tf_op jit(solution)/shard_map/while/body/eval_jaxpr/pallas_call | solution.py:302
  248.3 1.7 bitcast_select_fusion.2
  251.6 2.7 multiply_convert_fusion.3
  254.3 1.8 copy.71
  256.1 10.6 %eval_jaxpr.14 = bf16[32,24,128]{2,1,0:T(8,128)(2,1)} custom-call(bf16[32,24,128]{2,1,0:T(8,128)(2,1)} %bitcast.115), custom_call_target="tpu_custom_call" | custom-call | tf_op jit(solution)/shard_map/while/body/eval_jaxpr/pallas_call | solution.py:141
  266.7 1.5 fusion.147
  274.1 22.6 %eval_jaxpr.15 = (bf16[128,768]{1,0:T(8,128)(2,1)}, bf16[128,768]{1,0:T(8,128)(2,1)}) custom-call(f32[768,128]{1,0:T(8,128)} %bitcast_convert_fusion.2.sent_ref, f32[128,768]{1,0:T(8,128)} %get-tuple-element.794.d_out_ref, f32[128,768]{1,0:T(8,128)} %get-tuple-element.846.conv_ref, f32[128,768]{1,0:T(8,128)} %get-tuple-element.847.values_ref, ...), custom_call_target="tpu_custom_call" | custom-call | tf_op jit(solution)/shard_map/while/body/eval_jaxpr/pallas_call | solution.py:302
  296.7 1.7 bitcast_select_fusion.2
  300.1 2.7 multiply_convert_fusion.3
  302.8 1.8 copy.71
  304.5 10.6 %eval_jaxpr.14 = bf16[32,24,128]{2,1,0:T(8,128)(2,1)} custom-call(bf16[32,24,128]{2,1,0:T(8,128)(2,1)} %bitcast.115), custom_call_target="tpu_custom_call" | custom-call | tf_op jit(solution)/shard_map/while/body/eval_jaxpr/pallas_call | solution.py:141
  315.1 1.5 fusion.147
  322.6 22.6 %eval_jaxpr.15 = (bf16[128,768]{1,0:T(8,128)(2,1)}, bf16[128,768]{1,0:T(8,128)(2,1)}) custom-call(f32[768,128]{1,0:T(8,128)} %bitcast_convert_fusion.2.sent_ref, f32[128,768]{1,0:T(8,128)} %get-tuple-element.794.d_out_ref, f32[128,768]{1,0:T(8,128)} %get-tuple-element.846.conv_ref, f32[128,768]{1,0:T(8,128)} %get-tuple-element.847.values_ref, ...), custom_call_target="tpu_custom_call" | custom-call | tf_op jit(solution)/shard_map/while/body/eval_jaxpr/pallas_call | solution.py:302
  345.2 1.7 bitcast_select_fusion.2
  348.6 2.7 multiply_convert_fusion.3
  351.3 1.8 copy.71
  353.0 10.6 %eval_jaxpr.14 = bf16[32,24,128]{2,1,0:T(8,128)(2,1)} custom-call(bf16[32,24,128]{2,1,0:T(8,128)(2,1)} %bitcast.115), custom_call_target="tpu_custom_call" | custom-call | tf_op jit(solution)/shard_map/while/body/eval_jaxpr/pallas_call | solution.py:141
  363.6 1.5 fusion.147
  371.1 23.1 %eval_jaxpr.15 = (bf16[128,768]{1,0:T(8,128)(2,1)}, bf16[128,768]{1,0:T(8,128)(2,1)}) custom-call(f32[768,128]{1,0:T(8,128)} %bitcast_convert_fusion.2.sent_ref, f32[128,768]{1,0:T(8,128)} %get-tuple-element.794.d_out_ref, f32[128,768]{1,0:T(8,128)} %get-tuple-element.846.conv_ref, f32[128,768]{1,0:T(8,128)} %get-tuple-element.847.values_ref, ...), custom_call_target="tpu_custom_call" | custom-call | tf_op jit(solution)/shard_map/while/body/eval_jaxpr/pallas_call | solution.py:302
  394.2 1.7 bitcast_select_fusion.2
  397.5 2.7 multiply_convert_fusion.3
  400.2 1.8 copy.71
  401.9 10.9 %eval_jaxpr.14 = bf16[32,24,128]{2,1,0:T(8,128)(2,1)} custom-call(bf16[32,24,128]{2,1,0:T(8,128)(2,1)} %bitcast.115), custom_call_target="tpu_custom_call" | custom-call | tf_op jit(solution)/shard_map/while/body/eval_jaxpr/pallas_call | solution.py:141
  412.9 1.5 fusion.147
  420.3 21.4 %eval_jaxpr.15 = (bf16[128,768]{1,0:T(8,128)(2,1)}, bf16[128,768]{1,0:T(8,128)(2,1)}) custom-call(f32[768,128]{1,0:T(8,128)} %bitcast_convert_fusion.2.sent_ref, f32[128,768]{1,0:T(8,128)} %get-tuple-element.794.d_out_ref, f32[128,768]{1,0:T(8,128)} %get-tuple-element.846.conv_ref, f32[128,768]{1,0:T(8,128)} %get-tuple-element.847.values_ref, ...), custom_call_target="tpu_custom_call" | custom-call | tf_op jit(solution)/shard_map/while/body/eval_jaxpr/pallas_call | solution.py:302
  441.7 1.7 bitcast_select_fusion.2
  (212 shorter events, 68.6 us)
Async XLA Ops:
  0.0 18.1 %copy-start = (f32[1,768]{1,0:T(1,128)S(1)}, f32[1,768]{1,0:T(1,128)}, u32[]{:S(2)}) copy-start(f32[1,768]{1,0:T(1,128)} %param.15) | copy-start | bytes 9220
  0.8 6.5 %collective-permute-start = (bf16[2,2304]{1,0:T(2,128)(2,1)S(1)}, bf16[2,2304]{1,0:T(2,128)(2,1)S(1)}, u32[]{:S(2)}, u32[]{:S(2)}) collective-permute-start(bf16[2,2304]{1,0:T(2,128)(2,1)S(1)} %slice_bitcast_fusion.2), channel_id=1, source_target_pairs={{0,8},{8,16},{16,24},{24,32},{32,40},{40,48},{48,56},{56,64},{64,7... | collective-permute-start | bytes 27656 | tf_op jit(solution)/shard_map/ppermute | solution.py:17
  6.3 22.7 %copy-start.7 = (f32[128,32]{0,1:T(8,128)}, f32[128,32]{0,1:T(8,128)S(1)}, u32[]{:S(2)}) copy-start(f32[128,32]{0,1:T(8,128)S(1)} %pad_maximum_fusion.1) | copy-start | bytes 49156
  11.1 17.2 %all-to-all-start = ((bf16[2,128,768]{1,0,2:T(2,128)(2,1)}), bf16[2,128,768]{1,0,2:T(2,128)(2,1)S(1)}, u32[]{:S(2)}, u32[]{:S(2)}) async-start(bf16[2,128,768]{1,0,2:T(2,128)(2,1)} %copy.46), calls=%async_computation | async-start | bytes 786432 | tf_op jit(solution)/shard_map/all_to_all | solution.py:373
  18.6 14.8 %copy-start.10 = (f32[128,128]{1,0:T(8,128)}, f32[128,128]{1,0:T(8,128)S(1)}, u32[]{:S(2)}) copy-start(f32[128,128]{1,0:T(8,128)S(1)} %fusion.101) | copy-start | bytes 196612
  18.9 14.5 %copy-start.11 = (f32[128,128]{1,0:T(8,128)}, f32[128,128]{1,0:T(8,128)S(1)}, u32[]{:S(2)}) copy-start(f32[128,128]{1,0:T(8,128)S(1)} %get-tuple-element.666) | copy-start | bytes 196612
  18.9 14.5 %copy-start.12 = (f32[128,128]{1,0:T(8,128)}, f32[128,128]{1,0:T(8,128)S(1)}, u32[]{:S(2)}) copy-start(f32[128,128]{1,0:T(8,128)S(1)} %get-tuple-element.667) | copy-start | bytes 196612
  34.3 0.7 copy-start.8
  35.0 17.9 %copy-start.1 = (bf16[1,768,2304]{2,1,0:T(8,128)(2,1)S(1)}, bf16[1,768,2304]{2,1,0:T(8,128)(2,1)}, u32[]{:S(2)}) copy-start(bf16[1,768,2304]{2,1,0:T(8,128)(2,1)} %param.11) | copy-start | bytes 10616836
  36.3 13.0 %all-to-all-start.1 = ((bf16[32,128,24]{1,2,0:T(8,128)(2,1)}), bf16[32,128,24]{1,2,0:T(8,128)(2,1)}, u32[]{:S(2)}, u32[]{:S(2)}) async-start(bf16[32,128,24]{1,2,0:T(8,128)(2,1)} %copy.50), calls=%async_computation.1 | async-start | bytes 393216 | tf_op jit(solution)/shard_map/all_to_all | solution.py:379
  53.8 0.7 copy-start.2
  71.0 1.0 copy-start.4
  72.0 1.1 copy-start.5
  72.0 1.4 copy-start.6
  74.5 0.7 copy-start.9
  74.8 1.0 copy-start.3
  101.8 0.7 copy-start.2
  119.0 1.0 copy-start.4
  120.0 1.1 copy-start.5
  120.0 1.4 copy-start.6
  122.5 0.7 copy-start.9
  122.7 1.0 copy-start.3
  151.0 0.7 copy-start.2
  168.5 1.0 copy-start.4
  169.4 1.1 copy-start.5
  169.4 1.4 copy-start.6
  171.9 0.7 copy-start.9
  172.2 1.0 copy-start.3
  200.5 0.7 copy-start.2
  218.1 1.0 copy-start.4
  219.1 1.1 copy-start.5
  219.1 1.4 copy-start.6
  221.6 0.7 copy-start.9
  221.8 1.0 copy-start.3
  250.9 0.7 copy-start.2
  268.4 1.0 copy-start.4
  269.3 1.1 copy-start.5
  269.3 1.4 copy-start.6
  271.8 0.7 copy-start.9
  272.1 1.0 copy-start.3
  299.4 0.7 copy-start.2
  316.8 1.0 copy-start.4
  317.8 1.1 copy-start.5
  317.8 1.4 copy-start.6
  320.3 0.7 copy-start.9
  320.5 1.0 copy-start.3
  347.9 0.7 copy-start.2
  365.3 1.0 copy-start.4
  366.3 1.1 copy-start.5
  366.3 1.4 copy-start.6
  368.8 0.7 copy-start.9
  369.0 1.0 copy-start.3
  396.8 0.7 copy-start.2
  414.6 1.0 copy-start.4
  415.5 1.1 copy-start.5
  415.5 1.4 copy-start.6
  418.0 0.7 copy-start.9
  418.3 1.0 copy-start.3

commit v7 on v6

--- a/solution.py
+++ b/solution.py
@@ -96,8 +96,9 @@
     return (inverse_blocks(prod_real, prod_imag, tables) + direct).astype(jnp.bfloat16)
 
 
-def exchange_kernel(x_ref, o_ref, landed, send_sems, recv_sems):
-    count = x_ref.shape[0]
+def begin_kernel(grad_ref, weight_ref, query_ref, d_out_ref, o_ref, outgoing, landed, send_sems, recv_sems):
+    count = lax.axis_size("seq")
+    chans = o_ref.shape[0] // count
     me = lax.axis_index("seq")
     section = lax.axis_index("section")
     mesh_ids = pl.DeviceIdType.MESH
@@ -109,13 +110,19 @@
         return 0
 
     lax.fori_loop(1, count, greet, 0)
+    d_out = lax.dot_general(
+        grad_ref[...], weight_ref[...], (((1,), (1,)), ((), ())), preferred_element_type=jnp.float32
+    )
+    d_out_ref[...] = d_out
+    d_conv = (d_out * query_ref[...]).astype(jnp.bfloat16).astype(jnp.float32)
+    outgoing[...] = d_conv.T
     pl.semaphore_wait(barrier, count - 1)
 
     def describe(k):
         peer = lax.rem(me + k, count)
         return pltpu.make_async_remote_copy(
-            src_ref=x_ref.at[peer],
-            dst_ref=landed.at[me],
+            src_ref=outgoing.at[pl.ds(pl.multiple_of(peer * chans, 8), chans)],
+            dst_ref=landed.at[pl.ds(pl.multiple_of(me * chans, 8), chans)],
             send_sem=send_sems.at[k],
             recv_sem=recv_sems.at[k],
             device_id=(peer, section),
@@ -131,25 +138,33 @@
         return 0
 
     lax.fori_loop(1, count, send, 0)
+    own = pl.ds(pl.multiple_of(me * chans, 8), chans)
+    landed[own] = outgoing[own]
     lax.fori_loop(1, count, finish, 0)
     o_ref[...] = landed[...]
-    o_ref[pl.ds(me, 1)] = x_ref[pl.ds(me, 1)]
-
-
-def seq_exchange(blocks):
-    count = blocks.shape[0]
+
+
+def project_and_exchange(grad_out, weight_out, query):
+    count = lax.axis_size("seq")
+    rows, width = query.shape
+    vmem = pl.BlockSpec(memory_space=pltpu.VMEM)
+    block = (width, rows)
     return pl.pallas_call(
-        exchange_kernel,
-        out_shape=jax.ShapeDtypeStruct(blocks.shape, blocks.dtype),
-        in_specs=[pl.BlockSpec(memory_space=pltpu.VMEM)],
-        out_specs=pl.BlockSpec(memory_space=pltpu.VMEM),
+        begin_kernel,
+        out_shape=(
+            jax.ShapeDtypeStruct((rows, width), jnp.float32),
+            jax.ShapeDtypeStruct(block, jnp.float32),
+        ),
+        in_specs=[vmem] * 3,
+        out_specs=(vmem, vmem),
         scratch_shapes=[
-            pltpu.VMEM(blocks.shape, blocks.dtype),
+            pltpu.VMEM(block, jnp.float32),
+            pltpu.VMEM(block, jnp.float32),
             pltpu.SemaphoreType.DMA((count,)),
             pltpu.SemaphoreType.DMA((count,)),
         ],
         compiler_params=pltpu.CompilerParams(collective_id=0, has_side_effects=True),
-    )(blocks)
+    )(grad_out, weight_out, query)
 
 
 def finish_kernel(
@@ -381,9 +396,8 @@
 
     def stage(grad_out, top, slot):
         query, keys, values, conv_wide = forward[slot]
-        d_out = lax.dot_general(grad_out, weight_out, contract, preferred_element_type=jnp.float32)
-        d_conv = (d_out * query).astype(jnp.bfloat16)
-        sent = seq_exchange(d_conv.reshape(height, seq_count, chans).transpose(1, 2, 0))
+        d_out, sent = project_and_exchange(grad_out, weight_out, query)
+        sent = sent.reshape(seq_count, chans, height)
         d_prod_blocks = adjoint(sent)
         sent_back = d_prod_blocks.reshape(seq_count * chans, height).astype(jnp.float32)
         return exchange_and_finish(

time: 446 us -> 435 us (0.975)
  Pallas kernels: 269 us -> 290 us
  matrix products: 55 us -> 35.6 us
  other arithmetic: 39.7 us -> 31.1 us
    dot_general x8 -> x0, matrix products: 21.7 us -> none  [stage(): lax.dot_general(grad_out, weight_out, contract, preferred_element_type=jn...]
    pallas_call x8, Pallas kernels: 84.8 us -> 105 us  [project_and_exchange(): pl.pallas_call(begin_kernel, out_shape=(jax.ShapeDtypeStruct((rows, width...]
    convert_element_type x16 -> x0, other arithmetic: 8.37 us -> none  [the longest x8 6.23 us: stage(): d_prod_blocks.reshape(seq_count * chans, height).astype(jnp.float32)]
    convert_element_type x8, local copies, waits for them, and re-layouts: 14 us -> 7.78 us  [stage(): d_prod_blocks.reshape(seq_count * chans, height).astype(jnp.float32)]
    while x104 -> x88, local copies, waits for them, and re-layouts: 26.6 us -> 28.9 us
where the time goes in v7:
time: 435 us; the launch traced here: 432 us
  Pallas kernels  290 us (67%)
  local copies, waits for them, and re-layouts  45.7 us (11%)
  matrix products  35.6 us (8%)
  other arithmetic  31.1 us (7%)
  starting transfers between devices  16.1 us (4%)
  waiting for transfers between devices  13.1 us (3%)
    pallas_call x8, Pallas kernels, exchange_and_finish(): pl.pallas_call(finish_kernel, out_shape=(jax.ShapeDtypeStruct(grad_out.sh...  184 us
    pallas_call x8, Pallas kernels, project_and_exchange(): pl.pallas_call(begin_kernel, out_shape=(jax.ShapeDtypeStruct((rows, width...  105 us
    while x88, local copies, waits for them, and re-layouts  28.9 us
    dot_general x10, matrix products, forward_blocks(): one = jnp.einsum('kn,ncb->cbk', tables['outer'], blocks, precision=accuracy)  15.7 us
    select_n x8, other arithmetic, tick(): jnp.where(active, lax.dynamic_update_index_in_dim(grads, d_input, slot, 0...  13.7 us
    all_to_all x1, waiting for transfers between devices, shards(): both = lax.all_to_all(both, 'seq', split_axis=2, concat_axis=1, tiled=True)  9.36 us
  transfers between devices with their start and end apart: 3, of which 2 were waited for; matrix products, arithmetic and copies ran while one was open for 2% of the time, Pallas kernels for 0%

profile of v7, /device:TPU:1, one launch (start us, length us, event | category | flops | bytes accessed | tf_op | source)
XLA Modules:
  0.0 432.4 jit_solution(17036528889012082587)
XLA Ops:
  0.8 4.5 %collective-permute-start = (bf16[2,2304]{1,0:T(2,128)(2,1)S(1)}, bf16[2,2304]{1,0:T(2,128)(2,1)S(1)}, u32[]{:S(2)}, u32[]{:S(2)}) collective-permute-start(bf16[2,2304]{1,0:T(2,128)(2,1)S(1)} %slice_bitcast_fusion.2), channel_id=1, source_target_pairs={{0,8},{8,16},{16,24},{24,32},{32,40},{40,48},{48,56},{56,64},{64,7... | collective-permute-start | bytes 27656 | tf_op jit(solution)/shard_map/ppermute | solution.py:17
  6.3 1.0 convert_element_type.108
  7.3 1.2 maximum_convert_fusion
  8.9 1.1 fusion.132
  10.0 1.1 copy.46
  11.1 7.0 %all-to-all-start = ((bf16[2,128,768]{1,0,2:T(2,128)(2,1)}), bf16[2,128,768]{1,0,2:T(2,128)(2,1)S(1)}, u32[]{:S(2)}, u32[]{:S(2)}) async-start(bf16[2,128,768]{1,0,2:T(2,128)(2,1)} %copy.46), calls=%async_computation | async-start | bytes 786432 | tf_op jit(solution)/shard_map/all_to_all | solution.py:388
  19.0 9.4 %all-to-all-done = bf16[2,128,768]{1,0,2:T(2,128)(2,1)S(1)} async-done(((bf16[2,128,768]{1,0,2:T(2,128)(2,1)}), bf16[2,128,768]{1,0,2:T(2,128)(2,1)S(1)}, u32[]{:S(2)}, u32[]{:S(2)}) %all-to-all-start) | async-done | bytes 393248 | tf_op jit(solution)/shard_map/all_to_all | solution.py:388
  31.8 1.4 multiply_subtract_fusion.4
  36.0 4.5 %all-to-all-start.1 = ((bf16[32,128,24]{1,2,0:T(8,128)(2,1)}), bf16[32,128,24]{1,2,0:T(8,128)(2,1)}, u32[]{:S(2)}, u32[]{:S(2)}) async-start(bf16[32,128,24]{1,2,0:T(8,128)(2,1)} %copy.50), calls=%async_computation.1 | async-start | bytes 393216 | tf_op jit(solution)/shard_map/all_to_all | solution.py:394
  40.6 1.4 copy.63
  42.0 1.6 copy.71
  43.6 1.7 maximum_maximum_fusion
  45.3 3.8 all-to-all-done.1
  49.0 1.7 convert_element_type.120
  50.7 1.9 copy.51
  52.6 379.8 %while.19 = (s32[]{:T(128)}, bf16[128,768]{1,0:T(8,128)(2,1)}, bf16[1,128,768]{2,1,0:T(8,128)(2,1)}, bf16[768,768]{1,0:T(8,128)(2,1)}, f32[128,768]{1,0:T(8,128)...) while((s32[]{:T(128)}, bf16[128,768]{1,0:T(8,128)(2,1)}, ...), condition=%wide.region_1.2_spmd.clone.clone, body=%wide.region_0.1_spmd.clone.clone.sunk | while | flops 1364475904 | bytes 33128900 | solution.py:427
  52.6 1.6 copy.80.grad_ref
  54.2 12.1 %eval_jaxpr.14 = (f32[128,768]{1,0:T(8,128)}, f32[768,128]{1,0:T(8,128)}) custom-call(bf16[128,768]{1,0:T(8,128)(2,1)} %copy.80.grad_ref, bf16[768,768]{1,0:T(8,128)(2,1)} %get-tuple-element.838.weight_ref, f32[128,768]{1,0:T(8,128)} %get-tuple-element.839.query_ref), custom_call_target="tpu_custom_call" | custom-call | tf_op jit(solution)/shard_map/while/body/eval_jaxpr/pallas_call | solution.py:152
  66.3 1.8 fusion.154
  73.2 1.0 copy.69
  74.2 23.6 %eval_jaxpr.15 = (bf16[128,768]{1,0:T(8,128)(2,1)}, bf16[128,768]{1,0:T(8,128)(2,1)}) custom-call(f32[768,128]{1,0:T(8,128)} %bitcast.108, f32[128,768]{1,0:T(8,128)} %get-tuple-element.794.d_out_ref, f32[128,768]{1,0:T(8,128)} %get-tuple-element.846.conv_ref, f32[128,768]{1,0:T(8,128)} %get-tuple-element.847.values_ref, ...), custom_call_target="tpu_custom_call" | custom-call | tf_op jit(solution)/shard_map/while/body/eval_jaxpr/pallas_call | solution.py:317
  97.8 1.6 bitcast_select_fusion.2
  99.4 1.6 copy.80.grad_ref
  101.0 13.1 %eval_jaxpr.14 = (f32[128,768]{1,0:T(8,128)}, f32[768,128]{1,0:T(8,128)}) custom-call(bf16[128,768]{1,0:T(8,128)(2,1)} %copy.80.grad_ref, bf16[768,768]{1,0:T(8,128)(2,1)} %get-tuple-element.838.weight_ref, f32[128,768]{1,0:T(8,128)} %get-tuple-element.839.query_ref), custom_call_target="tpu_custom_call" | custom-call | tf_op jit(solution)/shard_map/while/body/eval_jaxpr/pallas_call | solution.py:152
  114.2 1.8 fusion.154
  121.1 1.0 copy.69
  122.1 23.3 %eval_jaxpr.15 = (bf16[128,768]{1,0:T(8,128)(2,1)}, bf16[128,768]{1,0:T(8,128)(2,1)}) custom-call(f32[768,128]{1,0:T(8,128)} %bitcast.108, f32[128,768]{1,0:T(8,128)} %get-tuple-element.794.d_out_ref, f32[128,768]{1,0:T(8,128)} %get-tuple-element.846.conv_ref, f32[128,768]{1,0:T(8,128)} %get-tuple-element.847.values_ref, ...), custom_call_target="tpu_custom_call" | custom-call | tf_op jit(solution)/shard_map/while/body/eval_jaxpr/pallas_call | solution.py:317
  145.4 1.7 bitcast_select_fusion.2
  147.2 1.6 copy.80.grad_ref
  148.8 13.3 %eval_jaxpr.14 = (f32[128,768]{1,0:T(8,128)}, f32[768,128]{1,0:T(8,128)}) custom-call(bf16[128,768]{1,0:T(8,128)(2,1)} %copy.80.grad_ref, bf16[768,768]{1,0:T(8,128)(2,1)} %get-tuple-element.838.weight_ref, f32[128,768]{1,0:T(8,128)} %get-tuple-element.839.query_ref), custom_call_target="tpu_custom_call" | custom-call | tf_op jit(solution)/shard_map/while/body/eval_jaxpr/pallas_call | solution.py:152
  162.1 1.8 fusion.154
  169.0 1.0 copy.69
  170.0 23.4 %eval_jaxpr.15 = (bf16[128,768]{1,0:T(8,128)(2,1)}, bf16[128,768]{1,0:T(8,128)(2,1)}) custom-call(f32[768,128]{1,0:T(8,128)} %bitcast.108, f32[128,768]{1,0:T(8,128)} %get-tuple-element.794.d_out_ref, f32[128,768]{1,0:T(8,128)} %get-tuple-element.846.conv_ref, f32[128,768]{1,0:T(8,128)} %get-tuple-element.847.values_ref, ...), custom_call_target="tpu_custom_call" | custom-call | tf_op jit(solution)/shard_map/while/body/eval_jaxpr/pallas_call | solution.py:317
  193.4 1.7 bitcast_select_fusion.2
  195.1 1.6 copy.80.grad_ref
  196.7 13.5 %eval_jaxpr.14 = (f32[128,768]{1,0:T(8,128)}, f32[768,128]{1,0:T(8,128)}) custom-call(bf16[128,768]{1,0:T(8,128)(2,1)} %copy.80.grad_ref, bf16[768,768]{1,0:T(8,128)(2,1)} %get-tuple-element.838.weight_ref, f32[128,768]{1,0:T(8,128)} %get-tuple-element.839.query_ref), custom_call_target="tpu_custom_call" | custom-call | tf_op jit(solution)/shard_map/while/body/eval_jaxpr/pallas_call | solution.py:152
  210.3 1.8 fusion.154
  217.2 1.0 copy.69
  218.2 24.4 %eval_jaxpr.15 = (bf16[128,768]{1,0:T(8,128)(2,1)}, bf16[128,768]{1,0:T(8,128)(2,1)}) custom-call(f32[768,128]{1,0:T(8,128)} %bitcast.108, f32[128,768]{1,0:T(8,128)} %get-tuple-element.794.d_out_ref, f32[128,768]{1,0:T(8,128)} %get-tuple-element.846.conv_ref, f32[128,768]{1,0:T(8,128)} %get-tuple-element.847.values_ref, ...), custom_call_target="tpu_custom_call" | custom-call | tf_op jit(solution)/shard_map/while/body/eval_jaxpr/pallas_call | solution.py:317
  242.5 1.7 bitcast_select_fusion.2
  244.3 1.6 copy.80.grad_ref
  245.9 13.3 %eval_jaxpr.14 = (f32[128,768]{1,0:T(8,128)}, f32[768,128]{1,0:T(8,128)}) custom-call(bf16[128,768]{1,0:T(8,128)(2,1)} %copy.80.grad_ref, bf16[768,768]{1,0:T(8,128)(2,1)} %get-tuple-element.838.weight_ref, f32[128,768]{1,0:T(8,128)} %get-tuple-element.839.query_ref), custom_call_target="tpu_custom_call" | custom-call | tf_op jit(solution)/shard_map/while/body/eval_jaxpr/pallas_call | solution.py:152
  259.2 1.8 fusion.154
  266.1 1.0 copy.69
  267.1 22.5 %eval_jaxpr.15 = (bf16[128,768]{1,0:T(8,128)(2,1)}, bf16[128,768]{1,0:T(8,128)(2,1)}) custom-call(f32[768,128]{1,0:T(8,128)} %bitcast.108, f32[128,768]{1,0:T(8,128)} %get-tuple-element.794.d_out_ref, f32[128,768]{1,0:T(8,128)} %get-tuple-element.846.conv_ref, f32[128,768]{1,0:T(8,128)} %get-tuple-element.847.values_ref, ...), custom_call_target="tpu_custom_call" | custom-call | tf_op jit(solution)/shard_map/while/body/eval_jaxpr/pallas_call | solution.py:317
  289.6 1.7 bitcast_select_fusion.2
  291.4 1.6 copy.80.grad_ref
  293.0 13.3 %eval_jaxpr.14 = (f32[128,768]{1,0:T(8,128)}, f32[768,128]{1,0:T(8,128)}) custom-call(bf16[128,768]{1,0:T(8,128)(2,1)} %copy.80.grad_ref, bf16[768,768]{1,0:T(8,128)(2,1)} %get-tuple-element.838.weight_ref, f32[128,768]{1,0:T(8,128)} %get-tuple-element.839.query_ref), custom_call_target="tpu_custom_call" | custom-call | tf_op jit(solution)/shard_map/while/body/eval_jaxpr/pallas_call | solution.py:152
  306.3 1.8 fusion.154
  313.2 1.0 copy.69
  314.2 22.5 %eval_jaxpr.15 = (bf16[128,768]{1,0:T(8,128)(2,1)}, bf16[128,768]{1,0:T(8,128)(2,1)}) custom-call(f32[768,128]{1,0:T(8,128)} %bitcast.108, f32[128,768]{1,0:T(8,128)} %get-tuple-element.794.d_out_ref, f32[128,768]{1,0:T(8,128)} %get-tuple-element.846.conv_ref, f32[128,768]{1,0:T(8,128)} %get-tuple-element.847.values_ref, ...), custom_call_target="tpu_custom_call" | custom-call | tf_op jit(solution)/shard_map/while/body/eval_jaxpr/pallas_call | solution.py:317
  336.7 1.7 bitcast_select_fusion.2
  338.5 1.6 copy.80.grad_ref
  340.1 13.3 %eval_jaxpr.14 = (f32[128,768]{1,0:T(8,128)}, f32[768,128]{1,0:T(8,128)}) custom-call(bf16[128,768]{1,0:T(8,128)(2,1)} %copy.80.grad_ref, bf16[768,768]{1,0:T(8,128)(2,1)} %get-tuple-element.838.weight_ref, f32[128,768]{1,0:T(8,128)} %get-tuple-element.839.query_ref), custom_call_target="tpu_custom_call" | custom-call | tf_op jit(solution)/shard_map/while/body/eval_jaxpr/pallas_call | solution.py:152
  353.4 1.8 fusion.154
  360.3 1.0 copy.69
  361.3 23.0 %eval_jaxpr.15 = (bf16[128,768]{1,0:T(8,128)(2,1)}, bf16[128,768]{1,0:T(8,128)(2,1)}) custom-call(f32[768,128]{1,0:T(8,128)} %bitcast.108, f32[128,768]{1,0:T(8,128)} %get-tuple-element.794.d_out_ref, f32[128,768]{1,0:T(8,128)} %get-tuple-element.846.conv_ref, f32[128,768]{1,0:T(8,128)} %get-tuple-element.847.values_ref, ...), custom_call_target="tpu_custom_call" | custom-call | tf_op jit(solution)/shard_map/while/body/eval_jaxpr/pallas_call | solution.py:317
  384.3 1.7 bitcast_select_fusion.2
  386.1 1.6 copy.80.grad_ref
  387.7 13.3 %eval_jaxpr.14 = (f32[128,768]{1,0:T(8,128)}, f32[768,128]{1,0:T(8,128)}) custom-call(bf16[128,768]{1,0:T(8,128)(2,1)} %copy.80.grad_ref, bf16[768,768]{1,0:T(8,128)(2,1)} %get-tuple-element.838.weight_ref, f32[128,768]{1,0:T(8,128)} %get-tuple-element.839.query_ref), custom_call_target="tpu_custom_call" | custom-call | tf_op jit(solution)/shard_map/while/body/eval_jaxpr/pallas_call | solution.py:152
  401.0 1.8 fusion.154
  407.9 1.0 copy.69
  408.9 21.8 %eval_jaxpr.15 = (bf16[128,768]{1,0:T(8,128)(2,1)}, bf16[128,768]{1,0:T(8,128)(2,1)}) custom-call(f32[768,128]{1,0:T(8,128)} %bitcast.108, f32[128,768]{1,0:T(8,128)} %get-tuple-element.794.d_out_ref, f32[128,768]{1,0:T(8,128)} %get-tuple-element.846.conv_ref, f32[128,768]{1,0:T(8,128)} %get-tuple-element.847.values_ref, ...), custom_call_target="tpu_custom_call" | custom-call | tf_op jit(solution)/shard_map/while/body/eval_jaxpr/pallas_call | solution.py:317
  430.7 1.7 bitcast_select_fusion.2
  (172 shorter events, 49.4 us)
Async XLA Ops:
  0.0 18.1 %copy-start = (f32[1,768]{1,0:T(1,128)S(1)}, f32[1,768]{1,0:T(1,128)}, u32[]{:S(2)}) copy-start(f32[1,768]{1,0:T(1,128)} %param.15) | copy-start | bytes 9220
  0.8 6.5 %collective-permute-start = (bf16[2,2304]{1,0:T(2,128)(2,1)S(1)}, bf16[2,2304]{1,0:T(2,128)(2,1)S(1)}, u32[]{:S(2)}, u32[]{:S(2)}) collective-permute-start(bf16[2,2304]{1,0:T(2,128)(2,1)S(1)} %slice_bitcast_fusion.2), channel_id=1, source_target_pairs={{0,8},{8,16},{16,24},{24,32},{32,40},{40,48},{48,56},{56,64},{64,7... | collective-permute-start | bytes 27656 | tf_op jit(solution)/shard_map/ppermute | solution.py:17
  6.3 22.8 %copy-start.6 = (f32[128,32]{0,1:T(8,128)}, f32[128,32]{0,1:T(8,128)S(1)}, u32[]{:S(2)}) copy-start(f32[128,32]{0,1:T(8,128)S(1)} %pad_maximum_fusion.1) | copy-start | bytes 49156
  11.1 17.2 %all-to-all-start = ((bf16[2,128,768]{1,0,2:T(2,128)(2,1)}), bf16[2,128,768]{1,0,2:T(2,128)(2,1)S(1)}, u32[]{:S(2)}, u32[]{:S(2)}) async-start(bf16[2,128,768]{1,0,2:T(2,128)(2,1)} %copy.46), calls=%async_computation | async-start | bytes 786432 | tf_op jit(solution)/shard_map/all_to_all | solution.py:388
  18.6 14.6 %copy-start.9 = (f32[128,128]{1,0:T(8,128)}, f32[128,128]{1,0:T(8,128)S(1)}, u32[]{:S(2)}) copy-start(f32[128,128]{1,0:T(8,128)S(1)} %fusion.115) | copy-start | bytes 196612
  18.9 14.3 %copy-start.10 = (f32[128,128]{1,0:T(8,128)}, f32[128,128]{1,0:T(8,128)S(1)}, u32[]{:S(2)}) copy-start(f32[128,128]{1,0:T(8,128)S(1)} %get-tuple-element.666) | copy-start | bytes 196612
  18.9 14.3 %copy-start.11 = (f32[128,128]{1,0:T(8,128)}, f32[128,128]{1,0:T(8,128)S(1)}, u32[]{:S(2)}) copy-start(f32[128,128]{1,0:T(8,128)S(1)} %get-tuple-element.667) | copy-start | bytes 196612
  34.0 0.7 copy-start.7
  34.8 17.8 %copy-start.1 = (bf16[1,768,2304]{2,1,0:T(8,128)(2,1)S(1)}, bf16[1,768,2304]{2,1,0:T(8,128)(2,1)}, u32[]{:S(2)}) copy-start(bf16[1,768,2304]{2,1,0:T(8,128)(2,1)} %param.11) | copy-start | bytes 10616836
  36.0 13.0 %all-to-all-start.1 = ((bf16[32,128,24]{1,2,0:T(8,128)(2,1)}), bf16[32,128,24]{1,2,0:T(8,128)(2,1)}, u32[]{:S(2)}, u32[]{:S(2)}) async-start(bf16[32,128,24]{1,2,0:T(8,128)(2,1)} %copy.50), calls=%async_computation.1 | async-start | bytes 393216 | tf_op jit(solution)/shard_map/all_to_all | solution.py:394
  68.3 1.0 copy-start.3
  69.2 1.1 copy-start.4
  69.2 1.4 copy-start.5
  71.7 1.0 copy-start.2
  71.7 1.0 copy-start.8
  116.1 1.0 copy-start.3
  117.1 1.1 copy-start.4
  117.1 1.4 copy-start.5
  119.6 1.0 copy-start.2
  119.6 1.0 copy-start.8
  164.0 1.0 copy-start.3
  165.0 1.1 copy-start.4
  165.0 1.4 copy-start.5
  167.5 1.0 copy-start.2
  167.5 1.0 copy-start.8
  212.2 1.0 copy-start.3
  213.2 1.1 copy-start.4
  213.2 1.4 copy-start.5
  215.7 1.0 copy-start.2
  215.7 1.0 copy-start.8
  261.2 1.0 copy-start.3
  262.1 1.1 copy-start.4
  262.1 1.4 copy-start.5
  264.6 1.0 copy-start.2
  264.6 1.0 copy-start.8
  308.3 1.0 copy-start.3
  309.2 1.1 copy-start.4
  309.2 1.4 copy-start.5
  311.7 1.0 copy-start.2
  311.7 1.0 copy-start.8
  355.4 1.0 copy-start.3
  356.3 1.1 copy-start.4
  356.3 1.4 copy-start.5
  358.8 1.0 copy-start.2
  358.8 1.0 copy-start.8
  403.0 1.0 copy-start.3
  403.9 1.1 copy-start.4
  403.9 1.4 copy-start.5
  406.4 1.0 copy-start.2
  406.4 1.0 copy-start.8
